TPU v7x, 32 devices: a whole 2x2x4 slice. The times are simulated.
32 devices in a mesh: blk: 4 (over y, x), batch: 8 (over z, core).
Axes of the slice: x: 2, y: 2, z: 4, core: 2. Of those that a mesh axis runs over, the one named last changes fastest.
Arguments:
- hidden_in: bfloat16 [4, 8, 512, 768], P('blk', 'batch'), may hold values from -6 to 6
- lengths: int32 [2, 8], P(None, 'batch'), may hold values from 576 to 1024, as said below
- head_order: int32 [12], replicated, may hold values from 0 to 11, each once
- w_qkv: bfloat16 [768, 2304], replicated, may hold values from -0.21875 to 0.21875
- w_out: bfloat16 [768, 768], replicated, may hold values from -3.5 to 3.5
- ln1_gain: float32 [768], replicated, may hold values from 0.25 to 1.75
- ln1_bias: float32 [768], replicated, may hold values from -3 to 3
- w_up: bfloat16 [768, 3072], replicated, may hold values from -0.21875 to 0.21875
- w_down: bfloat16 [3072, 768], replicated, may hold values from -0.109375 to 0.109375
- ln2_gain: float32 [768], replicated, may hold values from 0.25 to 1.75
- ln2_bias: float32 [768], replicated, may hold values from -3 to 3
- grad_out: bfloat16 [4, 8, 512, 768], P('blk', 'batch'), may hold values from -6 to 6
Outputs:
- hidden_out: bfloat16 [4, 8, 512, 768], P('blk', 'batch')
- grad_in: bfloat16 [4, 8, 512, 768], P('blk', 'batch')
- grad_w_qkv: float32 [768, 2304], P('batch', 'blk')
- grad_w_out: float32 [768, 768], P('batch', 'blk')
- grad_ln1_gain: float32 [768], P('batch')
- grad_ln1_bias: float32 [768], P('batch')
- grad_w_up: float32 [768, 3072], P('batch', 'blk')
- grad_w_down: float32 [3072, 768], P('batch', 'blk')
- grad_ln2_gain: float32 [768], P('batch')
- grad_ln2_bias: float32 [768], P('batch')
Inputs may be any that keep to these rules, and one draw needn't show every extreme that they name: `lengths`: real tokens of each sequence out of its 1024 slots; both the least and the most allowed length occur in every draw.
All inputs are finite; a program needn't handle non-finite values.
Results may differ from a plain program's by a relative error of at most 0.015.
Values may be sent and summed in bfloat16 or wider, within the bound.
No kernel may reach another device: no remote copies, remote signals or barrier semaphores. Data moves between devices by JAX's collectives and lax.ppermute only.
A program may use at most 128 MiB of HBM per device.

v0:
```python
import functools
import math

import jax
import jax.numpy as jnp
from jax import lax
from jax.experimental import pallas as pl
from jax.experimental.pallas import tpu as pltpu
from jax.sharding import PartitionSpec as P

F32 = jnp.float32
BF16 = jnp.bfloat16
MIB = 1 << 20
EPS = 1e-06
NEG = -1e30
LOG2E = math.log2(math.e)
FF_BLOCKS = 4
STEP = 48
EVERY = slice(None)
ME, CORE, LINE, NEAR, FAR, ORDER = range(6)


def swap(block, axis, bits):
    return lax.ppermute(block, axis, [(i, i ^ bits) for i in range(lax.axis_size(axis))])


def nn(a, b):
    return lax.dot_general(a, b, (((1,), (0,)), ((), ())), preferred_element_type=F32)


def nt(a, b):
    return lax.dot_general(a, b, (((1,), (1,)), ((), ())), preferred_element_type=F32)


def tn(a, b):
    return lax.dot_general(a, b, (((0,), (0,)), ((), ())), preferred_element_type=F32)


def call(kernel, scalars, ins, outs, scratch=(), mib=16, us=0):
    vmem = pl.BlockSpec(memory_space=pltpu.VMEM)
    return pl.pallas_call(
        kernel,
        in_specs=[pl.BlockSpec(memory_space=pltpu.SMEM)] + [vmem] * len(ins),
        out_specs=[vmem] * len(outs),
        out_shape=[jax.ShapeDtypeStruct(shape, dtype) for shape, dtype in outs],
        scratch_shapes=[pltpu.VMEM(shape, dtype) for shape, dtype in scratch],
        compiler_params=pltpu.CompilerParams(vmem_limit_bytes=mib * MIB),
        cost_estimate=pl.CostEstimate(
            flops=1000000 + us * 1150000000, bytes_accessed=10000, transcendentals=0
        ),
    )(scalars, *ins)


def rows_of(index, size):
    return pl.ds(pl.multiple_of(index * size, size), size)


def stacked(first, *rows):
    spare = lax.broadcasted_iota(jnp.int32, (16, first.shape[1]), 0)
    extra = jnp.zeros(spare.shape, F32)
    for i, row in enumerate(rows):
        extra = jnp.where(spare == i, row, extra)
    return jnp.concatenate([first, extra.astype(BF16)], axis=0)


def key_bias(valid, keys):
    place = lax.broadcasted_iota(jnp.int32, (1, keys), 1)
    return jnp.where(place < valid, 0.0, NEG)


def attend_head(coef, q, k, v, bias):
    dim = q.shape[0]
    raw = nn(stacked(k, bias).T, stacked(q, 1.0))
    top = jnp.max(raw, axis=0, keepdims=True)
    terms = jnp.exp2((raw - top) * coef).astype(BF16)
    got = nn(stacked(v, 1.0), terms)
    total = got[dim : dim + 1]
    return (got[:dim] / total).astype(BF16), top * coef + jnp.log2(total)


def attend_head_back(coef, scale, q, k, v, bias, lse, ctx, dctx):
    delta = jnp.sum(dctx.astype(F32) * ctx.astype(F32), axis=0, keepdims=True)
    raw = nn(stacked(k, bias).T, stacked(q, 1.0))
    probs = jnp.exp2(raw * coef - lse)
    draw = (probs * (nn(v.T, dctx) - delta)).astype(BF16)
    dv = nt(dctx, probs.astype(BF16)).astype(BF16)
    dk = (nt(q, draw) * scale).astype(BF16)
    dq = (nn(k, draw) * scale).astype(BF16)
    return dq, dk, dv


def norm_stats(hidden):
    mean = jnp.mean(hidden, axis=-1, keepdims=True)
    centred = hidden - mean
    var = jnp.mean(centred * centred, axis=-1, keepdims=True)
    inv = lax.rsqrt(var + EPS)
    return centred * inv, inv


def norm_back(grad, gain, hat, inv):
    scaled = grad * gain
    shift = jnp.mean(scaled, axis=-1, keepdims=True)
    slope = jnp.mean(scaled * hat, axis=-1, keepdims=True)
    back = inv * (scaled - shift - hat * slope)
    return back, jnp.sum(grad * hat, axis=0, keepdims=True), jnp.sum(grad, axis=0, keepdims=True)


def by_core(mat, core, lines):
    span = mat.shape[1] // (2 * lines)
    halves = [
        jnp.concatenate(
            [mat[:, (2 * z + p) * span : (2 * z + p + 1) * span] for z in range(lines)], axis=1
        )
        for p in range(2)
    ]
    even = core == 0
    return jnp.where(even, halves[0], halves[1]), jnp.where(even, halves[1], halves[0])


def rows_by_core(ref, core, lines):
    span = ref.shape[0] // (2 * lines)
    return [
        jnp.concatenate([ref[rows_of(2 * z + (core ^ which), span), :] for z in range(lines)], axis=0)
        for which in range(2)
    ]


def near_kernel(heads, lines, s_ref, x_ref, w_ref, qkv_ref, ctx_ref, lse_ref, *rest):
    width = x_ref.shape[1]
    dim = width // heads
    coef = LOG2E / math.sqrt(dim)
    turned = x_ref[...].T
    for part in range(3):
        at = slice(part * width, (part + 1) * width)
        qkv_ref[at, :] = tn(w_ref[:, at], turned).astype(BF16)
    if lines:
        rest[0][0], rest[0][1] = by_core(x_ref[...], s_ref[CORE], lines)
    bias = key_bias(s_ref[NEAR], x_ref.shape[0])

    def one(i, carry):
        head = s_ref[ORDER + i]
        at = rows_of(head, dim)
        ctx_ref[at, :], lse_ref[head] = attend_head(
            coef,
            qkv_ref[at, :],
            qkv_ref[rows_of(heads + head, dim), :],
            qkv_ref[rows_of(2 * heads + head, dim), :],
            bias,
        )
        return carry

    lax.fori_loop(0, heads // 2, one, 0, unroll=3)


def ffn_kernel(
    heads, blks, lines, s_ref, x_ref, xp_ref, w_ref, qkv_ref, near_ref, wo_ref, gain1_ref,
    bias1_ref, gain2_ref, bias2_ref, dout_ref, wu_ref, wd_ref,
    kv_ref, ctx_ref, lse_ref, hid_ref, slope_ref, dtwo_ref, upt_ref, resid_ref, gains_ref, *rest,
):
    act_ref = rest[-1]
    rows, width = x_ref.shape
    dim = width // heads
    coef = LOG2E / math.sqrt(dim)
    me, core = s_ref[ME], s_ref[CORE]
    turned = xp_ref[...].T
    for part in range(2):
        at = slice((part + 1) * width, (part + 2) * width)
        kv_ref[part * width : (part + 1) * width, :] = tn(w_ref[:, at], turned).astype(BF16)
    bias = key_bias(s_ref[FAR], rows)

    def one(i, carry):
        head = s_ref[ORDER + heads // 2 + i]
        at = rows_of(head, dim)
        ctx_ref[at, :], lse_ref[head] = attend_head(
            coef, qkv_ref[at, :], kv_ref[at, :], kv_ref[rows_of(heads + head, dim), :], bias
        )
        mine = rows_of(s_ref[ORDER + i], dim)
        ctx_ref[mine, :] = near_ref[mine, :]
        return carry

    lax.fori_loop(0, heads // 2, one, 0, unroll=3)

    resid = x_ref[...].astype(F32) + tn(ctx_ref[...], wo_ref[...])
    resid_ref[...] = resid
    hat, _ = norm_stats(resid)
    one_in = hat * gain1_ref[...] + bias1_ref[...]
    low = one_in.astype(BF16)
    upt_ref[...] = low.T
    total = one_in
    blk = wu_ref.shape[1] // FF_BLOCKS
    for j in range(FF_BLOCKS):
        at = slice(j * blk, (j + 1) * blk)
        pre = nn(low, wu_ref[:, at])
        cdf = 0.5 + 0.5 * lax.erf(pre * math.sqrt(0.5))
        pdf = jnp.exp2(pre * pre * (-0.5 * LOG2E)) * (1.0 / math.sqrt(2.0 * math.pi))
        slope_ref[:, at] = (cdf + pre * pdf).astype(BF16)
        act = (pre * cdf).astype(BF16)
        act_ref[:, at] = act
        total = total + nn(act, wd_ref[at, :])
    hat, inv = norm_stats(total)
    hid_ref[...] = (hat * gain2_ref[...] + bias2_ref[...]).astype(BF16)
    back, gain, shift = norm_back(dout_ref[...].astype(F32), gain2_ref[...], hat, inv)
    dtwo_ref[...] = back
    gains_ref[0:1, :] = gain
    gains_ref[1:2, :] = shift
    turned = back.astype(BF16).T
    if lines:
        high = width // blks
        span = act_ref.shape[1] // (2 * lines)
        for which in (1, 0):
            for z in range(0, lines, 2):
                pair = [act_ref[:, rows_of(2 * (z + i) + (core ^ which), span)] for i in range(2)]
                prod = nn(turned, jnp.concatenate(pair, axis=1)).astype(BF16)
                for k in range(blks):
                    rest[which][k ^ me, :, z * span : (z + 2) * span] = prod[
                        k * high : (k + 1) * high
                    ]
        rest[2][0], rest[2][1] = by_core(xp_ref[...], core, lines)
    else:
        rest[0][...] = nn(turned, act_ref[...]).astype(BF16)


def pre_back_kernel(
    blks, lines, s_ref, dtwo_ref, slope_ref, wd_ref, wu_ref, upt_ref, dpre_ref, done_ref, *outs
):
    me, core = s_ref[ME], s_ref[CORE]
    low = dtwo_ref[...].astype(BF16)
    total = dtwo_ref[...]
    blk = wu_ref.shape[1] // blks
    ups = rows_by_core(upt_ref, core, lines) if lines else ()
    for k in range(blks):
        at = slice(k * blk, (k + 1) * blk)
        dpre = (nt(low, wd_ref[at, :]) * slope_ref[:, at].astype(F32)).astype(BF16)
        if not lines:
            dpre_ref[:, at] = dpre
        total = total + nt(dpre, wu_ref[:, at])
        for out, rows in zip(outs, ups):
            prod = nn(rows, dpre).astype(BF16)
            half = prod.shape[0]
            for p in range(blk // half):
                out[k ^ me, p * half : (p + 1) * half, :] = prod[:, p * half : (p + 1) * half]
    done_ref[...] = total
    if not lines:
        outs[0][...] = nn(upt_ref[...], dpre_ref[...]).astype(BF16)


def norm_back_kernel(
    blks, lines, s_ref, done_ref, resid_ref, gain1_ref, gains_ref, wo_ref, ctx_ref, dres_ref,
    dctx_ref, *outs,
):
    me, core = s_ref[ME], s_ref[CORE]
    hat, inv = norm_stats(resid_ref[...])
    back, gain, shift = norm_back(done_ref[...], gain1_ref[...], hat, inv)
    dres_ref[...] = back
    turned = back.astype(BF16).T
    dctx_ref[...] = nn(wo_ref[...], turned).astype(BF16)
    row = lax.broadcasted_iota(jnp.int32, (16, gain.shape[1]), 0)
    sums = jnp.where(row == 0, gain, jnp.where(row == 1, shift, 0.0))
    sums = jnp.where(row == 2, gains_ref[0:1, :], sums)
    sums = jnp.where(row == 3, gains_ref[1:2, :], sums).astype(BF16)
    if not lines:
        outs[0][...] = nt(turned, ctx_ref[...]).astype(BF16)
        outs[1][...] = sums
        return
    ctxs = rows_by_core(ctx_ref, core, lines)
    sums = by_core(sums, core, lines)
    high = turned.shape[0] // blks
    both = nt(turned, jnp.concatenate(ctxs, axis=0)).astype(BF16)
    half = both.shape[1] // 2
    for which, (out, thin) in enumerate(zip(outs, sums)):
        for k in range(blks):
            out[k ^ me, :high, :] = both[k * high : (k + 1) * high, which * half : (which + 1) * half]
            out[k ^ me, high:, :] = thin


def far_back_kernel(
    heads, s_ref, qkv_ref, kv_ref, ctx_ref, dctx_ref, lse_ref, w_ref, dq_ref, dkv_ref, give_ref,
    rest_ref, wide_ref,
):
    width, rows = ctx_ref.shape
    dim = width // heads
    half = heads // 2
    scale = 1.0 / math.sqrt(dim)
    bias = key_bias(s_ref[FAR], rows)
    wide_ref[...] = jnp.zeros_like(wide_ref)

    def one(i, carry):
        head = s_ref[ORDER + half + i]
        at, low = rows_of(head, dim), rows_of(heads + head, dim)
        dq, dk, dv = attend_head_back(
            LOG2E * scale, scale, qkv_ref[at, :], kv_ref[at, :], kv_ref[low, :], bias,
            lse_ref[head], ctx_ref[at, :], dctx_ref[at, :],
        )
        dq_ref[rows_of(i, dim), :] = dq
        dkv_ref[rows_of(i, dim), :] = dk
        dkv_ref[rows_of(half + i, dim), :] = dv
        wide_ref[at, :] = dk
        wide_ref[low, :] = dv
        return carry

    lax.fori_loop(0, half, one, 0, unroll=3)
    give = nn(w_ref[:, width:], wide_ref[...]).astype(BF16)
    give_ref[...] = give[: give_ref.shape[0]]
    rest_ref[...] = give[give_ref.shape[0] :]


def near_back_kernel(
    heads, blks, lines, s_ref, qkv_ref, ctx_ref, dctx_ref, lse_ref, farq_ref, farkv_ref, x_ref,
    xp_ref, dqkv_ref, *rest,
):
    outs, near_ref = rest[:-1], rest[-1]
    width, rows = ctx_ref.shape
    dim = width // heads
    half = heads // 2
    scale = 1.0 / math.sqrt(dim)
    bias = key_bias(s_ref[NEAR], rows)
    me = s_ref[ME]
    dqkv_ref[width:, :] = jnp.zeros((2 * width, rows), BF16)

    def one(i, carry):
        head = s_ref[ORDER + i]
        at = rows_of(head, dim)
        key, value = rows_of(heads + head, dim), rows_of(2 * heads + head, dim)
        dq, dk, dv = attend_head_back(
            LOG2E * scale, scale, qkv_ref[at, :], qkv_ref[key, :], qkv_ref[value, :], bias,
            lse_ref[head], ctx_ref[at, :], dctx_ref[at, :],
        )
        dqkv_ref[at, :] = dq
        dqkv_ref[key, :] = dk
        dqkv_ref[value, :] = dv
        near_ref[rows_of(i, dim), :] = dk
        near_ref[rows_of(half + i, dim), :] = dv
        dqkv_ref[rows_of(s_ref[ORDER + half + i], dim), :] = farq_ref[rows_of(i, dim), :]
        return carry

    lax.fori_loop(0, half, one, 0, unroll=3)
    per = 3 * heads // blks

    def store(unit, prod):
        if not lines:
            outs[0][rows_of(unit, dim), :] = prod
            return
        at = ((unit // per) ^ me, rows_of(unit % per, dim), EVERY)
        keep = outs[0].shape[2]
        outs[0][at] = prod[:, :keep]
        for i, out in enumerate(outs[1:]):
            out[at] = prod[:, keep + i * 128 : keep + (i + 1) * 128]

    x = jnp.concatenate([x_ref[0], x_ref[1]], axis=1) if lines else x_ref[...]
    xp = jnp.concatenate([xp_ref[0], xp_ref[1]], axis=1) if lines else xp_ref[...]
    prod = nn(dqkv_ref[:width, :], x).astype(BF16)
    for h in range(heads):
        store(h, prod[h * dim : (h + 1) * dim])
    for first, grads, inputs in ((0, near_ref, x), (half, farkv_ref, xp)):
        prod = nn(grads[...], inputs).astype(BF16)
        for i in range(half):
            head = s_ref[ORDER + first + i]
            store(heads + head, prod[i * dim : (i + 1) * dim])
            low = (half + i) * dim
            store(2 * heads + head, prod[low : low + dim])


def through_kernel(s_ref, w_ref, dqkv_ref, own_ref):
    own_ref[...] = nn(w_ref[...], dqkv_ref[...])


def input_kernel(s_ref, own_ref, got_ref, rest_ref, dres_ref, out_ref):
    cut = got_ref.shape[0]
    for at, got in ((slice(0, cut), got_ref), (slice(cut, None), rest_ref)):
        total = own_ref[at, :] + got[...].astype(F32)
        out_ref[:, at] = (total.T + dres_ref[:, at]).astype(BF16)


def add_up(*parts):
    total = parts[0].astype(F32)
    for part in parts[1:]:
        total = total + part.astype(F32)
    return total


def after(scalars, *arrays):
    return lax.optimization_barrier((scalars,) + arrays)[0]


def block_at(ref, at):
    at = tuple(at) + (EVERY,) * (len(ref.shape) - len(at))
    first, last, _ = at[-2].indices(ref.shape[-2])
    return at[:-2], first, last - first, at[-1]


def sums_kernel(plan, lines, inputs, s_ref, *refs):
    ins, outs = refs[:inputs], refs[inputs:]

    def run(odd, upper):
        for terms, targets in plan(odd, upper) if lines else plan():
            found = [(ins[i],) + block_at(ins[i], src) for i, src in terms]
            places = [(outs[out],) + block_at(outs[out], dst) + (part,) for out, dst, part in targets]
            rows = found[0][3]

            def add(at, size):
                total = add_up(
                    *(ref[leads + (pl.ds(at + row, size), col)] for ref, leads, row, _, col in found)
                ).astype(BF16)
                for ref, leads, row, _, col, part in places:
                    ref[leads + (pl.ds(at + row, size), col)] = total[:, part]

            def body(i, carry):
                add(pl.multiple_of(i * STEP, STEP), STEP)
                return carry

            if rows >= 2 * STEP:
                lax.fori_loop(0, rows // STEP, body, 0)
                if rows % STEP:
                    add(rows // STEP * STEP, rows % STEP)
            else:
                add(0, rows)

    if lines:
        line = s_ref[LINE]
        for odd in range(2):
            pl.when(line % 2 == odd)(functools.partial(run, odd, line // 2))
    else:
        run(0, 0)


def sums(scalars, ins, shapes, plan, lines=False):
    kernel = functools.partial(sums_kernel, plan, lines, len(ins))
    return call(kernel, scalars, ins, [(shape, BF16) for shape in shapes], mib=4)


def span_of(index, size):
    return slice(index * size, (index + 1) * size)


def by_line(z, odd, upper):
    return (z % 2) ^ odd, (z // 2) ^ upper


class Halves:
    def __init__(self, cut, rows, cols):
        self.cut, self.rows, self.cols = cut, rows, cols
        self.sizes = (cut, rows - cut)
        self.at = (slice(0, cut), slice(cut, rows))

    def first(self, s, keeps, gots, cuts):
        shapes = [(2, size, self.cols) for size in self.sizes for _ in range(2)]
        picks = ((0, 0, (0, 2)), (1, 0, (1, 3)), (2, 1, (0, 1)), (3, 1, (2, 3)))

        def plan():
            found = []
            for out, half, group in picks:
                start, end = self.at[half].start, self.at[half].stop
                for i, (first, last) in enumerate(zip(cuts, cuts[1:])):
                    low, up = max(first, start), min(last, end)
                    if low < up:
                        for slot, j in enumerate(group):
                            src = (j, slice(low - first, up - first), EVERY)
                            here = (slot, slice(low - start, up - start), EVERY)
                            terms = [(i, src), (len(keeps) + i, src)]
                            found.append((terms, [(out, here, EVERY)]))
            return found

        return sums(s, (*keeps, *gots), shapes, plan)

    def second(self, s, chip):
        got = (swap(chip[1], "blk", 1), swap(chip[3], "blk", 2))
        shapes = [(size, self.cols) for size in self.sizes for _ in range(2)]

        def plan():
            return [
                ([(half, (slot,)), (2 + half, (slot,))], [(2 * half + slot, (EVERY,), EVERY)])
                for half in range(2)
                for slot in range(2)
            ]

        return sums(s, (chip[0], chip[2]) + got, shapes, plan)

    def third(self, s, pair, wide, size, lines):
        got = (swap(pair[1], "blk", 2), swap(pair[3], "blk", 1))
        half = self.cols
        shape = (self.rows - wide, half + 128)

        def plan(odd, upper):
            found = []
            for p in range(wide // half):
                for z in range(lines):
                    row = p * half + z * size
                    which = int(row >= self.cut)
                    row -= which * self.cut
                    out, slot = by_line(z, odd, upper)
                    src = (slice(row, row + size), EVERY)
                    dst = (slot, span_of(p, size), slice(0, half))
                    found.append(([(which, src), (2 + which, src)], [(out, dst, EVERY)]))
            src = (slice(wide - self.cut, None), EVERY)
            targets = []
            for z in range(lines):
                out, slot = by_line(z, odd, upper)
                targets.append((out, (slot, EVERY, slice(half, half + size)), span_of(z, size)))
            return found + [([(1, src), (3, src)], targets)]

        return sums(s, (pair[0], pair[2]) + got, [(2,) + shape] * 2, plan, True)


def proj_first(s, keep, gots):
    blks, rows, cols = keep.shape

    def plan():
        return [
            ([(0, (j, EVERY, span_of(i, 128))), (1 + i, (j,))], [(j, (EVERY, span_of(i, 128)), EVERY)])
            for j in range(blks)
            for i in range(len(gots))
        ]

    return sums(s, (keep,) + tuple(gots), [(rows, cols)] * blks, plan)


def proj_second(s, chip, lines):
    parts = [chip[0]] + [swap(chip[i], "blk", i) for i in range(1, len(chip))]
    rows, cols = chip[0].shape
    size = cols // lines

    def plan(odd, upper):
        targets = []
        for z in range(lines):
            out, slot = by_line(z, odd, upper)
            targets.append((out, (slot,), span_of(z, size)))
        return [([(i, (EVERY,)) for i in range(len(parts))], targets)]

    return sums(s, parts, [(2, rows, size)] * 2, plan, True)


def fourth(s, mine):
    return paired(s, mine[0], swap(mine[1], "batch", 2))


def dealt(s, keep, got):
    def plan():
        return [
            ([(i, (2 * out + slot,)) for i in range(2)], [(out, (slot,), EVERY)])
            for out in range(2)
            for slot in range(2)
        ]

    return sums(s, (keep, got), [(2,) + keep.shape[1:]] * 2, plan)


def paired(s, keep, got):
    def plan():
        return [([(0, (i,)), (1, (i,))], [(i, (EVERY,), EVERY)]) for i in range(2)]

    return sums(s, (keep, got), [keep.shape[1:]] * 2, plan)


def down_first(s, keep, got, lines):
    blks, high, cols = keep.shape
    size = cols // lines

    def plan(odd, upper):
        found = []
        for z in range(lines):
            out, slot = by_line(z, odd, upper)
            for j in range(blks):
                src = (j, EVERY, span_of(z, size))
                found.append(([(0, src), (1, src)], [(out, (slot, j), EVERY)]))
        return found

    return sums(s, (keep, got), [(2, blks, high, size)] * 2, plan, True)


def down_final_kernel(s_ref, *refs):
    refs[-1][...] = add_up(*(ref[...] for ref in refs[:-1]))


def turned_final_kernel(s_ref, *refs):
    refs[-1][...] = add_up(*(ref[...] for ref in refs[:-1])).T


def up_final_kernel(high, half, size, s_ref, *refs):
    up_ref, out_ref, sums_ref = refs[-3:]
    total = add_up(*(ref[...] for ref in refs[:-3]))
    for p in range(high // size):
        up_ref[:, span_of(p, half)] = total[span_of(p, size), :half]
    out_ref[...] = total[:high, half : half + size].T
    sums_ref[...] = total[high : high + 8, half:]


def reduce_any(mats, thin=None):
    blks = lax.axis_size("blk")
    lines = lax.axis_size("batch") // 2
    me = lax.axis_index("blk")
    core = lax.axis_index("batch") % 2
    line = lax.axis_index("batch") // 2
    pieces = []
    for mat in mats:
        rows = mat.shape[0] // (2 * lines)
        pieces.append(mat.reshape(lines, 2, rows, blks, -1))
    if thin is not None:
        thin = thin.reshape(lines, 2, rows, 1, -1)
        pieces.append(jnp.broadcast_to(thin, thin.shape[:3] + (blks,) + thin.shape[4:]))
    every = jnp.concatenate(pieces, axis=4)

    def half(which, distance):
        part = lax.dynamic_index_in_dim(every, which, 1, keepdims=False)
        return lax.dynamic_index_in_dim(part, me ^ distance, 2, keepdims=False)

    keep = [half(core, distance) for distance in range(blks)]
    got = swap(jnp.stack([half(1 - core, i) for i in range(blks)]), "batch", 1)
    chip = [add_up(part, got[i]).astype(BF16) for i, part in enumerate(keep)]
    total = add_up(chip[0], *(swap(chip[i], "blk", i) for i in range(1, blks)))
    while lines > 1:
        lines //= 2
        upper = line // lines
        pairs = total.astype(BF16).reshape((2, lines) + total.shape[1:])
        mine = lax.dynamic_index_in_dim(pairs, upper, 0, keepdims=False)
        theirs = lax.dynamic_index_in_dim(pairs, 1 - upper, 0, keepdims=False)
        total = add_up(mine, swap(theirs, "batch", 2 * lines))
        line = line % lines
    return total[0]


def shards(
    hidden_in, lengths, head_order, w_qkv, w_out, ln1_gain, ln1_bias, w_up, w_down, ln2_gain,
    ln2_bias, grad_out,
):
    _, _, rows, width = hidden_in.shape
    heads = head_order.shape[0]
    blks = lax.axis_size("blk")
    batch = lax.axis_size("batch")
    inner = w_up.shape[1]
    me = lax.axis_index("blk")
    at = lax.axis_index("batch")
    fast = batch == 8 and blks == 4 and width % (16 * batch) == 0
    lines = batch // 2 if fast else 0
    wide = inner // blks
    size = width // batch
    half = width // 2
    high = width // blks
    cols = 3 * width // blks

    x = hidden_in.reshape(rows, width)
    dout = grad_out.reshape(rows, width)
    xp = swap(x, "blk", 1)
    gain1, bias1, gain2, bias2 = (
        part.reshape(1, width) for part in (ln1_gain, ln1_bias, ln2_gain, ln2_bias)
    )
    length = lax.dynamic_index_in_dim(lengths[:, 0], me // 2, 0, keepdims=False)
    ids = jnp.arange(heads, dtype=jnp.int32)
    order = jnp.sum(jnp.where(head_order[None, :] == ids[:, None], ids[None, :], 0), axis=1)
    parts = [me, at % 2, at // 2, length - rows * (me % 2), length - rows * (1 - me % 2)]
    s = jnp.concatenate([jnp.stack(parts).astype(jnp.int32), order.astype(jnp.int32)])

    square = ((width, rows), BF16)
    lse = ((heads, 1, rows), F32)
    split = [((2, rows, width // 2), BF16)] if lines else []
    qkv, near_ctx, near_lse, *x_parts = call(
        functools.partial(near_kernel, heads, lines), s, (x, w_qkv),
        [((3 * width, rows), BF16), square, lse] + split, mib=8, us=8,
    )

    if lines:
        down_out = [((blks, high, inner // 2), BF16)] * 2 + split
    else:
        down_out = [((width, inner), BF16)]
    kv, ctx, far_lse, hid, slope, dtwo, upt, resid, gains, *down = call(
        functools.partial(ffn_kernel, heads, blks, lines), s,
        (x, xp, w_qkv, qkv, near_ctx, w_out, gain1, bias1, gain2, bias2, dout, w_up, w_down),
        [((2 * width, rows), BF16), square, lse, ((rows, width), BF16), ((rows, inner), BF16),
         ((rows, width), F32), square, ((rows, width), F32), ((8, width), F32)] + down_out,
        [((rows, inner), BF16)], mib=16, us=18,
    )

    s = after(s, dtwo)
    if lines:
        ups = Halves(half + size, wide + high + 16, half)
        up_out = [((blks, wide, half), BF16)] * 2
        thin_out = [((blks, high + 16, half), BF16)] * 2
        proj_out = [((blks, cols, half), BF16)] + [((blks, cols, 128), BF16)] * (half // 128)
    else:
        up_out = [((width, inner), BF16)]
        thin_out = [((width, width), BF16), ((16, width), BF16)]
        proj_out = [((3 * width, width), BF16)]
    pre_shape = (16, 128) if lines else (rows, inner)
    _, done, *up = call(
        functools.partial(pre_back_kernel, blks, lines), s, (dtwo, slope, w_down, w_up, upt),
        [(pre_shape, BF16), ((rows, width), F32)] + up_out, mib=8,
    )
    s = after(s, done)
    if lines:
        chip1 = down_first(s, down[0], swap(down[1], "batch", 1), lines)
        s = after(s, chip1[0])
    dres, dctx, *thin = call(
        functools.partial(norm_back_kernel, blks, lines), s,
        (done, resid, gain1, gains, w_out, ctx), [((rows, width), F32), square] + thin_out, mib=8,
    )
    s = after(s, dctx)
    if lines:
        gots = [swap(part, "batch", 1) for part in (up[1], thin[1])]
        chip2 = ups.first(s, (up[0], thin[0]), gots, (0, wide, ups.rows))
        s = after(s, chip2[0])
    far_q, far_kv, *give = call(
        functools.partial(far_back_kernel, heads), s, (qkv, kv, ctx, dctx, far_lse, w_qkv),
        [((width // 2, rows), BF16), square, ((width - 128, rows), BF16), ((128, rows), BF16)],
        [((2 * width, rows), BF16)], mib=8,
    )
    s = after(s, far_q)
    if not lines:
        got_in = [swap(part, "blk", 1) for part in give]
    dqkv, *proj = call(
        functools.partial(near_back_kernel, heads, blks, lines), s,
        (qkv, ctx, dctx, near_lse, far_q, far_kv)
        + ((x_parts[0], down[2]) if lines else (x, xp)),
        [((3 * width, rows), BF16)] + proj_out, [square], mib=8,
    )
    s = after(s, dqkv)
    if lines:
        line1 = fourth(s, chip1)
        s = after(s, line1[0])
        pair2 = ups.second(s, chip2)
        s = after(s, pair2[0])
        got_in = [swap(part, "blk", 1) for part in lax.optimization_barrier((pair2[0], *give))[1:]]
        chip3 = proj_first(s, proj[0], [swap(part, "batch", 1) for part in proj[1:]])
        s = after(s, chip3[0])
        line2 = ups.third(s, pair2, wide, size, lines)
        s = after(s, line2[0])
        far1 = dealt(s, line1[0], swap(line1[1], "batch", 4))
        s = after(s, far1[0])
    (own,) = call(through_kernel, s, (w_qkv, dqkv), [((width, rows), F32)], mib=4)
    s = after(s, own)
    if lines:
        line3 = proj_second(s, chip3, lines)
        s = after(s, line3[0])
        last2 = fourth(s, line2)
        s = after(s, last2[0])
        last1 = paired(s, far1[0], swap(far1[1], "blk", 2))
        s = after(s, last1[0])
        last3 = fourth(s, line3)
        s = after(s, last3[0])
        (own_down,) = call(
            down_final_kernel, s, (last1[0], swap(last1[1], "blk", 1)),
            [((high, inner // batch), F32)], mib=4,
        )
        s = after(s, own_down)
        own_down = own_down.T
        own_up, own_out, thin = call(
            functools.partial(up_final_kernel, high, half, size), s,
            (last2[0], swap(last2[1], "batch", 4)),
            [((size, wide), F32), ((size, high), F32), ((8, 128), F32)], mib=4,
        )
        thin = thin[:4, :size]
        s = after(s, own_up)
    (grad_in,) = call(input_kernel, s, (own, *got_in, dres), [((rows, width), BF16)], mib=4)
    if lines:
        s = after(s, grad_in)
        (own_qkv,) = call(
            turned_final_kernel, s, (last3[0], swap(last3[1], "batch", 4)),
            [((size, cols), F32)], mib=4,
        )
    else:
        own_down = reduce_any([down[0].T])
        both = reduce_any([up[0], thin[0].T], thin[1][:4].T)
        own_up, own_out, thin = both[:, :wide], both[:, wide : wide + high], both[:, wide + high :].T
        own_qkv = reduce_any([proj[0].T])
    return (
        hid.reshape(hidden_in.shape),
        grad_in.reshape(hidden_in.shape),
        own_qkv,
        own_out,
        thin[0],
        thin[1],
        own_up,
        own_down,
        thin[2],
        thin[3],
    )


def solution(mesh):
    rows = P("blk", "batch", None, None)
    both = P("batch", "blk")
    return jax.shard_map(
        shards,
        mesh=mesh,
        in_specs=(rows, P(None, "batch")) + (P(),) * 9 + (rows,),
        out_specs=(rows, rows, both, both, P("batch"), P("batch"), both, both)
        + (P("batch"), P("batch")),
        check_vma=False,
    )
```

profile of v0, /device:TPU:0, one launch (start us, length us, event | category | flops | bytes accessed | tf_op | source)
XLA Modules:
  0.0 140.7 jit_solution(7826175941699749757)
XLA Ops:
  0.7 3.0 %collective-permute-start = (bf16[512,768]{1,0:T(8,128)(2,1)}, bf16[512,768]{1,0:T(8,128)(2,1)S(1)}, u32[]{:S(2)}, u32[]{:S(2)}) collective-permute-start(bf16[512,768]{1,0:T(8,128)(2,1)} %bitcast.19), channel_id=1, source_target_pairs={{0,8},{8,0},{16,24},{24,16},{1,9},{9,1},{17,25},{25,17},{2,10},{10... | collective-permute-start | bytes 2359304 | tf_op jit(solution)/shard_map/ppermute | solution.py:24
  3.7 0.6 constant_dynamic-slice_fusion
  5.5 0.8 select_reduce_fusion
  6.3 0.7 reshape.48.gain1_ref
  7.0 0.7 reshape.49.bias1_ref
  7.7 0.7 reshape.50.gain2_ref
  8.4 0.7 reshape.51.bias2_ref
  9.1 0.1 concatenate.3.s_ref
  9.2 2.0 %copy-done.2 = bf16[768,2304]{1,0:T(8,128)(2,1)S(1)} copy-done((bf16[768,2304]{1,0:T(8,128)(2,1)S(1)}, bf16[768,2304]{1,0:T(8,128)(2,1)}, u32[]{:S(2)}) %copy-start.2) | copy-done | bytes 3538968
  11.2 1.1 copy-done.7
  12.3 5.8 %shard_map.195 = (bf16[2304,512]{1,0:T(8,128)(2,1)S(1)}, bf16[768,512]{1,0:T(8,128)(2,1)S(1)}, f32[12,1,512]{2,1,0:T(1,128)S(1)}, bf16[2,512,384]{2,1,0:T(8,128)(2,1)S(1)}) custom-call(s32[17]{0:T(128)S(1)} %concatenate.3.s_ref, bf16[512,768]{1,0:T(8,128)(2,1)S(1)} %bitcast.20, bf16[768,2304]{1,0:T(8,128)(2,1)S(1)} %copy-done.2), custom_call_target="tpu_custom_call" | custom-call | flops 9201000448 | bytes 10000 | tf_op jit(solution)/shard_map/pallas_call | solution.py:41
  18.1 3.3 %collective-permute-done.xp_ref = bf16[512,768]{1,0:T(8,128)(2,1)S(1)} collective-permute-done((bf16[512,768]{1,0:T(8,128)(2,1)}, bf16[512,768]{1,0:T(8,128)(2,1)S(1)}, u32[]{:S(2)}, u32[]{:S(2)}) %collective-permute-start) | collective-permute-done | bytes 786464 | tf_op jit(solution)/shard_map/ppermute | solution.py:24
  21.5 17.6 %shard_map.196 = (bf16[1536,512]{1,0:T(8,128)(2,1)S(1)}, bf16[768,512]{1,0:T(8,128)(2,1)S(1)}, f32[12,1,512]{2,1,0:T(1,128)S(1)}, bf16[512,768]{1,0:T(8,128)(2,1...) custom-call(s32[17]{0:T(128)S(1)} %concatenate.3.s_ref, ...), custom_call_target="tpu_custom_call" | custom-call | flops 20700999680 | bytes 10000 | tf_op jit(solution)/shard_map/pallas_call | solution.py:41
  39.1 9.0 %shard_map.197 = (bf16[16,128]{1,0:T(8,128)(2,1)}, f32[512,768]{1,0:T(8,128)S(1)}, bf16[4,768,384]{2,1,0:T(8,128)(2,1)S(1)}, bf16[4,768,384]{2,1,0:T(8,128)(2,1)S(1)}) custom-call(s32[17]{0:T(128)S(1)} %concatenate.3.s_ref, f32[512,768]{1,0:T(8,128)S(1)} %get-tuple-element.98.dtwo_ref, bf16[512,3072]{1,0:T(8,128)(2,1)S(1)} %get-tuple-element.100.slope_ref, ...), custom_call_target="tpu_custom_call" | custom-call | flops 1000000 | bytes 10000 | tf_op jit(solution)/shard_map/pallas_call | solution.py:41
  48.1 0.5 collective-permute-start.2
  48.6 1.5 %shard_map.198 = (bf16[2,4,192,384]{3,2,1,0:T(8,128)(2,1)S(1)}, bf16[2,4,192,384]{3,2,1,0:T(8,128)(2,1)S(1)}) custom-call(s32[17]{0:T(128)S(1)} %concatenate.3.s_ref, bf16[4,192,1536]{2,1,0:T(8,128)(2,1)S(1)} %get-tuple-element.104.refs_0_, bf16[4,192,1536]{2,1,0:T(8,128)(2,1)S(1)} %collective-permute-done.1.refs_1_), custom_call_target="tpu_custom_call" | custom-call | flops 1000000 | bytes 10000 | tf_op jit(solution)/shard_map/pallas_call | solution.py:41
  50.2 1.9 %collective-permute-start.4 = (bf16[2,4,192,384]{3,2,1,0:T(8,128)(2,1)S(1)}, bf16[2,4,192,384]{3,2,1,0:T(8,128)(2,1)S(1)}, u32[]{:S(2)}, u32[]{:S(2)}) collective-permute-start(bf16[2,4,192,384]{3,2,1,0:T(8,128)(2,1)S(1)} %get-tuple-element.129), channel_id=1, source_target_pairs={{0,2},{1,3},{2,0},{3,1},{4,6},{5,7},{6,4},{7,5},{8,10},{9,11},{10,... | collective-permute-start | bytes 3538952 | tf_op jit(solution)/shard_map/ppermute | solution.py:24
  52.0 3.0 %shard_map.199 = (f32[512,768]{1,0:T(8,128)S(1)}, bf16[768,512]{1,0:T(8,128)(2,1)S(1)}, bf16[4,208,384]{2,1,0:T(8,128)(2,1)S(1)}, bf16[4,208,384]{2,1,0:T(8,128)(2,1)S(1)}) custom-call(s32[17]{0:T(128)S(1)} %concatenate.3.s_ref, f32[512,768]{1,0:T(8,128)S(1)} %get-tuple-element.102.done_ref, f32[512,768]{1,0:T(8,128)S(1)} %get-tuple-element.108.resid_ref, ...), custom_call_target="tpu_custom_call" | custom-call | flops 1000000 | bytes 10000 | tf_op jit(solution)/shard_map/pallas_call | solution.py:41
  55.1 0.1 collective-permute-start.3
  55.2 2.1 %collective-permute-done.3.refs_3_ = bf16[4,208,384]{2,1,0:T(8,128)(2,1)S(1)} collective-permute-done((bf16[4,208,384]{2,1,0:T(8,128)(2,1)S(1)}, bf16[4,208,384]{2,1,0:T(8,128)(2,1)S(1)}, u32[]{:S(2)}, u32[]{:S(2)}) %collective-permute-start.3) | collective-permute-done | bytes 639008 | tf_op jit(solution)/shard_map/ppermute | solution.py:24
  57.2 2.0 %shard_map.200 = (bf16[2,480,384]{2,1,0:T(8,128)(2,1)S(1)}, bf16[2,480,384]{2,1,0:T(8,128)(2,1)S(1)}, bf16[2,496,384]{2,1,0:T(8,128)(2,1)S(1)}, bf16[2,496,384]{2,1,0:T(8,128)(2,1)S(1)}) custom-call(s32[17]{0:T(128)S(1)} %concatenate.3.s_ref, bf16[4,768,384]{2,1,0:T(8,128)(2,1)S(1)} %get-tuple-element.113.refs_0_, ...), custom_call_target="tpu_custom_call" | custom-call | flops 1000000 | bytes 10000 | tf_op jit(solution)/shard_map/pallas_call | solution.py:41
  59.2 1.6 %collective-permute-start.6 = (bf16[2,496,384]{2,1,0:T(8,128)(2,1)S(1)}, bf16[2,496,384]{2,1,0:T(8,128)(2,1)S(1)}, u32[]{:S(2)}, u32[]{:S(2)}) collective-permute-start(bf16[2,496,384]{2,1,0:T(8,128)(2,1)S(1)} %get-tuple-element.134), channel_id=1, source_target_pairs={{0,16},{8,24},{16,0},{24,8},{1,17},{9,25},{17,1},{25,9},{2,18},{10... | collective-permute-start | bytes 2285576 | tf_op jit(solution)/shard_map/ppermute | solution.py:24
  60.8 1.5 %collective-permute-start.5 = (bf16[2,480,384]{2,1,0:T(8,128)(2,1)S(1)}, bf16[2,480,384]{2,1,0:T(8,128)(2,1)S(1)}, u32[]{:S(2)}, u32[]{:S(2)}) collective-permute-start(bf16[2,480,384]{2,1,0:T(8,128)(2,1)S(1)} %get-tuple-element.133), channel_id=1, source_target_pairs={{0,8},{8,0},{16,24},{24,16},{1,9},{9,1},{17,25},{25,17},{2,10},{10... | collective-permute-start | bytes 2211848 | tf_op jit(solution)/shard_map/ppermute | solution.py:24
  62.3 6.2 %shard_map.201 = (bf16[384,512]{1,0:T(8,128)(2,1)S(1)}, bf16[768,512]{1,0:T(8,128)(2,1)S(1)}, bf16[640,512]{1,0:T(8,128)(2,1)S(1)}, bf16[128,512]{1,0:T(8,128)(2,1)S(1)}) custom-call(s32[17]{0:T(128)S(1)} %concatenate.3.s_ref, bf16[2304,512]{1,0:T(8,128)(2,1)S(1)} %get-tuple-element.95.qkv_ref, bf16[1536,512]{1,0:T(8,128)(2,1)S(1)} %get-tuple-element.119.kv_ref, ...), custom_call_target="tpu_custom_call" | custom-call | flops 1000000 | bytes 10000 | tf_op jit(solution)/shard_map/pallas_call | solution.py:41
  68.5 6.9 %shard_map.202 = (bf16[2304,512]{1,0:T(8,128)(2,1)S(1)}, bf16[4,576,384]{2,1,0:T(8,128)(2,1)S(1)}, bf16[4,576,128]{2,1,0:T(8,128)(2,1)S(1)}, bf16[4,576,128]{2,1,0:T(8,128)(2,1)S(1)}, bf16[4,576,128]{2,1,0:T(8,128)(2,1)S(1)}) custom-call(s32[17]{0:T(128)S(1)} %concatenate.3.s_ref, bf16[2304,512]{1,0:T(8,128)(2,1)S(1)} %get-tuple-element.95.qkv_ref, ...), custom_call_target="tpu_custom_call" | custom-call | flops 1000000 | bytes 10000 | tf_op jit(solution)/shard_map/pallas_call | solution.py:41
  75.4 0.1 collective-permute-start.7
  75.5 0.5 collective-permute-start.8
  76.0 2.2 %collective-permute-done.4.refs_1_ = bf16[2,4,192,384]{3,2,1,0:T(8,128)(2,1)S(1)} collective-permute-done((bf16[2,4,192,384]{3,2,1,0:T(8,128)(2,1)S(1)}, bf16[2,4,192,384]{3,2,1,0:T(8,128)(2,1)S(1)}, u32[]{:S(2)}, u32[]{:S(2)}) %collective-permute-start.4) | collective-permute-done | bytes 1179680 | tf_op jit(solution)/shard_map/ppermute | solution.py:24
  78.2 0.9 shard_map.203
  79.1 0.0 collective-permute-done.5.refs_2_
  79.1 1.1 shard_map.204
  80.2 1.7 %collective-permute-start.10 = (bf16[480,384]{1,0:T(8,128)(2,1)S(1)}, bf16[480,384]{1,0:T(8,128)(2,1)S(1)}, u32[]{:S(2)}, u32[]{:S(2)}) collective-permute-start(bf16[480,384]{1,0:T(8,128)(2,1)S(1)} %get-tuple-element.144), channel_id=1, source_target_pairs={{0,16},{8,24},{16,0},{24,8},{1,17},{9,25},{17,1},{25,9},{2,18},{10... | collective-permute-start | bytes 1105928 | tf_op jit(solution)/shard_map/ppermute | solution.py:24
  82.0 2.6 %collective-permute-start.12 = (bf16[4,192,384]{2,1,0:T(8,128)(2,1)S(1)}, bf16[4,192,384]{2,1,0:T(8,128)(2,1)S(1)}, u32[]{:S(2)}, u32[]{:S(2)}) collective-permute-start(bf16[4,192,384]{2,1,0:T(8,128)(2,1)S(1)} %get-tuple-element.148), channel_id=1, source_target_pairs={{0,4},{1,5},{2,6},{3,7},{4,0},{5,1},{6,2},{7,3},{8,12},{9,13},{10,... | collective-permute-start | bytes 1769480 | tf_op jit(solution)/shard_map/ppermute | solution.py:24
  84.6 1.5 %collective-permute-start.11 = (bf16[496,384]{1,0:T(8,128)(2,1)S(1)}, bf16[496,384]{1,0:T(8,128)(2,1)S(1)}, u32[]{:S(2)}, u32[]{:S(2)}) collective-permute-start(bf16[496,384]{1,0:T(8,128)(2,1)S(1)} %get-tuple-element.145), channel_id=1, source_target_pairs={{0,8},{8,0},{16,24},{24,16},{1,9},{9,1},{17,25},{25,17},{2,10},{10... | collective-permute-start | bytes 1142792 | tf_op jit(solution)/shard_map/ppermute | solution.py:24
  86.1 1.8 %shard_map.205 = (bf16[576,384]{1,0:T(8,128)(2,1)S(1)}, bf16[576,384]{1,0:T(8,128)(2,1)S(1)}, bf16[576,384]{1,0:T(8,128)(2,1)S(1)}, bf16[576,384]{1,0:T(8,128)(2,1)S(1)}) custom-call(s32[17]{0:T(128)S(1)} %concatenate.3.s_ref, bf16[4,576,384]{2,1,0:T(8,128)(2,1)S(1)} %get-tuple-element.137.refs_0_, bf16[4,576,128]{2,1,0:T(8,128)(2,1)S(1)} %collective-permute-done.7.refs_1_, ...), custom_call_target="tpu_custom_call" | custom-call | flops 1000000 | bytes 10000 | tf_op jit(solution)/shard_map/pallas_call | solution.py:41
  87.9 0.6 collective-permute-start.13
  88.5 0.5 collective-permute-start.14
  89.0 2.7 %collective-permute-done.10.refs_2_ = bf16[480,384]{1,0:T(8,128)(2,1)S(1)} collective-permute-done((bf16[480,384]{1,0:T(8,128)(2,1)S(1)}, bf16[480,384]{1,0:T(8,128)(2,1)S(1)}, u32[]{:S(2)}, u32[]{:S(2)}) %collective-permute-start.10) | collective-permute-done | bytes 368672 | tf_op jit(solution)/shard_map/ppermute | solution.py:24
  91.7 2.6 %collective-permute-start.15 = (bf16[576,384]{1,0:T(8,128)(2,1)S(1)}, bf16[576,384]{1,0:T(8,128)(2,1)S(1)}, u32[]{:S(2)}, u32[]{:S(2)}) collective-permute-start(bf16[576,384]{1,0:T(8,128)(2,1)S(1)} %get-tuple-element.154), channel_id=1, source_target_pairs={{0,24},{8,16},{16,8},{24,0},{1,25},{9,17},{17,9},{25,1},{2,26},{10... | collective-permute-start | bytes 1327112 | tf_op jit(solution)/shard_map/ppermute | solution.py:24
  94.3 2.0 %collective-permute-done.11.refs_3_ = bf16[496,384]{1,0:T(8,128)(2,1)S(1)} collective-permute-done((bf16[496,384]{1,0:T(8,128)(2,1)S(1)}, bf16[496,384]{1,0:T(8,128)(2,1)S(1)}, u32[]{:S(2)}, u32[]{:S(2)}) %collective-permute-start.11) | collective-permute-done | bytes 380960 | tf_op jit(solution)/shard_map/ppermute | solution.py:24
  96.3 1.2 shard_map.206
  97.5 1.6 %collective-permute-start.16 = (bf16[2,208,512]{2,1,0:T(8,128)(2,1)S(1)}, bf16[2,208,512]{2,1,0:T(8,128)(2,1)S(1)}, u32[]{:S(2)}, u32[]{:S(2)}) collective-permute-start(bf16[2,208,512]{2,1,0:T(8,128)(2,1)S(1)} %get-tuple-element.157), channel_id=1, source_target_pairs={{0,2},{1,3},{2,0},{3,1},{4,6},{5,7},{6,4},{7,5},{8,10},{9,11},{10,... | collective-permute-start | bytes 1277960 | tf_op jit(solution)/shard_map/ppermute | solution.py:24
  99.1 12.0 %collective-permute-done.12.refs_1_ = bf16[4,192,384]{2,1,0:T(8,128)(2,1)S(1)} collective-permute-done((bf16[4,192,384]{2,1,0:T(8,128)(2,1)S(1)}, bf16[4,192,384]{2,1,0:T(8,128)(2,1)S(1)}, u32[]{:S(2)}, u32[]{:S(2)}) %collective-permute-start.12) | collective-permute-done | bytes 589856 | tf_op jit(solution)/shard_map/ppermute | solution.py:24
  111.1 0.8 shard_map.207
  111.9 0.5 collective-permute-start.17
  112.4 1.5 %collective-permute-start.21 = (bf16[640,512]{1,0:T(8,128)(2,1)S(1)}, bf16[640,512]{1,0:T(8,128)(2,1)S(1)}, u32[]{:S(2)}, u32[]{:S(2)}) collective-permute-start(bf16[640,512]{1,0:T(8,128)(2,1)S(1)} %get-tuple-element.173), channel_id=1, source_target_pairs={{0,8},{8,0},{16,24},{24,16},{1,9},{9,1},{17,25},{25,17},{2,10},{10... | collective-permute-start | bytes 1966088 | tf_op jit(solution)/shard_map/ppermute | solution.py:24
  114.0 2.5 %shard_map.208.own_ref = f32[768,512]{1,0:T(8,128)S(1)} custom-call(s32[17]{0:T(128)S(1)} %concatenate.3.s_ref, bf16[768,2304]{1,0:T(8,128)(2,1)S(1)} %copy-done.3, bf16[2304,512]{1,0:T(8,128)(2,1)S(1)} %get-tuple-element.127.dqkv_ref), custom_call_target="tpu_custom_call" | custom-call | flops 1000000 | bytes 10000 | tf_op jit(solution)/shard_map/pallas_call | solution.py:41
  116.5 1.7 %shard_map.209 = (bf16[2,576,96]{2,1,0:T(8,128)(2,1)S(1)}, bf16[2,576,96]{2,1,0:T(8,128)(2,1)S(1)}) custom-call(s32[17]{0:T(128)S(1)} %concatenate.3.s_ref, bf16[576,384]{1,0:T(8,128)(2,1)S(1)} %get-tuple-element.141.refs_0_, bf16[576,384]{1,0:T(8,128)(2,1)S(1)} %collective-permute-done.13.refs_1_, bf16[576,384]{1,0:T(8,128)(2,1)S(1)} %collective-permute-done.14.refs_2_, ...), custom_call_target="tpu_custom_call" | custom-call | flops 1000000 | bytes 10000 | tf_op jit(solution)/shard_map/pallas_call | solution.py:41
  118.2 0.7 collective-permute-start.18
  118.9 0.7 shard_map.210
  119.6 3.5 %collective-permute-start.20 = (bf16[208,512]{1,0:T(8,128)(2,1)S(1)}, bf16[208,512]{1,0:T(8,128)(2,1)S(1)}, u32[]{:S(2)}, u32[]{:S(2)}) collective-permute-start(bf16[208,512]{1,0:T(8,128)(2,1)S(1)} %get-tuple-element.168), channel_id=1, source_target_pairs={{0,4},{1,5},{2,6},{3,7},{4,0},{5,1},{6,2},{7,3},{8,12},{9,13},{10,... | collective-permute-start | bytes 638984 | tf_op jit(solution)/shard_map/ppermute | solution.py:24
  123.1 0.7 shard_map.211
  123.8 0.6 collective-permute-start.19
  124.4 1.5 %collective-permute-start.22 = (bf16[128,512]{1,0:T(8,128)(2,1)S(1)}, bf16[128,512]{1,0:T(8,128)(2,1)S(1)}, u32[]{:S(2)}, u32[]{:S(2)}) collective-permute-start(bf16[128,512]{1,0:T(8,128)(2,1)S(1)} %get-tuple-element.174), channel_id=1, source_target_pairs={{0,8},{8,0},{16,24},{24,16},{1,9},{9,1},{17,25},{25,17},{2,10},{10... | collective-permute-start | bytes 393224 | tf_op jit(solution)/shard_map/ppermute | solution.py:24
  125.9 4.7 %collective-permute-done.18.refs_1_ = bf16[2,576,96]{2,1,0:T(8,128)(2,1)S(1)} collective-permute-done((bf16[2,576,96]{2,1,0:T(8,128)(2,1)S(1)}, bf16[2,576,96]{2,1,0:T(8,128)(2,1)S(1)}, u32[]{:S(2)}, u32[]{:S(2)}) %collective-permute-start.18) | collective-permute-done | bytes 221216 | tf_op jit(solution)/shard_map/ppermute | solution.py:24
  130.6 0.7 shard_map.212
  131.3 1.3 collective-permute-start.23
  132.7 0.2 collective-permute-done.19.refs_1_
  132.9 1.3 shard_map.213
  134.1 1.3 shard_map.214
  135.5 0.5 slice_bitcast_fusion
  136.0 1.9 %shard_map.215 = bf16[512,768]{1,0:T(8,128)(2,1)} custom-call(s32[17]{0:T(128)S(1)} %concatenate.3.s_ref, f32[768,512]{1,0:T(8,128)S(1)} %shard_map.208.own_ref, bf16[640,512]{1,0:T(8,128)(2,1)S(1)} %collective-permute-done.21.got_ref, bf16[128,512]{1,0:T(8,128)(2,1)S(1)} %collective-permute-done.22.rest_ref, f32[512,768]{1,0:T(8,128)S(1)} %get-tuple-element.175.dres_ref), custom_call_target="tpu_custom_call" | custom-call | flops 1000000 | bytes 10000 | tf_op jit(solution)/shard_map/pallas_call | solution.py:41
  137.9 1.3 collective-permute-done.23.refs_1_
  139.3 1.4 shard_map.216
  (34 shorter events, 0.1 us)
Async XLA Ops:
  0.6 3.0 %copy-start = (s32[2,1]{0,1:T(1,128)S(1)}, s32[2,1]{0,1:T(1,128)}, u32[]{:S(2)}) copy-start(s32[2,1]{0,1:T(1,128)} %param.13) | copy-start | bytes 28
  0.7 20.8 %collective-permute-start = (bf16[512,768]{1,0:T(8,128)(2,1)}, bf16[512,768]{1,0:T(8,128)(2,1)S(1)}, u32[]{:S(2)}, u32[]{:S(2)}) collective-permute-start(bf16[512,768]{1,0:T(8,128)(2,1)} %bitcast.19), channel_id=1, source_target_pairs={{0,8},{8,0},{16,24},{24,16},{1,9},{9,1},{17,25},{25,17},{2,10},{10... | collective-permute-start | bytes 2359304 | tf_op jit(solution)/shard_map/ppermute | solution.py:24
  9.2 2.0 %copy-start.2 = (bf16[768,2304]{1,0:T(8,128)(2,1)S(1)}, bf16[768,2304]{1,0:T(8,128)(2,1)}, u32[]{:S(2)}) copy-start(bf16[768,2304]{1,0:T(8,128)(2,1)} %w_ref.7) | copy-start | bytes 10616836
  11.2 1.1 copy-start.7
  12.3 9.1 %copy-start.3 = (bf16[768,2304]{1,0:T(8,128)(2,1)S(1)}, bf16[768,2304]{1,0:T(8,128)(2,1)}, u32[]{:S(2)}) copy-start(bf16[768,2304]{1,0:T(8,128)(2,1)} %w_ref.7) | copy-start | bytes 10616836
  12.3 9.1 %copy-start.4 = (bf16[768,3072]{1,0:T(8,128)(2,1)S(1)}, bf16[768,3072]{1,0:T(8,128)(2,1)}, u32[]{:S(2)}) copy-start(bf16[768,3072]{1,0:T(8,128)(2,1)} %wu_ref.3) | copy-start | bytes 14155780
  12.3 9.1 %copy-start.5 = (bf16[3072,768]{1,0:T(8,128)(2,1)S(1)}, bf16[3072,768]{1,0:T(8,128)(2,1)}, u32[]{:S(2)}) copy-start(bf16[3072,768]{1,0:T(8,128)(2,1)} %wd_ref.3) | copy-start | bytes 14155780
  12.3 9.1 %copy-start.6 = (bf16[768,768]{1,0:T(8,128)(2,1)S(1)}, bf16[768,768]{1,0:T(8,128)(2,1)}, u32[]{:S(2)}) copy-start(bf16[768,768]{1,0:T(8,128)(2,1)} %wo_ref.3) | copy-start | bytes 3538948
  12.3 9.1 %copy-start.8 = (bf16[1,1,512,768]{3,2,1,0:T(8,128)(2,1)S(1)}, bf16[1,1,512,768]{3,2,1,0:T(8,128)(2,1)}, u32[]{:S(2)}) copy-start(bf16[1,1,512,768]{3,2,1,0:T(8,128)(2,1)} %param.12) | copy-start | bytes 2359300
  12.3 9.1 %copy-start.9 = (bf16[1,1,512,768]{3,2,1,0:T(8,128)(2,1)S(1)}, bf16[1,1,512,768]{3,2,1,0:T(8,128)(2,1)}, u32[]{:S(2)}) copy-start(bf16[1,1,512,768]{3,2,1,0:T(8,128)(2,1)} %param.23) | copy-start | bytes 2359300
  39.1 9.5 %collective-permute-start.1 = (bf16[4,192,1536]{2,1,0:T(8,128)(2,1)S(1)}, bf16[4,192,1536]{2,1,0:T(8,128)(2,1)S(1)}, u32[]{:S(2)}, u32[]{:S(2)}) collective-permute-start(bf16[4,192,1536]{2,1,0:T(8,128)(2,1)S(1)} %get-tuple-element.105), channel_id=1, source_target_pairs={{0,1},{1,0},{2,3},{3,2},{4,5},{5,4},{6,7},{7,6},{8,9},{9,8},{10,11... | collective-permute-start | bytes 7077896 | tf_op jit(solution)/shard_map/ppermute | solution.py:24
  48.1 7.0 %collective-permute-start.2 = (bf16[4,768,384]{2,1,0:T(8,128)(2,1)S(1)}, bf16[4,768,384]{2,1,0:T(8,128)(2,1)S(1)}, u32[]{:S(2)}, u32[]{:S(2)}) collective-permute-start(bf16[4,768,384]{2,1,0:T(8,128)(2,1)S(1)} %get-tuple-element.115), channel_id=1, source_target_pairs={{0,1},{1,0},{2,3},{3,2},{4,5},{5,4},{6,7},{7,6},{8,9},{9,8},{10,11... | collective-permute-start | bytes 7077896 | tf_op jit(solution)/shard_map/ppermute | solution.py:24
  50.2 28.0 %collective-permute-start.4 = (bf16[2,4,192,384]{3,2,1,0:T(8,128)(2,1)S(1)}, bf16[2,4,192,384]{3,2,1,0:T(8,128)(2,1)S(1)}, u32[]{:S(2)}, u32[]{:S(2)}) collective-permute-start(bf16[2,4,192,384]{3,2,1,0:T(8,128)(2,1)S(1)} %get-tuple-element.129), channel_id=1, source_target_pairs={{0,2},{1,3},{2,0},{3,1},{4,6},{5,7},{6,4},{7,5},{8,10},{9,11},{10,... | collective-permute-start | bytes 3538952 | tf_op jit(solution)/shard_map/ppermute | solution.py:24
  55.1 2.1 %collective-permute-start.3 = (bf16[4,208,384]{2,1,0:T(8,128)(2,1)S(1)}, bf16[4,208,384]{2,1,0:T(8,128)(2,1)S(1)}, u32[]{:S(2)}, u32[]{:S(2)}) collective-permute-start(bf16[4,208,384]{2,1,0:T(8,128)(2,1)S(1)} %get-tuple-element.116), channel_id=1, source_target_pairs={{0,1},{1,0},{2,3},{3,2},{4,5},{5,4},{6,7},{7,6},{8,9},{9,8},{10,11... | collective-permute-start | bytes 1916936 | tf_op jit(solution)/shard_map/ppermute | solution.py:24
  59.2 19.9 %collective-permute-start.6 = (bf16[2,496,384]{2,1,0:T(8,128)(2,1)S(1)}, bf16[2,496,384]{2,1,0:T(8,128)(2,1)S(1)}, u32[]{:S(2)}, u32[]{:S(2)}) collective-permute-start(bf16[2,496,384]{2,1,0:T(8,128)(2,1)S(1)} %get-tuple-element.134), channel_id=1, source_target_pairs={{0,16},{8,24},{16,0},{24,8},{1,17},{9,25},{17,1},{25,9},{2,18},{10... | collective-permute-start | bytes 2285576 | tf_op jit(solution)/shard_map/ppermute | solution.py:24
  60.8 18.2 %collective-permute-start.5 = (bf16[2,480,384]{2,1,0:T(8,128)(2,1)S(1)}, bf16[2,480,384]{2,1,0:T(8,128)(2,1)S(1)}, u32[]{:S(2)}, u32[]{:S(2)}) collective-permute-start(bf16[2,480,384]{2,1,0:T(8,128)(2,1)S(1)} %get-tuple-element.133), channel_id=1, source_target_pairs={{0,8},{8,0},{16,24},{24,16},{1,9},{9,1},{17,25},{25,17},{2,10},{10... | collective-permute-start | bytes 2211848 | tf_op jit(solution)/shard_map/ppermute | solution.py:24
  75.4 9.2 %collective-permute-start.7 = (bf16[4,576,128]{2,1,0:T(8,128)(2,1)S(1)}, bf16[4,576,128]{2,1,0:T(8,128)(2,1)S(1)}, u32[]{:S(2)}, u32[]{:S(2)}) collective-permute-start(bf16[4,576,128]{2,1,0:T(8,128)(2,1)S(1)} %get-tuple-element.138), channel_id=1, source_target_pairs={{0,1},{1,0},{2,3},{3,2},{4,5},{5,4},{6,7},{7,6},{8,9},{9,8},{10,11... | collective-permute-start | bytes 1769480 | tf_op jit(solution)/shard_map/ppermute | solution.py:24
  75.5 10.6 %collective-permute-start.8 = (bf16[4,576,128]{2,1,0:T(8,128)(2,1)S(1)}, bf16[4,576,128]{2,1,0:T(8,128)(2,1)S(1)}, u32[]{:S(2)}, u32[]{:S(2)}) collective-permute-start(bf16[4,576,128]{2,1,0:T(8,128)(2,1)S(1)} %get-tuple-element.139), channel_id=1, source_target_pairs={{0,1},{1,0},{2,3},{3,2},{4,5},{5,4},{6,7},{7,6},{8,9},{9,8},{10,11... | collective-permute-start | bytes 1769480 | tf_op jit(solution)/shard_map/ppermute | solution.py:24
  78.2 7.9 %collective-permute-start.9 = (bf16[4,576,128]{2,1,0:T(8,128)(2,1)S(1)}, bf16[4,576,128]{2,1,0:T(8,128)(2,1)S(1)}, u32[]{:S(2)}, u32[]{:S(2)}) collective-permute-start(bf16[4,576,128]{2,1,0:T(8,128)(2,1)S(1)} %get-tuple-element.140), channel_id=1, source_target_pairs={{0,1},{1,0},{2,3},{3,2},{4,5},{5,4},{6,7},{7,6},{8,9},{9,8},{10,11... | collective-permute-start | bytes 1769480 | tf_op jit(solution)/shard_map/ppermute | solution.py:24
  80.2 11.4 %collective-permute-start.10 = (bf16[480,384]{1,0:T(8,128)(2,1)S(1)}, bf16[480,384]{1,0:T(8,128)(2,1)S(1)}, u32[]{:S(2)}, u32[]{:S(2)}) collective-permute-start(bf16[480,384]{1,0:T(8,128)(2,1)S(1)} %get-tuple-element.144), channel_id=1, source_target_pairs={{0,16},{8,24},{16,0},{24,8},{1,17},{9,25},{17,1},{25,9},{2,18},{10... | collective-permute-start | bytes 1105928 | tf_op jit(solution)/shard_map/ppermute | solution.py:24
  82.0 29.1 %collective-permute-start.12 = (bf16[4,192,384]{2,1,0:T(8,128)(2,1)S(1)}, bf16[4,192,384]{2,1,0:T(8,128)(2,1)S(1)}, u32[]{:S(2)}, u32[]{:S(2)}) collective-permute-start(bf16[4,192,384]{2,1,0:T(8,128)(2,1)S(1)} %get-tuple-element.148), channel_id=1, source_target_pairs={{0,4},{1,5},{2,6},{3,7},{4,0},{5,1},{6,2},{7,3},{8,12},{9,13},{10,... | collective-permute-start | bytes 1769480 | tf_op jit(solution)/shard_map/ppermute | solution.py:24
  84.6 11.7 %collective-permute-start.11 = (bf16[496,384]{1,0:T(8,128)(2,1)S(1)}, bf16[496,384]{1,0:T(8,128)(2,1)S(1)}, u32[]{:S(2)}, u32[]{:S(2)}) collective-permute-start(bf16[496,384]{1,0:T(8,128)(2,1)S(1)} %get-tuple-element.145), channel_id=1, source_target_pairs={{0,8},{8,0},{16,24},{24,16},{1,9},{9,1},{17,25},{25,17},{2,10},{10... | collective-permute-start | bytes 1142792 | tf_op jit(solution)/shard_map/ppermute | solution.py:24
  87.9 24.5 %collective-permute-start.13 = (bf16[576,384]{1,0:T(8,128)(2,1)S(1)}, bf16[576,384]{1,0:T(8,128)(2,1)S(1)}, u32[]{:S(2)}, u32[]{:S(2)}) collective-permute-start(bf16[576,384]{1,0:T(8,128)(2,1)S(1)} %get-tuple-element.152), channel_id=1, source_target_pairs={{0,8},{8,0},{16,24},{24,16},{1,9},{9,1},{17,25},{25,17},{2,10},{10... | collective-permute-start | bytes 1327112 | tf_op jit(solution)/shard_map/ppermute | solution.py:24
  88.5 28.0 %collective-permute-start.14 = (bf16[576,384]{1,0:T(8,128)(2,1)S(1)}, bf16[576,384]{1,0:T(8,128)(2,1)S(1)}, u32[]{:S(2)}, u32[]{:S(2)}) collective-permute-start(bf16[576,384]{1,0:T(8,128)(2,1)S(1)} %get-tuple-element.153), channel_id=1, source_target_pairs={{0,16},{8,24},{16,0},{24,8},{1,17},{9,25},{17,1},{25,9},{2,18},{10... | collective-permute-start | bytes 1327112 | tf_op jit(solution)/shard_map/ppermute | solution.py:24
  91.7 24.8 %collective-permute-start.15 = (bf16[576,384]{1,0:T(8,128)(2,1)S(1)}, bf16[576,384]{1,0:T(8,128)(2,1)S(1)}, u32[]{:S(2)}, u32[]{:S(2)}) collective-permute-start(bf16[576,384]{1,0:T(8,128)(2,1)S(1)} %get-tuple-element.154), channel_id=1, source_target_pairs={{0,24},{8,16},{16,8},{24,0},{1,25},{9,17},{17,9},{25,1},{2,26},{10... | collective-permute-start | bytes 1327112 | tf_op jit(solution)/shard_map/ppermute | solution.py:24
  97.5 21.4 %collective-permute-start.16 = (bf16[2,208,512]{2,1,0:T(8,128)(2,1)S(1)}, bf16[2,208,512]{2,1,0:T(8,128)(2,1)S(1)}, u32[]{:S(2)}, u32[]{:S(2)}) collective-permute-start(bf16[2,208,512]{2,1,0:T(8,128)(2,1)S(1)} %get-tuple-element.157), channel_id=1, source_target_pairs={{0,2},{1,3},{2,0},{3,1},{4,6},{5,7},{6,4},{7,5},{8,10},{9,11},{10,... | collective-permute-start | bytes 1277960 | tf_op jit(solution)/shard_map/ppermute | solution.py:24
  111.9 11.2 %collective-permute-start.17 = (bf16[2,192,384]{2,1,0:T(8,128)(2,1)S(1)}, bf16[2,192,384]{2,1,0:T(8,128)(2,1)S(1)}, u32[]{:S(2)}, u32[]{:S(2)}) collective-permute-start(bf16[2,192,384]{2,1,0:T(8,128)(2,1)S(1)} %get-tuple-element.160), channel_id=1, source_target_pairs={{0,16},{8,24},{16,0},{24,8},{1,17},{9,25},{17,1},{25,9},{2,18},{10... | collective-permute-start | bytes 884744 | tf_op jit(solution)/shard_map/ppermute | solution.py:24
  112.4 23.6 %collective-permute-start.21 = (bf16[640,512]{1,0:T(8,128)(2,1)S(1)}, bf16[640,512]{1,0:T(8,128)(2,1)S(1)}, u32[]{:S(2)}, u32[]{:S(2)}) collective-permute-start(bf16[640,512]{1,0:T(8,128)(2,1)S(1)} %get-tuple-element.173), channel_id=1, source_target_pairs={{0,8},{8,0},{16,24},{24,16},{1,9},{9,1},{17,25},{25,17},{2,10},{10... | collective-permute-start | bytes 1966088 | tf_op jit(solution)/shard_map/ppermute | solution.py:24
  118.2 12.3 %collective-permute-start.18 = (bf16[2,576,96]{2,1,0:T(8,128)(2,1)S(1)}, bf16[2,576,96]{2,1,0:T(8,128)(2,1)S(1)}, u32[]{:S(2)}, u32[]{:S(2)}) collective-permute-start(bf16[2,576,96]{2,1,0:T(8,128)(2,1)S(1)} %get-tuple-element.163), channel_id=1, source_target_pairs={{0,2},{1,3},{2,0},{3,1},{4,6},{5,7},{6,4},{7,5},{8,10},{9,11},{10,... | collective-permute-start | bytes 663560 | tf_op jit(solution)/shard_map/ppermute | solution.py:24
  119.6 14.5 %collective-permute-start.20 = (bf16[208,512]{1,0:T(8,128)(2,1)S(1)}, bf16[208,512]{1,0:T(8,128)(2,1)S(1)}, u32[]{:S(2)}, u32[]{:S(2)}) collective-permute-start(bf16[208,512]{1,0:T(8,128)(2,1)S(1)} %get-tuple-element.168), channel_id=1, source_target_pairs={{0,4},{1,5},{2,6},{3,7},{4,0},{5,1},{6,2},{7,3},{8,12},{9,13},{10,... | collective-permute-start | bytes 638984 | tf_op jit(solution)/shard_map/ppermute | solution.py:24
  123.8 9.1 %collective-permute-start.19 = (bf16[192,384]{1,0:T(8,128)(2,1)S(1)}, bf16[192,384]{1,0:T(8,128)(2,1)S(1)}, u32[]{:S(2)}, u32[]{:S(2)}) collective-permute-start(bf16[192,384]{1,0:T(8,128)(2,1)S(1)} %get-tuple-element.166), channel_id=1, source_target_pairs={{0,8},{8,0},{16,24},{24,16},{1,9},{9,1},{17,25},{25,17},{2,10},{10... | collective-permute-start | bytes 442376 | tf_op jit(solution)/shard_map/ppermute | solution.py:24
  124.4 11.6 %collective-permute-start.22 = (bf16[128,512]{1,0:T(8,128)(2,1)S(1)}, bf16[128,512]{1,0:T(8,128)(2,1)S(1)}, u32[]{:S(2)}, u32[]{:S(2)}) collective-permute-start(bf16[128,512]{1,0:T(8,128)(2,1)S(1)} %get-tuple-element.174), channel_id=1, source_target_pairs={{0,8},{8,0},{16,24},{24,16},{1,9},{9,1},{17,25},{25,17},{2,10},{10... | collective-permute-start | bytes 393224 | tf_op jit(solution)/shard_map/ppermute | solution.py:24
  131.3 8.0 %collective-permute-start.23 = (bf16[576,96]{1,0:T(8,128)(2,1)S(1)}, bf16[576,96]{1,0:T(8,128)(2,1)S(1)}, u32[]{:S(2)}, u32[]{:S(2)}) collective-permute-start(bf16[576,96]{1,0:T(8,128)(2,1)S(1)} %get-tuple-element.177), channel_id=1, source_target_pairs={{0,4},{1,5},{2,6},{3,7},{4,0},{5,1},{6,2},{7,3},{8,12},{9,13},{10,... | collective-permute-start | bytes 331784 | tf_op jit(solution)/shard_map/ppermute | solution.py:24
  136.0 4.7 %copy-start.1 = (s32[2,1]{0,1:T(1,128)S(1)}, s32[2,1]{0,1:T(1,128)}, u32[]{:S(2)}) copy-start(s32[2,1]{0,1:T(1,128)} %param.13) | copy-start | bytes 28
where the time goes:
time: 141 us
  Pallas kernels  70.2 us (50%)
  waiting for transfers between devices  30.5 us (22%)
  starting transfers between devices  29.9 us (21%)
  local copies, waits for them, and re-layouts  7.13 us (5%)
  between operations  2.18 us (2%)
    pallas_call x22, Pallas kernels, call(): pl.pallas_call(kernel, in_specs=[pl.BlockSpec(memory_space=pltpu.SMEM)] +...  70.2 us
    ppermute x24, waiting for transfers between devices, swap(): lax.ppermute(block, axis, [(i, i ^ bits) for i in range(lax.axis_size(axi...  30.5 us
    ppermute x24, starting transfers between devices, swap(): lax.ppermute(block, axis, [(i, i ^ bits) for i in range(lax.axis_size(axi...  29.9 us
    unnamed x20, local copies, waits for them, and re-layouts  3.18 us
  transfers between devices with their start and end apart: 24, of which 9 were waited for; matrix products, arithmetic and copies ran while one was open for 3% of the time, Pallas kernels for 36%

commit v1 on v0

--- a/solution.py
+++ b/solution.py
@@ -220,28 +220,41 @@
         rest[0][...] = nn(turned, act_ref[...]).astype(BF16)
 
 
-def pre_back_kernel(
-    blks, lines, s_ref, dtwo_ref, slope_ref, wd_ref, wu_ref, upt_ref, dpre_ref, done_ref, *outs
-):
-    me, core = s_ref[ME], s_ref[CORE]
+def pre_back_kernel(blks, s_ref, dtwo_ref, slope_ref, wd_ref, wu_ref, dpre_ref, done_ref):
     low = dtwo_ref[...].astype(BF16)
     total = dtwo_ref[...]
     blk = wu_ref.shape[1] // blks
-    ups = rows_by_core(upt_ref, core, lines) if lines else ()
     for k in range(blks):
         at = slice(k * blk, (k + 1) * blk)
         dpre = (nt(low, wd_ref[at, :]) * slope_ref[:, at].astype(F32)).astype(BF16)
-        if not lines:
-            dpre_ref[:, at] = dpre
+        dpre_ref[:, at] = dpre
         total = total + nt(dpre, wu_ref[:, at])
-        for out, rows in zip(outs, ups):
-            prod = nn(rows, dpre).astype(BF16)
-            half = prod.shape[0]
-            for p in range(blk // half):
-                out[k ^ me, p * half : (p + 1) * half, :] = prod[:, p * half : (p + 1) * half]
     done_ref[...] = total
+
+
+def up_kernel(blks, lines, s_ref, dpre_ref, upt_ref, *outs):
     if not lines:
         outs[0][...] = nn(upt_ref[...], dpre_ref[...]).astype(BF16)
+        return
+    me, core = s_ref[ME], s_ref[CORE]
+    blk = dpre_ref.shape[1] // blks
+    high = outs[1].shape[1]
+    for which, rows in ((1, 1), (0, 0)):
+        mine = rows_by_core(upt_ref, core, lines)[rows]
+        half = mine.shape[0]
+        for k in range(blks):
+            prod = nn(mine, dpre_ref[:, k * blk : (k + 1) * blk]).astype(BF16)
+            if not which:
+                for p in range(blk // half):
+                    outs[0][k ^ me, p * half : (p + 1) * half, :] = prod[:, p * half : (p + 1) * half]
+                continue
+            for i, out in enumerate(outs[1:]):
+                for p in range(blk // half):
+                    low, end = max(p * half, i * high), min((p + 1) * half, (i + 1) * high)
+                    if low < end:
+                        out[k ^ me, low - i * high : end - i * high, :] = prod[
+                            low - p * half : end - p * half, p * half : (p + 1) * half
+                        ]
 
 
 def norm_back_kernel(
@@ -398,9 +411,10 @@
             rows = found[0][3]
 
             def add(at, size):
-                total = add_up(
-                    *(ref[leads + (pl.ds(at + row, size), col)] for ref, leads, row, _, col in found)
-                ).astype(BF16)
+                blocks = [
+                    ref[leads + (pl.ds(at + row, size), col)] for ref, leads, row, _, col in found
+                ]
+                total = sum(blocks[1:], blocks[0]) if len(blocks) == 2 else add_up(*blocks).astype(BF16)
                 for ref, leads, row, _, col, part in places:
                     ref[leads + (pl.ds(at + row, size), col)] = total[:, part]
 
@@ -442,22 +456,26 @@
         self.sizes = (cut, rows - cut)
         self.at = (slice(0, cut), slice(cut, rows))
 
-    def first(self, s, keeps, gots, cuts):
+    def first(self, s, keeps, gots):
         shapes = [(2, size, self.cols) for size in self.sizes for _ in range(2)]
         picks = ((0, 0, (0, 2)), (1, 0, (1, 3)), (2, 1, (0, 1)), (3, 1, (2, 3)))
+        wide = keeps[0].shape[1]
 
         def plan():
             found = []
             for out, half, group in picks:
                 start, end = self.at[half].start, self.at[half].stop
-                for i, (first, last) in enumerate(zip(cuts, cuts[1:])):
+                first = 0
+                for i, got in enumerate(gots):
+                    last = first + got.shape[1]
                     low, up = max(first, start), min(last, end)
-                    if low < up:
-                        for slot, j in enumerate(group):
-                            src = (j, slice(low - first, up - first), EVERY)
-                            here = (slot, slice(low - start, up - start), EVERY)
-                            terms = [(i, src), (len(keeps) + i, src)]
-                            found.append((terms, [(out, here, EVERY)]))
+                    kept = int(low >= wide)
+                    for slot, j in enumerate(group) if low < up else ():
+                        keep = (kept, (j, slice(low - kept * wide, up - kept * wide), EVERY))
+                        other = (len(keeps) + i, (j, slice(low - first, up - first), EVERY))
+                        here = (slot, slice(low - start, up - start), EVERY)
+                        found.append(([keep, other], [(out, here, EVERY)]))
+                    first = last
             return found
 
         return sums(s, (*keeps, *gots), shapes, plan)
@@ -672,30 +690,31 @@
     s = after(s, dtwo)
     if lines:
         ups = Halves(half + size, wide + high + 16, half)
-        up_out = [((blks, wide, half), BF16)] * 2
+        up_out = [((blks, wide, half), BF16)] + [((blks, wide // 3, half), BF16)] * 3
         thin_out = [((blks, high + 16, half), BF16)] * 2
         proj_out = [((blks, cols, half), BF16)] + [((blks, cols, 128), BF16)] * (half // 128)
     else:
         up_out = [((width, inner), BF16)]
         thin_out = [((width, width), BF16), ((16, width), BF16)]
         proj_out = [((3 * width, width), BF16)]
-    pre_shape = (16, 128) if lines else (rows, inner)
-    _, done, *up = call(
-        functools.partial(pre_back_kernel, blks, lines), s, (dtwo, slope, w_down, w_up, upt),
-        [(pre_shape, BF16), ((rows, width), F32)] + up_out, mib=8,
+    dpre, done = call(
+        functools.partial(pre_back_kernel, blks), s, (dtwo, slope, w_down, w_up),
+        [((rows, inner), BF16), ((rows, width), F32)], mib=8,
     )
     s = after(s, done)
     if lines:
         chip1 = down_first(s, down[0], swap(down[1], "batch", 1), lines)
         s = after(s, chip1[0])
+    up = call(functools.partial(up_kernel, blks, lines), s, (dpre, upt), up_out, mib=8)
+    s = after(s, up[0])
     dres, dctx, *thin = call(
         functools.partial(norm_back_kernel, blks, lines), s,
         (done, resid, gain1, gains, w_out, ctx), [((rows, width), F32), square] + thin_out, mib=8,
     )
     s = after(s, dctx)
     if lines:
-        gots = [swap(part, "batch", 1) for part in (up[1], thin[1])]
-        chip2 = ups.first(s, (up[0], thin[0]), gots, (0, wide, ups.rows))
+        gots = [swap(part, "batch", 1) for part in (*up[1:], thin[1])]
+        chip2 = ups.first(s, (up[0], thin[0]), gots)
         s = after(s, chip2[0])
     far_q, far_kv, *give = call(
         functools.partial(far_back_kernel, heads), s, (qkv, kv, ctx, dctx, far_lse, w_qkv),

time: 141 us -> 139 us (0.986)
  starting transfers between devices: 29.9 us -> 27 us
  waiting for transfers between devices: 30.5 us -> 32.4 us
    ppermute x24 -> x26, starting transfers between devices: 29.9 us -> 27 us  [swap(): lax.ppermute(block, axis, [(i, i ^ bits) for i in range(lax.axis_size(axi...]
    ppermute x24 -> x26, waiting for transfers between devices: 30.5 us -> 32.4 us  [swap(): lax.ppermute(block, axis, [(i, i ^ bits) for i in range(lax.axis_size(axi...]
    pallas_call x22 -> x23, Pallas kernels: 70.2 us -> 69.1 us  [call(): pl.pallas_call(kernel, in_specs=[pl.BlockSpec(memory_space=pltpu.SMEM)] +...]
  transfers between devices with their start and end apart: 24 -> 26, of which waited for: 9 -> 10; matrix products, arithmetic and copies ran while one was open for 3% -> 3% of each run, Pallas kernels for 36% -> 35%
where the time goes in v1:
time: 139 us
  Pallas kernels  69.1 us (50%)
  waiting for transfers between devices  32.4 us (23%)
  starting transfers between devices  27 us (19%)
  local copies, waits for them, and re-layouts  7.13 us (5%)
  between operations  2.22 us (2%)
    pallas_call x23, Pallas kernels, call(): pl.pallas_call(kernel, in_specs=[pl.BlockSpec(memory_space=pltpu.SMEM)] +...  69.1 us
    ppermute x26, waiting for transfers between devices, swap(): lax.ppermute(block, axis, [(i, i ^ bits) for i in range(lax.axis_size(axi...  32.4 us
    ppermute x26, starting transfers between devices, swap(): lax.ppermute(block, axis, [(i, i ^ bits) for i in range(lax.axis_size(axi...  27 us
    unnamed x20, local copies, waits for them, and re-layouts  3.18 us
  transfers between devices with their start and end apart: 26, of which 10 were waited for; matrix products, arithmetic and copies ran while one was open for 3% of the time, Pallas kernels for 35%

profile of v1, /device:TPU:0, one launch (start us, length us, event | category | flops | bytes accessed | tf_op | source)
XLA Modules:
  0.0 138.6 jit_solution(5765977792030269052)
XLA Ops:
  0.7 3.0 %collective-permute-start = (bf16[512,768]{1,0:T(8,128)(2,1)}, bf16[512,768]{1,0:T(8,128)(2,1)S(1)}, u32[]{:S(2)}, u32[]{:S(2)}) collective-permute-start(bf16[512,768]{1,0:T(8,128)(2,1)} %bitcast.19), channel_id=1, source_target_pairs={{0,8},{8,0},{16,24},{24,16},{1,9},{9,1},{17,25},{25,17},{2,10},{10... | collective-permute-start | bytes 2359304 | tf_op jit(solution)/shard_map/ppermute | solution.py:24
  3.7 0.6 constant_dynamic-slice_fusion
  5.5 0.8 select_reduce_fusion
  6.3 0.7 reshape.48.gain1_ref
  7.0 0.7 reshape.49.bias1_ref
  7.7 0.7 reshape.50.gain2_ref
  8.4 0.7 reshape.51.bias2_ref
  9.1 0.1 concatenate.3.s_ref
  9.2 2.0 %copy-done.2 = bf16[768,2304]{1,0:T(8,128)(2,1)S(1)} copy-done((bf16[768,2304]{1,0:T(8,128)(2,1)S(1)}, bf16[768,2304]{1,0:T(8,128)(2,1)}, u32[]{:S(2)}) %copy-start.2) | copy-done | bytes 3538968
  11.2 1.1 copy-done.7
  12.3 5.8 %shard_map.195 = (bf16[2304,512]{1,0:T(8,128)(2,1)S(1)}, bf16[768,512]{1,0:T(8,128)(2,1)S(1)}, f32[12,1,512]{2,1,0:T(1,128)S(1)}, bf16[2,512,384]{2,1,0:T(8,128)(2,1)S(1)}) custom-call(s32[17]{0:T(128)S(1)} %concatenate.3.s_ref, bf16[512,768]{1,0:T(8,128)(2,1)S(1)} %bitcast.20, bf16[768,2304]{1,0:T(8,128)(2,1)S(1)} %copy-done.2), custom_call_target="tpu_custom_call" | custom-call | flops 9201000448 | bytes 10000 | tf_op jit(solution)/shard_map/pallas_call | solution.py:41
  18.1 3.3 %collective-permute-done.xp_ref = bf16[512,768]{1,0:T(8,128)(2,1)S(1)} collective-permute-done((bf16[512,768]{1,0:T(8,128)(2,1)}, bf16[512,768]{1,0:T(8,128)(2,1)S(1)}, u32[]{:S(2)}, u32[]{:S(2)}) %collective-permute-start) | collective-permute-done | bytes 786464 | tf_op jit(solution)/shard_map/ppermute | solution.py:24
  21.5 17.6 %shard_map.196 = (bf16[1536,512]{1,0:T(8,128)(2,1)S(1)}, bf16[768,512]{1,0:T(8,128)(2,1)S(1)}, f32[12,1,512]{2,1,0:T(1,128)S(1)}, bf16[512,768]{1,0:T(8,128)(2,1...) custom-call(s32[17]{0:T(128)S(1)} %concatenate.3.s_ref, ...), custom_call_target="tpu_custom_call" | custom-call | flops 20700999680 | bytes 10000 | tf_op jit(solution)/shard_map/pallas_call | solution.py:41
  39.0 6.1 %shard_map.197 = (bf16[512,3072]{1,0:T(8,128)(2,1)S(1)}, f32[512,768]{1,0:T(8,128)S(1)}) custom-call(s32[17]{0:T(128)S(1)} %concatenate.3.s_ref, f32[512,768]{1,0:T(8,128)S(1)} %get-tuple-element.102.dtwo_ref, bf16[512,3072]{1,0:T(8,128)(2,1)S(1)} %get-tuple-element.104.slope_ref, bf16[3072,768]{1,0:T(8,128)(2,1)S(1)} %copy-done.5, ...), custom_call_target="tpu_custom_call" | custom-call | flops 1000000 | bytes 10000 | tf_op jit(solution)/shard_map/pallas_call | solution.py:41
  45.2 1.3 shard_map.198
  46.4 1.9 %collective-permute-start.6 = (bf16[2,4,192,384]{3,2,1,0:T(8,128)(2,1)S(1)}, bf16[2,4,192,384]{3,2,1,0:T(8,128)(2,1)S(1)}, u32[]{:S(2)}, u32[]{:S(2)}) collective-permute-start(bf16[2,4,192,384]{3,2,1,0:T(8,128)(2,1)S(1)} %get-tuple-element.137), channel_id=1, source_target_pairs={{0,2},{1,3},{2,0},{3,1},{4,6},{5,7},{6,4},{7,5},{8,10},{9,11},{10,... | collective-permute-start | bytes 3538952 | tf_op jit(solution)/shard_map/ppermute | solution.py:24
  48.3 3.2 %shard_map.199 = (bf16[4,768,384]{2,1,0:T(8,128)(2,1)S(1)}, bf16[4,256,384]{2,1,0:T(8,128)(2,1)S(1)}, bf16[4,256,384]{2,1,0:T(8,128)(2,1)S(1)}, bf16[4,256,384]{2,1,0:T(8,128)(2,1)S(1)}) custom-call(s32[17]{0:T(128)S(1)} %concatenate.3.s_ref, bf16[512,3072]{1,0:T(8,128)(2,1)S(1)} %get-tuple-element.111.dpre_ref, bf16[768,512]{1,0:T(8,128)(2,1)S(1)} %get-tuple-element.112.upt_ref), custom_call_target="tpu_custom_call" | custom-call | flops 1000000 | bytes 10000 | tf_op jit(solution)/shard_map/pallas_call | solution.py:41
  51.5 0.3 collective-permute-start.2
  51.8 0.3 collective-permute-start.3
  52.1 0.2 collective-permute-start.4
  52.3 3.0 %shard_map.200 = (f32[512,768]{1,0:T(8,128)S(1)}, bf16[768,512]{1,0:T(8,128)(2,1)S(1)}, bf16[4,208,384]{2,1,0:T(8,128)(2,1)S(1)}, bf16[4,208,384]{2,1,0:T(8,128)(2,1)S(1)}) custom-call(s32[17]{0:T(128)S(1)} %concatenate.3.s_ref, f32[512,768]{1,0:T(8,128)S(1)} %get-tuple-element.105.done_ref, f32[512,768]{1,0:T(8,128)S(1)} %get-tuple-element.115.resid_ref, ...), custom_call_target="tpu_custom_call" | custom-call | flops 1000000 | bytes 10000 | tf_op jit(solution)/shard_map/pallas_call | solution.py:41
  55.3 0.4 collective-permute-start.5
  55.7 1.8 %collective-permute-done.5.refs_5_ = bf16[4,208,384]{2,1,0:T(8,128)(2,1)S(1)} collective-permute-done((bf16[4,208,384]{2,1,0:T(8,128)(2,1)S(1)}, bf16[4,208,384]{2,1,0:T(8,128)(2,1)S(1)}, u32[]{:S(2)}, u32[]{:S(2)}) %collective-permute-start.5) | collective-permute-done | bytes 639008 | tf_op jit(solution)/shard_map/ppermute | solution.py:24
  57.5 1.6 %shard_map.201 = (bf16[2,480,384]{2,1,0:T(8,128)(2,1)S(1)}, bf16[2,480,384]{2,1,0:T(8,128)(2,1)S(1)}, bf16[2,496,384]{2,1,0:T(8,128)(2,1)S(1)}, bf16[2,496,384]{2,1,0:T(8,128)(2,1)S(1)}) custom-call(s32[17]{0:T(128)S(1)} %concatenate.3.s_ref, bf16[4,768,384]{2,1,0:T(8,128)(2,1)S(1)} %get-tuple-element.113.refs_0_, ...), custom_call_target="tpu_custom_call" | custom-call | flops 1000000 | bytes 10000 | tf_op jit(solution)/shard_map/pallas_call | solution.py:41
  59.1 1.6 %collective-permute-start.8 = (bf16[2,496,384]{2,1,0:T(8,128)(2,1)S(1)}, bf16[2,496,384]{2,1,0:T(8,128)(2,1)S(1)}, u32[]{:S(2)}, u32[]{:S(2)}) collective-permute-start(bf16[2,496,384]{2,1,0:T(8,128)(2,1)S(1)} %get-tuple-element.142), channel_id=1, source_target_pairs={{0,16},{8,24},{16,0},{24,8},{1,17},{9,25},{17,1},{25,9},{2,18},{10... | collective-permute-start | bytes 2285576 | tf_op jit(solution)/shard_map/ppermute | solution.py:24
  60.7 1.5 %collective-permute-start.7 = (bf16[2,480,384]{2,1,0:T(8,128)(2,1)S(1)}, bf16[2,480,384]{2,1,0:T(8,128)(2,1)S(1)}, u32[]{:S(2)}, u32[]{:S(2)}) collective-permute-start(bf16[2,480,384]{2,1,0:T(8,128)(2,1)S(1)} %get-tuple-element.141), channel_id=1, source_target_pairs={{0,8},{8,0},{16,24},{24,16},{1,9},{9,1},{17,25},{25,17},{2,10},{10... | collective-permute-start | bytes 2211848 | tf_op jit(solution)/shard_map/ppermute | solution.py:24
  62.2 6.2 %shard_map.202 = (bf16[384,512]{1,0:T(8,128)(2,1)S(1)}, bf16[768,512]{1,0:T(8,128)(2,1)S(1)}, bf16[640,512]{1,0:T(8,128)(2,1)S(1)}, bf16[128,512]{1,0:T(8,128)(2,1)S(1)}) custom-call(s32[17]{0:T(128)S(1)} %concatenate.3.s_ref, bf16[2304,512]{1,0:T(8,128)(2,1)S(1)} %get-tuple-element.99.qkv_ref, bf16[1536,512]{1,0:T(8,128)(2,1)S(1)} %get-tuple-element.127.kv_ref, ...), custom_call_target="tpu_custom_call" | custom-call | flops 1000000 | bytes 10000 | tf_op jit(solution)/shard_map/pallas_call | solution.py:41
  68.4 6.9 %shard_map.203 = (bf16[2304,512]{1,0:T(8,128)(2,1)S(1)}, bf16[4,576,384]{2,1,0:T(8,128)(2,1)S(1)}, bf16[4,576,128]{2,1,0:T(8,128)(2,1)S(1)}, bf16[4,576,128]{2,1,0:T(8,128)(2,1)S(1)}, bf16[4,576,128]{2,1,0:T(8,128)(2,1)S(1)}) custom-call(s32[17]{0:T(128)S(1)} %concatenate.3.s_ref, bf16[2304,512]{1,0:T(8,128)(2,1)S(1)} %get-tuple-element.99.qkv_ref, ...), custom_call_target="tpu_custom_call" | custom-call | flops 1000000 | bytes 10000 | tf_op jit(solution)/shard_map/pallas_call | solution.py:41
  75.3 0.5 collective-permute-start.10
  75.9 0.7 shard_map.204
  76.7 2.4 %collective-permute-done.7.refs_2_ = bf16[2,480,384]{2,1,0:T(8,128)(2,1)S(1)} collective-permute-done((bf16[2,480,384]{2,1,0:T(8,128)(2,1)S(1)}, bf16[2,480,384]{2,1,0:T(8,128)(2,1)S(1)}, u32[]{:S(2)}, u32[]{:S(2)}) %collective-permute-start.7) | collective-permute-done | bytes 737312 | tf_op jit(solution)/shard_map/ppermute | solution.py:24
  79.1 1.0 shard_map.205
  80.1 0.9 collective-permute-start.12
  80.9 2.6 %collective-permute-start.14 = (bf16[4,192,384]{2,1,0:T(8,128)(2,1)S(1)}, bf16[4,192,384]{2,1,0:T(8,128)(2,1)S(1)}, u32[]{:S(2)}, u32[]{:S(2)}) collective-permute-start(bf16[4,192,384]{2,1,0:T(8,128)(2,1)S(1)} %get-tuple-element.156), channel_id=1, source_target_pairs={{0,4},{1,5},{2,6},{3,7},{4,0},{5,1},{6,2},{7,3},{8,12},{9,13},{10,... | collective-permute-start | bytes 1769480 | tf_op jit(solution)/shard_map/ppermute | solution.py:24
  83.5 1.5 %collective-permute-start.13 = (bf16[496,384]{1,0:T(8,128)(2,1)S(1)}, bf16[496,384]{1,0:T(8,128)(2,1)S(1)}, u32[]{:S(2)}, u32[]{:S(2)}) collective-permute-start(bf16[496,384]{1,0:T(8,128)(2,1)S(1)} %get-tuple-element.153), channel_id=1, source_target_pairs={{0,8},{8,0},{16,24},{24,16},{1,9},{9,1},{17,25},{25,17},{2,10},{10... | collective-permute-start | bytes 1142792 | tf_op jit(solution)/shard_map/ppermute | solution.py:24
  85.0 1.8 %shard_map.206 = (bf16[576,384]{1,0:T(8,128)(2,1)S(1)}, bf16[576,384]{1,0:T(8,128)(2,1)S(1)}, bf16[576,384]{1,0:T(8,128)(2,1)S(1)}, bf16[576,384]{1,0:T(8,128)(2,1)S(1)}) custom-call(s32[17]{0:T(128)S(1)} %concatenate.3.s_ref, bf16[4,576,384]{2,1,0:T(8,128)(2,1)S(1)} %get-tuple-element.145.refs_0_, bf16[4,576,128]{2,1,0:T(8,128)(2,1)S(1)} %collective-permute-done.9.refs_1_, ...), custom_call_target="tpu_custom_call" | custom-call | flops 1000000 | bytes 10000 | tf_op jit(solution)/shard_map/pallas_call | solution.py:41
  86.8 0.6 collective-permute-start.15
  87.4 1.2 collective-permute-start.16
  88.7 2.5 %collective-permute-done.12.refs_2_ = bf16[480,384]{1,0:T(8,128)(2,1)S(1)} collective-permute-done((bf16[480,384]{1,0:T(8,128)(2,1)S(1)}, bf16[480,384]{1,0:T(8,128)(2,1)S(1)}, u32[]{:S(2)}, u32[]{:S(2)}) %collective-permute-start.12) | collective-permute-done | bytes 368672 | tf_op jit(solution)/shard_map/ppermute | solution.py:24
  91.1 2.3 %collective-permute-start.17 = (bf16[576,384]{1,0:T(8,128)(2,1)S(1)}, bf16[576,384]{1,0:T(8,128)(2,1)S(1)}, u32[]{:S(2)}, u32[]{:S(2)}) collective-permute-start(bf16[576,384]{1,0:T(8,128)(2,1)S(1)} %get-tuple-element.162), channel_id=1, source_target_pairs={{0,24},{8,16},{16,8},{24,0},{1,25},{9,17},{17,9},{25,1},{2,26},{10... | collective-permute-start | bytes 1327112 | tf_op jit(solution)/shard_map/ppermute | solution.py:24
  93.4 1.9 %collective-permute-done.13.refs_3_ = bf16[496,384]{1,0:T(8,128)(2,1)S(1)} collective-permute-done((bf16[496,384]{1,0:T(8,128)(2,1)S(1)}, bf16[496,384]{1,0:T(8,128)(2,1)S(1)}, u32[]{:S(2)}, u32[]{:S(2)}) %collective-permute-start.13) | collective-permute-done | bytes 380960 | tf_op jit(solution)/shard_map/ppermute | solution.py:24
  95.3 1.1 shard_map.207
  96.4 0.5 collective-permute-start.18
  96.9 12.0 %collective-permute-done.14.refs_1_ = bf16[4,192,384]{2,1,0:T(8,128)(2,1)S(1)} collective-permute-done((bf16[4,192,384]{2,1,0:T(8,128)(2,1)S(1)}, bf16[4,192,384]{2,1,0:T(8,128)(2,1)S(1)}, u32[]{:S(2)}, u32[]{:S(2)}) %collective-permute-start.14) | collective-permute-done | bytes 589856 | tf_op jit(solution)/shard_map/ppermute | solution.py:24
  108.9 0.7 shard_map.208
  109.6 1.0 collective-permute-start.19
  110.6 1.5 %collective-permute-start.23 = (bf16[640,512]{1,0:T(8,128)(2,1)S(1)}, bf16[640,512]{1,0:T(8,128)(2,1)S(1)}, u32[]{:S(2)}, u32[]{:S(2)}) collective-permute-start(bf16[640,512]{1,0:T(8,128)(2,1)S(1)} %get-tuple-element.181), channel_id=1, source_target_pairs={{0,8},{8,0},{16,24},{24,16},{1,9},{9,1},{17,25},{25,17},{2,10},{10... | collective-permute-start | bytes 1966088 | tf_op jit(solution)/shard_map/ppermute | solution.py:24
  112.1 2.5 %shard_map.209.own_ref = f32[768,512]{1,0:T(8,128)S(1)} custom-call(s32[17]{0:T(128)S(1)} %concatenate.3.s_ref, bf16[768,2304]{1,0:T(8,128)(2,1)S(1)} %copy-done.3, bf16[2304,512]{1,0:T(8,128)(2,1)S(1)} %get-tuple-element.135.dqkv_ref), custom_call_target="tpu_custom_call" | custom-call | flops 1000000 | bytes 10000 | tf_op jit(solution)/shard_map/pallas_call | solution.py:41
  114.6 1.7 %shard_map.210 = (bf16[2,576,96]{2,1,0:T(8,128)(2,1)S(1)}, bf16[2,576,96]{2,1,0:T(8,128)(2,1)S(1)}) custom-call(s32[17]{0:T(128)S(1)} %concatenate.3.s_ref, bf16[576,384]{1,0:T(8,128)(2,1)S(1)} %get-tuple-element.149.refs_0_, bf16[576,384]{1,0:T(8,128)(2,1)S(1)} %collective-permute-done.15.refs_1_, bf16[576,384]{1,0:T(8,128)(2,1)S(1)} %collective-permute-done.16.refs_2_, ...), custom_call_target="tpu_custom_call" | custom-call | flops 1000000 | bytes 10000 | tf_op jit(solution)/shard_map/pallas_call | solution.py:41
  116.5 0.2 collective-permute-done.18.refs_1_
  116.7 0.6 shard_map.211
  117.3 3.0 %collective-permute-start.22 = (bf16[208,512]{1,0:T(8,128)(2,1)S(1)}, bf16[208,512]{1,0:T(8,128)(2,1)S(1)}, u32[]{:S(2)}, u32[]{:S(2)}) collective-permute-start(bf16[208,512]{1,0:T(8,128)(2,1)S(1)} %get-tuple-element.176), channel_id=1, source_target_pairs={{0,4},{1,5},{2,6},{3,7},{4,0},{5,1},{6,2},{7,3},{8,12},{9,13},{10,... | collective-permute-start | bytes 638984 | tf_op jit(solution)/shard_map/ppermute | solution.py:24
  120.3 0.6 shard_map.212
  120.9 0.6 collective-permute-start.21
  121.5 1.5 %collective-permute-start.24 = (bf16[128,512]{1,0:T(8,128)(2,1)S(1)}, bf16[128,512]{1,0:T(8,128)(2,1)S(1)}, u32[]{:S(2)}, u32[]{:S(2)}) collective-permute-start(bf16[128,512]{1,0:T(8,128)(2,1)S(1)} %get-tuple-element.182), channel_id=1, source_target_pairs={{0,8},{8,0},{16,24},{24,16},{1,9},{9,1},{17,25},{25,17},{2,10},{10... | collective-permute-start | bytes 393224 | tf_op jit(solution)/shard_map/ppermute | solution.py:24
  123.0 6.3 %collective-permute-done.20.refs_1_ = bf16[2,576,96]{2,1,0:T(8,128)(2,1)S(1)} collective-permute-done((bf16[2,576,96]{2,1,0:T(8,128)(2,1)S(1)}, bf16[2,576,96]{2,1,0:T(8,128)(2,1)S(1)}, u32[]{:S(2)}, u32[]{:S(2)}) %collective-permute-start.20) | collective-permute-done | bytes 221216 | tf_op jit(solution)/shard_map/ppermute | solution.py:24
  129.3 0.7 shard_map.213
  130.1 1.3 collective-permute-done.21.refs_1_
  131.4 1.3 shard_map.214
  132.7 1.3 shard_map.215
  134.0 0.5 slice_bitcast_fusion
  134.6 1.9 %shard_map.216 = bf16[512,768]{1,0:T(8,128)(2,1)} custom-call(s32[17]{0:T(128)S(1)} %concatenate.3.s_ref, f32[768,512]{1,0:T(8,128)S(1)} %shard_map.209.own_ref, bf16[640,512]{1,0:T(8,128)(2,1)S(1)} %collective-permute-done.23.got_ref, bf16[128,512]{1,0:T(8,128)(2,1)S(1)} %collective-permute-done.24.rest_ref, f32[512,768]{1,0:T(8,128)S(1)} %get-tuple-element.183.dres_ref), custom_call_target="tpu_custom_call" | custom-call | flops 1000000 | bytes 10000 | tf_op jit(solution)/shard_map/pallas_call | solution.py:41
  136.5 0.7 collective-permute-done.25.refs_1_
  137.2 1.4 %shard_map.217 = f32[96,576]{1,0:T(8,128)} custom-call(s32[17]{0:T(128)S(1)} %concatenate.3.s_ref, bf16[576,96]{1,0:T(8,128)(2,1)S(1)} %get-tuple-element.172.refs_0_, bf16[576,96]{1,0:T(8,128)(2,1)S(1)} %collective-permute-done.25.refs_1_), custom_call_target="tpu_custom_call" | custom-call | flops 1000000 | bytes 10000 | tf_op jit(solution)/shard_map/pallas_call | solution.py:41
  (39 shorter events, 0.4 us)
Async XLA Ops:
  0.6 3.0 %copy-start = (s32[2,1]{0,1:T(1,128)S(1)}, s32[2,1]{0,1:T(1,128)}, u32[]{:S(2)}) copy-start(s32[2,1]{0,1:T(1,128)} %param.13) | copy-start | bytes 28
  0.7 20.8 %collective-permute-start = (bf16[512,768]{1,0:T(8,128)(2,1)}, bf16[512,768]{1,0:T(8,128)(2,1)S(1)}, u32[]{:S(2)}, u32[]{:S(2)}) collective-permute-start(bf16[512,768]{1,0:T(8,128)(2,1)} %bitcast.19), channel_id=1, source_target_pairs={{0,8},{8,0},{16,24},{24,16},{1,9},{9,1},{17,25},{25,17},{2,10},{10... | collective-permute-start | bytes 2359304 | tf_op jit(solution)/shard_map/ppermute | solution.py:24
  9.2 2.0 %copy-start.2 = (bf16[768,2304]{1,0:T(8,128)(2,1)S(1)}, bf16[768,2304]{1,0:T(8,128)(2,1)}, u32[]{:S(2)}) copy-start(bf16[768,2304]{1,0:T(8,128)(2,1)} %w_ref.7) | copy-start | bytes 10616836
  11.2 1.1 copy-start.7
  12.3 9.1 %copy-start.3 = (bf16[768,2304]{1,0:T(8,128)(2,1)S(1)}, bf16[768,2304]{1,0:T(8,128)(2,1)}, u32[]{:S(2)}) copy-start(bf16[768,2304]{1,0:T(8,128)(2,1)} %w_ref.7) | copy-start | bytes 10616836
  12.3 9.1 %copy-start.4 = (bf16[768,3072]{1,0:T(8,128)(2,1)S(1)}, bf16[768,3072]{1,0:T(8,128)(2,1)}, u32[]{:S(2)}) copy-start(bf16[768,3072]{1,0:T(8,128)(2,1)} %wu_ref.3) | copy-start | bytes 14155780
  12.3 9.1 %copy-start.5 = (bf16[3072,768]{1,0:T(8,128)(2,1)S(1)}, bf16[3072,768]{1,0:T(8,128)(2,1)}, u32[]{:S(2)}) copy-start(bf16[3072,768]{1,0:T(8,128)(2,1)} %wd_ref.3) | copy-start | bytes 14155780
  12.3 9.1 %copy-start.6 = (bf16[768,768]{1,0:T(8,128)(2,1)S(1)}, bf16[768,768]{1,0:T(8,128)(2,1)}, u32[]{:S(2)}) copy-start(bf16[768,768]{1,0:T(8,128)(2,1)} %wo_ref.3) | copy-start | bytes 3538948
  12.3 9.1 %copy-start.8 = (bf16[1,1,512,768]{3,2,1,0:T(8,128)(2,1)S(1)}, bf16[1,1,512,768]{3,2,1,0:T(8,128)(2,1)}, u32[]{:S(2)}) copy-start(bf16[1,1,512,768]{3,2,1,0:T(8,128)(2,1)} %param.12) | copy-start | bytes 2359300
  12.3 9.1 %copy-start.9 = (bf16[1,1,512,768]{3,2,1,0:T(8,128)(2,1)S(1)}, bf16[1,1,512,768]{3,2,1,0:T(8,128)(2,1)}, u32[]{:S(2)}) copy-start(bf16[1,1,512,768]{3,2,1,0:T(8,128)(2,1)} %param.23) | copy-start | bytes 2359300
  39.0 6.1 %collective-permute-start.1 = (bf16[4,192,1536]{2,1,0:T(8,128)(2,1)S(1)}, bf16[4,192,1536]{2,1,0:T(8,128)(2,1)S(1)}, u32[]{:S(2)}, u32[]{:S(2)}) collective-permute-start(bf16[4,192,1536]{2,1,0:T(8,128)(2,1)S(1)} %get-tuple-element.108), channel_id=1, source_target_pairs={{0,1},{1,0},{2,3},{3,2},{4,5},{5,4},{6,7},{7,6},{8,9},{9,8},{10,11... | collective-permute-start | bytes 7077896 | tf_op jit(solution)/shard_map/ppermute | solution.py:24
  46.4 29.4 %collective-permute-start.6 = (bf16[2,4,192,384]{3,2,1,0:T(8,128)(2,1)S(1)}, bf16[2,4,192,384]{3,2,1,0:T(8,128)(2,1)S(1)}, u32[]{:S(2)}, u32[]{:S(2)}) collective-permute-start(bf16[2,4,192,384]{3,2,1,0:T(8,128)(2,1)S(1)} %get-tuple-element.137), channel_id=1, source_target_pairs={{0,2},{1,3},{2,0},{3,1},{4,6},{5,7},{6,4},{7,5},{8,10},{9,11},{10,... | collective-permute-start | bytes 3538952 | tf_op jit(solution)/shard_map/ppermute | solution.py:24
  51.5 6.0 %collective-permute-start.2 = (bf16[4,256,384]{2,1,0:T(8,128)(2,1)S(1)}, bf16[4,256,384]{2,1,0:T(8,128)(2,1)S(1)}, u32[]{:S(2)}, u32[]{:S(2)}) collective-permute-start(bf16[4,256,384]{2,1,0:T(8,128)(2,1)S(1)} %get-tuple-element.121), channel_id=1, source_target_pairs={{0,1},{1,0},{2,3},{3,2},{4,5},{5,4},{6,7},{7,6},{8,9},{9,8},{10,11... | collective-permute-start | bytes 2359304 | tf_op jit(solution)/shard_map/ppermute | solution.py:24
  51.8 5.7 %collective-permute-start.3 = (bf16[4,256,384]{2,1,0:T(8,128)(2,1)S(1)}, bf16[4,256,384]{2,1,0:T(8,128)(2,1)S(1)}, u32[]{:S(2)}, u32[]{:S(2)}) collective-permute-start(bf16[4,256,384]{2,1,0:T(8,128)(2,1)S(1)} %get-tuple-element.122), channel_id=1, source_target_pairs={{0,1},{1,0},{2,3},{3,2},{4,5},{5,4},{6,7},{7,6},{8,9},{9,8},{10,11... | collective-permute-start | bytes 2359304 | tf_op jit(solution)/shard_map/ppermute | solution.py:24
  52.1 5.4 %collective-permute-start.4 = (bf16[4,256,384]{2,1,0:T(8,128)(2,1)S(1)}, bf16[4,256,384]{2,1,0:T(8,128)(2,1)S(1)}, u32[]{:S(2)}, u32[]{:S(2)}) collective-permute-start(bf16[4,256,384]{2,1,0:T(8,128)(2,1)S(1)} %get-tuple-element.123), channel_id=1, source_target_pairs={{0,1},{1,0},{2,3},{3,2},{4,5},{5,4},{6,7},{7,6},{8,9},{9,8},{10,11... | collective-permute-start | bytes 2359304 | tf_op jit(solution)/shard_map/ppermute | solution.py:24
  55.3 2.1 %collective-permute-start.5 = (bf16[4,208,384]{2,1,0:T(8,128)(2,1)S(1)}, bf16[4,208,384]{2,1,0:T(8,128)(2,1)S(1)}, u32[]{:S(2)}, u32[]{:S(2)}) collective-permute-start(bf16[4,208,384]{2,1,0:T(8,128)(2,1)S(1)} %get-tuple-element.124), channel_id=1, source_target_pairs={{0,1},{1,0},{2,3},{3,2},{4,5},{5,4},{6,7},{7,6},{8,9},{9,8},{10,11... | collective-permute-start | bytes 1916936 | tf_op jit(solution)/shard_map/ppermute | solution.py:24
  59.1 20.0 %collective-permute-start.8 = (bf16[2,496,384]{2,1,0:T(8,128)(2,1)S(1)}, bf16[2,496,384]{2,1,0:T(8,128)(2,1)S(1)}, u32[]{:S(2)}, u32[]{:S(2)}) collective-permute-start(bf16[2,496,384]{2,1,0:T(8,128)(2,1)S(1)} %get-tuple-element.142), channel_id=1, source_target_pairs={{0,16},{8,24},{16,0},{24,8},{1,17},{9,25},{17,1},{25,9},{2,18},{10... | collective-permute-start | bytes 2285576 | tf_op jit(solution)/shard_map/ppermute | solution.py:24
  60.7 18.4 %collective-permute-start.7 = (bf16[2,480,384]{2,1,0:T(8,128)(2,1)S(1)}, bf16[2,480,384]{2,1,0:T(8,128)(2,1)S(1)}, u32[]{:S(2)}, u32[]{:S(2)}) collective-permute-start(bf16[2,480,384]{2,1,0:T(8,128)(2,1)S(1)} %get-tuple-element.141), channel_id=1, source_target_pairs={{0,8},{8,0},{16,24},{24,16},{1,9},{9,1},{17,25},{25,17},{2,10},{10... | collective-permute-start | bytes 2211848 | tf_op jit(solution)/shard_map/ppermute | solution.py:24
  75.2 8.3 %collective-permute-start.9 = (bf16[4,576,128]{2,1,0:T(8,128)(2,1)S(1)}, bf16[4,576,128]{2,1,0:T(8,128)(2,1)S(1)}, u32[]{:S(2)}, u32[]{:S(2)}) collective-permute-start(bf16[4,576,128]{2,1,0:T(8,128)(2,1)S(1)} %get-tuple-element.146), channel_id=1, source_target_pairs={{0,1},{1,0},{2,3},{3,2},{4,5},{5,4},{6,7},{7,6},{8,9},{9,8},{10,11... | collective-permute-start | bytes 1769480 | tf_op jit(solution)/shard_map/ppermute | solution.py:24
  75.3 9.7 %collective-permute-start.10 = (bf16[4,576,128]{2,1,0:T(8,128)(2,1)S(1)}, bf16[4,576,128]{2,1,0:T(8,128)(2,1)S(1)}, u32[]{:S(2)}, u32[]{:S(2)}) collective-permute-start(bf16[4,576,128]{2,1,0:T(8,128)(2,1)S(1)} %get-tuple-element.147), channel_id=1, source_target_pairs={{0,1},{1,0},{2,3},{3,2},{4,5},{5,4},{6,7},{7,6},{8,9},{9,8},{10,11... | collective-permute-start | bytes 1769480 | tf_op jit(solution)/shard_map/ppermute | solution.py:24
  75.8 9.2 %collective-permute-start.11 = (bf16[4,576,128]{2,1,0:T(8,128)(2,1)S(1)}, bf16[4,576,128]{2,1,0:T(8,128)(2,1)S(1)}, u32[]{:S(2)}, u32[]{:S(2)}) collective-permute-start(bf16[4,576,128]{2,1,0:T(8,128)(2,1)S(1)} %get-tuple-element.148), channel_id=1, source_target_pairs={{0,1},{1,0},{2,3},{3,2},{4,5},{5,4},{6,7},{7,6},{8,9},{9,8},{10,11... | collective-permute-start | bytes 1769480 | tf_op jit(solution)/shard_map/ppermute | solution.py:24
  80.1 11.0 %collective-permute-start.12 = (bf16[480,384]{1,0:T(8,128)(2,1)S(1)}, bf16[480,384]{1,0:T(8,128)(2,1)S(1)}, u32[]{:S(2)}, u32[]{:S(2)}) collective-permute-start(bf16[480,384]{1,0:T(8,128)(2,1)S(1)} %get-tuple-element.152), channel_id=1, source_target_pairs={{0,16},{8,24},{16,0},{24,8},{1,17},{9,25},{17,1},{25,9},{2,18},{10... | collective-permute-start | bytes 1105928 | tf_op jit(solution)/shard_map/ppermute | solution.py:24
  80.9 28.0 %collective-permute-start.14 = (bf16[4,192,384]{2,1,0:T(8,128)(2,1)S(1)}, bf16[4,192,384]{2,1,0:T(8,128)(2,1)S(1)}, u32[]{:S(2)}, u32[]{:S(2)}) collective-permute-start(bf16[4,192,384]{2,1,0:T(8,128)(2,1)S(1)} %get-tuple-element.156), channel_id=1, source_target_pairs={{0,4},{1,5},{2,6},{3,7},{4,0},{5,1},{6,2},{7,3},{8,12},{9,13},{10,... | collective-permute-start | bytes 1769480 | tf_op jit(solution)/shard_map/ppermute | solution.py:24
  83.5 11.8 %collective-permute-start.13 = (bf16[496,384]{1,0:T(8,128)(2,1)S(1)}, bf16[496,384]{1,0:T(8,128)(2,1)S(1)}, u32[]{:S(2)}, u32[]{:S(2)}) collective-permute-start(bf16[496,384]{1,0:T(8,128)(2,1)S(1)} %get-tuple-element.153), channel_id=1, source_target_pairs={{0,8},{8,0},{16,24},{24,16},{1,9},{9,1},{17,25},{25,17},{2,10},{10... | collective-permute-start | bytes 1142792 | tf_op jit(solution)/shard_map/ppermute | solution.py:24
  86.8 23.8 %collective-permute-start.15 = (bf16[576,384]{1,0:T(8,128)(2,1)S(1)}, bf16[576,384]{1,0:T(8,128)(2,1)S(1)}, u32[]{:S(2)}, u32[]{:S(2)}) collective-permute-start(bf16[576,384]{1,0:T(8,128)(2,1)S(1)} %get-tuple-element.160), channel_id=1, source_target_pairs={{0,8},{8,0},{16,24},{24,16},{1,9},{9,1},{17,25},{25,17},{2,10},{10... | collective-permute-start | bytes 1327112 | tf_op jit(solution)/shard_map/ppermute | solution.py:24
  87.4 27.2 %collective-permute-start.16 = (bf16[576,384]{1,0:T(8,128)(2,1)S(1)}, bf16[576,384]{1,0:T(8,128)(2,1)S(1)}, u32[]{:S(2)}, u32[]{:S(2)}) collective-permute-start(bf16[576,384]{1,0:T(8,128)(2,1)S(1)} %get-tuple-element.161), channel_id=1, source_target_pairs={{0,16},{8,24},{16,0},{24,8},{1,17},{9,25},{17,1},{25,9},{2,18},{10... | collective-permute-start | bytes 1327112 | tf_op jit(solution)/shard_map/ppermute | solution.py:24
  91.1 23.5 %collective-permute-start.17 = (bf16[576,384]{1,0:T(8,128)(2,1)S(1)}, bf16[576,384]{1,0:T(8,128)(2,1)S(1)}, u32[]{:S(2)}, u32[]{:S(2)}) collective-permute-start(bf16[576,384]{1,0:T(8,128)(2,1)S(1)} %get-tuple-element.162), channel_id=1, source_target_pairs={{0,24},{8,16},{16,8},{24,0},{1,25},{9,17},{17,9},{25,1},{2,26},{10... | collective-permute-start | bytes 1327112 | tf_op jit(solution)/shard_map/ppermute | solution.py:24
  96.4 20.2 %collective-permute-start.18 = (bf16[2,208,512]{2,1,0:T(8,128)(2,1)S(1)}, bf16[2,208,512]{2,1,0:T(8,128)(2,1)S(1)}, u32[]{:S(2)}, u32[]{:S(2)}) collective-permute-start(bf16[2,208,512]{2,1,0:T(8,128)(2,1)S(1)} %get-tuple-element.165), channel_id=1, source_target_pairs={{0,2},{1,3},{2,0},{3,1},{4,6},{5,7},{6,4},{7,5},{8,10},{9,11},{10,... | collective-permute-start | bytes 1277960 | tf_op jit(solution)/shard_map/ppermute | solution.py:24
  109.6 10.7 %collective-permute-start.19 = (bf16[2,192,384]{2,1,0:T(8,128)(2,1)S(1)}, bf16[2,192,384]{2,1,0:T(8,128)(2,1)S(1)}, u32[]{:S(2)}, u32[]{:S(2)}) collective-permute-start(bf16[2,192,384]{2,1,0:T(8,128)(2,1)S(1)} %get-tuple-element.168), channel_id=1, source_target_pairs={{0,16},{8,24},{16,0},{24,8},{1,17},{9,25},{17,1},{25,9},{2,18},{10... | collective-permute-start | bytes 884744 | tf_op jit(solution)/shard_map/ppermute | solution.py:24
  110.6 23.9 %collective-permute-start.23 = (bf16[640,512]{1,0:T(8,128)(2,1)S(1)}, bf16[640,512]{1,0:T(8,128)(2,1)S(1)}, u32[]{:S(2)}, u32[]{:S(2)}) collective-permute-start(bf16[640,512]{1,0:T(8,128)(2,1)S(1)} %get-tuple-element.181), channel_id=1, source_target_pairs={{0,8},{8,0},{16,24},{24,16},{1,9},{9,1},{17,25},{25,17},{2,10},{10... | collective-permute-start | bytes 1966088 | tf_op jit(solution)/shard_map/ppermute | solution.py:24
  116.4 12.9 %collective-permute-start.20 = (bf16[2,576,96]{2,1,0:T(8,128)(2,1)S(1)}, bf16[2,576,96]{2,1,0:T(8,128)(2,1)S(1)}, u32[]{:S(2)}, u32[]{:S(2)}) collective-permute-start(bf16[2,576,96]{2,1,0:T(8,128)(2,1)S(1)} %get-tuple-element.171), channel_id=1, source_target_pairs={{0,2},{1,3},{2,0},{3,1},{4,6},{5,7},{6,4},{7,5},{8,10},{9,11},{10,... | collective-permute-start | bytes 663560 | tf_op jit(solution)/shard_map/ppermute | solution.py:24
  117.3 15.4 %collective-permute-start.22 = (bf16[208,512]{1,0:T(8,128)(2,1)S(1)}, bf16[208,512]{1,0:T(8,128)(2,1)S(1)}, u32[]{:S(2)}, u32[]{:S(2)}) collective-permute-start(bf16[208,512]{1,0:T(8,128)(2,1)S(1)} %get-tuple-element.176), channel_id=1, source_target_pairs={{0,4},{1,5},{2,6},{3,7},{4,0},{5,1},{6,2},{7,3},{8,12},{9,13},{10,... | collective-permute-start | bytes 638984 | tf_op jit(solution)/shard_map/ppermute | solution.py:24
  120.9 10.5 %collective-permute-start.21 = (bf16[192,384]{1,0:T(8,128)(2,1)S(1)}, bf16[192,384]{1,0:T(8,128)(2,1)S(1)}, u32[]{:S(2)}, u32[]{:S(2)}) collective-permute-start(bf16[192,384]{1,0:T(8,128)(2,1)S(1)} %get-tuple-element.174), channel_id=1, source_target_pairs={{0,8},{8,0},{16,24},{24,16},{1,9},{9,1},{17,25},{25,17},{2,10},{10... | collective-permute-start | bytes 442376 | tf_op jit(solution)/shard_map/ppermute | solution.py:24
  121.5 13.0 %collective-permute-start.24 = (bf16[128,512]{1,0:T(8,128)(2,1)S(1)}, bf16[128,512]{1,0:T(8,128)(2,1)S(1)}, u32[]{:S(2)}, u32[]{:S(2)}) collective-permute-start(bf16[128,512]{1,0:T(8,128)(2,1)S(1)} %get-tuple-element.182), channel_id=1, source_target_pairs={{0,8},{8,0},{16,24},{24,16},{1,9},{9,1},{17,25},{25,17},{2,10},{10... | collective-permute-start | bytes 393224 | tf_op jit(solution)/shard_map/ppermute | solution.py:24
  130.0 7.2 %collective-permute-start.25 = (bf16[576,96]{1,0:T(8,128)(2,1)S(1)}, bf16[576,96]{1,0:T(8,128)(2,1)S(1)}, u32[]{:S(2)}, u32[]{:S(2)}) collective-permute-start(bf16[576,96]{1,0:T(8,128)(2,1)S(1)} %get-tuple-element.185), channel_id=1, source_target_pairs={{0,4},{1,5},{2,6},{3,7},{4,0},{5,1},{6,2},{7,3},{8,12},{9,13},{10,... | collective-permute-start | bytes 331784 | tf_op jit(solution)/shard_map/ppermute | solution.py:24
  134.5 4.1 %copy-start.1 = (s32[2,1]{0,1:T(1,128)S(1)}, s32[2,1]{0,1:T(1,128)}, u32[]{:S(2)}) copy-start(s32[2,1]{0,1:T(1,128)} %param.13) | copy-start | bytes 28

commit v2 on v1

--- a/solution.py
+++ b/solution.py
@@ -15,7 +15,7 @@
 NEG = -1e30
 LOG2E = math.log2(math.e)
 FF_BLOCKS = 4
-STEP = 48
+STEP = 96
 EVERY = slice(None)
 ME, CORE, LINE, NEAR, FAR, ORDER = range(6)
 

time: 139 us -> 138 us (level)
  Pallas kernels: 69.1 us -> 67.5 us
    pallas_call x23, Pallas kernels: 69.1 us -> 67.5 us  [call(): pl.pallas_call(kernel, in_specs=[pl.BlockSpec(memory_space=pltpu.SMEM)] +...]
  transfers between devices with their start and end apart: 26 -> 26, of which waited for: 10 -> 10; matrix products, arithmetic and copies ran while one was open for 3% -> 3% of each run, Pallas kernels for 35% -> 34%
where the time goes in v2:
time: 138 us
  Pallas kernels  67.5 us (49%)
  waiting for transfers between devices  33.7 us (24%)
  starting transfers between devices  26.3 us (19%)
  local copies, waits for them, and re-layouts  7.13 us (5%)
  between operations  2.2 us (2%)
    pallas_call x23, Pallas kernels, call(): pl.pallas_call(kernel, in_specs=[pl.BlockSpec(memory_space=pltpu.SMEM)] +...  67.5 us
    ppermute x26, waiting for transfers between devices, swap(): lax.ppermute(block, axis, [(i, i ^ bits) for i in range(lax.axis_size(axi...  33.7 us
    ppermute x26, starting transfers between devices, swap(): lax.ppermute(block, axis, [(i, i ^ bits) for i in range(lax.axis_size(axi...  26.3 us
    unnamed x20, local copies, waits for them, and re-layouts  3.18 us
  transfers between devices with their start and end apart: 26, of which 10 were waited for; matrix products, arithmetic and copies ran while one was open for 3% of the time, Pallas kernels for 34%

profile of v2, /device:TPU:0, one launch (start us, length us, event | category | flops | bytes accessed | tf_op | source)
XLA Modules:
  0.0 137.6 jit_solution(13432042513397861184)
XLA Ops:
  0.7 3.0 %collective-permute-start = (bf16[512,768]{1,0:T(8,128)(2,1)}, bf16[512,768]{1,0:T(8,128)(2,1)S(1)}, u32[]{:S(2)}, u32[]{:S(2)}) collective-permute-start(bf16[512,768]{1,0:T(8,128)(2,1)} %bitcast.19), channel_id=1, source_target_pairs={{0,8},{8,0},{16,24},{24,16},{1,9},{9,1},{17,25},{25,17},{2,10},{10... | collective-permute-start | bytes 2359304 | tf_op jit(solution)/shard_map/ppermute | solution.py:24
  3.7 0.6 constant_dynamic-slice_fusion
  5.5 0.8 select_reduce_fusion
  6.3 0.7 reshape.48.gain1_ref
  7.0 0.7 reshape.49.bias1_ref
  7.7 0.7 reshape.50.gain2_ref
  8.4 0.7 reshape.51.bias2_ref
  9.1 0.1 concatenate.3.s_ref
  9.2 2.0 %copy-done.2 = bf16[768,2304]{1,0:T(8,128)(2,1)S(1)} copy-done((bf16[768,2304]{1,0:T(8,128)(2,1)S(1)}, bf16[768,2304]{1,0:T(8,128)(2,1)}, u32[]{:S(2)}) %copy-start.2) | copy-done | bytes 3538968
  11.2 1.1 copy-done.7
  12.3 5.8 %shard_map.195 = (bf16[2304,512]{1,0:T(8,128)(2,1)S(1)}, bf16[768,512]{1,0:T(8,128)(2,1)S(1)}, f32[12,1,512]{2,1,0:T(1,128)S(1)}, bf16[2,512,384]{2,1,0:T(8,128)(2,1)S(1)}) custom-call(s32[17]{0:T(128)S(1)} %concatenate.3.s_ref, bf16[512,768]{1,0:T(8,128)(2,1)S(1)} %bitcast.20, bf16[768,2304]{1,0:T(8,128)(2,1)S(1)} %copy-done.2), custom_call_target="tpu_custom_call" | custom-call | flops 9201000448 | bytes 10000 | tf_op jit(solution)/shard_map/pallas_call | solution.py:41
  18.1 3.3 %collective-permute-done.xp_ref = bf16[512,768]{1,0:T(8,128)(2,1)S(1)} collective-permute-done((bf16[512,768]{1,0:T(8,128)(2,1)}, bf16[512,768]{1,0:T(8,128)(2,1)S(1)}, u32[]{:S(2)}, u32[]{:S(2)}) %collective-permute-start) | collective-permute-done | bytes 786464 | tf_op jit(solution)/shard_map/ppermute | solution.py:24
  21.5 17.6 %shard_map.196 = (bf16[1536,512]{1,0:T(8,128)(2,1)S(1)}, bf16[768,512]{1,0:T(8,128)(2,1)S(1)}, f32[12,1,512]{2,1,0:T(1,128)S(1)}, bf16[512,768]{1,0:T(8,128)(2,1...) custom-call(s32[17]{0:T(128)S(1)} %concatenate.3.s_ref, ...), custom_call_target="tpu_custom_call" | custom-call | flops 20700999680 | bytes 10000 | tf_op jit(solution)/shard_map/pallas_call | solution.py:41
  39.0 6.1 %shard_map.197 = (bf16[512,3072]{1,0:T(8,128)(2,1)S(1)}, f32[512,768]{1,0:T(8,128)S(1)}) custom-call(s32[17]{0:T(128)S(1)} %concatenate.3.s_ref, f32[512,768]{1,0:T(8,128)S(1)} %get-tuple-element.102.dtwo_ref, bf16[512,3072]{1,0:T(8,128)(2,1)S(1)} %get-tuple-element.104.slope_ref, bf16[3072,768]{1,0:T(8,128)(2,1)S(1)} %copy-done.5, ...), custom_call_target="tpu_custom_call" | custom-call | flops 1000000 | bytes 10000 | tf_op jit(solution)/shard_map/pallas_call | solution.py:41
  45.2 1.1 shard_map.198
  46.2 1.9 %collective-permute-start.6 = (bf16[2,4,192,384]{3,2,1,0:T(8,128)(2,1)S(1)}, bf16[2,4,192,384]{3,2,1,0:T(8,128)(2,1)S(1)}, u32[]{:S(2)}, u32[]{:S(2)}) collective-permute-start(bf16[2,4,192,384]{3,2,1,0:T(8,128)(2,1)S(1)} %get-tuple-element.137), channel_id=1, source_target_pairs={{0,2},{1,3},{2,0},{3,1},{4,6},{5,7},{6,4},{7,5},{8,10},{9,11},{10,... | collective-permute-start | bytes 3538952 | tf_op jit(solution)/shard_map/ppermute | solution.py:24
  48.1 3.2 %shard_map.199 = (bf16[4,768,384]{2,1,0:T(8,128)(2,1)S(1)}, bf16[4,256,384]{2,1,0:T(8,128)(2,1)S(1)}, bf16[4,256,384]{2,1,0:T(8,128)(2,1)S(1)}, bf16[4,256,384]{2,1,0:T(8,128)(2,1)S(1)}) custom-call(s32[17]{0:T(128)S(1)} %concatenate.3.s_ref, bf16[512,3072]{1,0:T(8,128)(2,1)S(1)} %get-tuple-element.111.dpre_ref, bf16[768,512]{1,0:T(8,128)(2,1)S(1)} %get-tuple-element.112.upt_ref), custom_call_target="tpu_custom_call" | custom-call | flops 1000000 | bytes 10000 | tf_op jit(solution)/shard_map/pallas_call | solution.py:41
  51.3 0.3 collective-permute-start.2
  51.6 0.3 collective-permute-start.3
  51.9 0.2 collective-permute-start.4
  52.1 3.0 %shard_map.200 = (f32[512,768]{1,0:T(8,128)S(1)}, bf16[768,512]{1,0:T(8,128)(2,1)S(1)}, bf16[4,208,384]{2,1,0:T(8,128)(2,1)S(1)}, bf16[4,208,384]{2,1,0:T(8,128)(2,1)S(1)}) custom-call(s32[17]{0:T(128)S(1)} %concatenate.3.s_ref, f32[512,768]{1,0:T(8,128)S(1)} %get-tuple-element.105.done_ref, f32[512,768]{1,0:T(8,128)S(1)} %get-tuple-element.115.resid_ref, ...), custom_call_target="tpu_custom_call" | custom-call | flops 1000000 | bytes 10000 | tf_op jit(solution)/shard_map/pallas_call | solution.py:41
  55.1 0.4 collective-permute-start.5
  55.5 1.8 %collective-permute-done.5.refs_5_ = bf16[4,208,384]{2,1,0:T(8,128)(2,1)S(1)} collective-permute-done((bf16[4,208,384]{2,1,0:T(8,128)(2,1)S(1)}, bf16[4,208,384]{2,1,0:T(8,128)(2,1)S(1)}, u32[]{:S(2)}, u32[]{:S(2)}) %collective-permute-start.5) | collective-permute-done | bytes 639008 | tf_op jit(solution)/shard_map/ppermute | solution.py:24
  57.3 1.4 %shard_map.201 = (bf16[2,480,384]{2,1,0:T(8,128)(2,1)S(1)}, bf16[2,480,384]{2,1,0:T(8,128)(2,1)S(1)}, bf16[2,496,384]{2,1,0:T(8,128)(2,1)S(1)}, bf16[2,496,384]{2,1,0:T(8,128)(2,1)S(1)}) custom-call(s32[17]{0:T(128)S(1)} %concatenate.3.s_ref, bf16[4,768,384]{2,1,0:T(8,128)(2,1)S(1)} %get-tuple-element.113.refs_0_, ...), custom_call_target="tpu_custom_call" | custom-call | flops 1000000 | bytes 10000 | tf_op jit(solution)/shard_map/pallas_call | solution.py:41
  58.7 1.6 %collective-permute-start.8 = (bf16[2,496,384]{2,1,0:T(8,128)(2,1)S(1)}, bf16[2,496,384]{2,1,0:T(8,128)(2,1)S(1)}, u32[]{:S(2)}, u32[]{:S(2)}) collective-permute-start(bf16[2,496,384]{2,1,0:T(8,128)(2,1)S(1)} %get-tuple-element.142), channel_id=1, source_target_pairs={{0,16},{8,24},{16,0},{24,8},{1,17},{9,25},{17,1},{25,9},{2,18},{10... | collective-permute-start | bytes 2285576 | tf_op jit(solution)/shard_map/ppermute | solution.py:24
  60.3 1.5 %collective-permute-start.7 = (bf16[2,480,384]{2,1,0:T(8,128)(2,1)S(1)}, bf16[2,480,384]{2,1,0:T(8,128)(2,1)S(1)}, u32[]{:S(2)}, u32[]{:S(2)}) collective-permute-start(bf16[2,480,384]{2,1,0:T(8,128)(2,1)S(1)} %get-tuple-element.141), channel_id=1, source_target_pairs={{0,8},{8,0},{16,24},{24,16},{1,9},{9,1},{17,25},{25,17},{2,10},{10... | collective-permute-start | bytes 2211848 | tf_op jit(solution)/shard_map/ppermute | solution.py:24
  61.8 6.2 %shard_map.202 = (bf16[384,512]{1,0:T(8,128)(2,1)S(1)}, bf16[768,512]{1,0:T(8,128)(2,1)S(1)}, bf16[640,512]{1,0:T(8,128)(2,1)S(1)}, bf16[128,512]{1,0:T(8,128)(2,1)S(1)}) custom-call(s32[17]{0:T(128)S(1)} %concatenate.3.s_ref, bf16[2304,512]{1,0:T(8,128)(2,1)S(1)} %get-tuple-element.99.qkv_ref, bf16[1536,512]{1,0:T(8,128)(2,1)S(1)} %get-tuple-element.127.kv_ref, ...), custom_call_target="tpu_custom_call" | custom-call | flops 1000000 | bytes 10000 | tf_op jit(solution)/shard_map/pallas_call | solution.py:41
  68.0 6.9 %shard_map.203 = (bf16[2304,512]{1,0:T(8,128)(2,1)S(1)}, bf16[4,576,384]{2,1,0:T(8,128)(2,1)S(1)}, bf16[4,576,128]{2,1,0:T(8,128)(2,1)S(1)}, bf16[4,576,128]{2,1,0:T(8,128)(2,1)S(1)}, bf16[4,576,128]{2,1,0:T(8,128)(2,1)S(1)}) custom-call(s32[17]{0:T(128)S(1)} %concatenate.3.s_ref, bf16[2304,512]{1,0:T(8,128)(2,1)S(1)} %get-tuple-element.99.qkv_ref, ...), custom_call_target="tpu_custom_call" | custom-call | flops 1000000 | bytes 10000 | tf_op jit(solution)/shard_map/pallas_call | solution.py:41
  75.0 0.5 collective-permute-start.10
  75.6 0.8 shard_map.204
  76.3 2.4 %collective-permute-done.7.refs_2_ = bf16[2,480,384]{2,1,0:T(8,128)(2,1)S(1)} collective-permute-done((bf16[2,480,384]{2,1,0:T(8,128)(2,1)S(1)}, bf16[2,480,384]{2,1,0:T(8,128)(2,1)S(1)}, u32[]{:S(2)}, u32[]{:S(2)}) %collective-permute-start.7) | collective-permute-done | bytes 737312 | tf_op jit(solution)/shard_map/ppermute | solution.py:24
  78.7 0.9 shard_map.205
  79.6 0.9 collective-permute-start.12
  80.5 2.6 %collective-permute-start.14 = (bf16[4,192,384]{2,1,0:T(8,128)(2,1)S(1)}, bf16[4,192,384]{2,1,0:T(8,128)(2,1)S(1)}, u32[]{:S(2)}, u32[]{:S(2)}) collective-permute-start(bf16[4,192,384]{2,1,0:T(8,128)(2,1)S(1)} %get-tuple-element.156), channel_id=1, source_target_pairs={{0,4},{1,5},{2,6},{3,7},{4,0},{5,1},{6,2},{7,3},{8,12},{9,13},{10,... | collective-permute-start | bytes 1769480 | tf_op jit(solution)/shard_map/ppermute | solution.py:24
  83.1 1.5 %collective-permute-start.13 = (bf16[496,384]{1,0:T(8,128)(2,1)S(1)}, bf16[496,384]{1,0:T(8,128)(2,1)S(1)}, u32[]{:S(2)}, u32[]{:S(2)}) collective-permute-start(bf16[496,384]{1,0:T(8,128)(2,1)S(1)} %get-tuple-element.153), channel_id=1, source_target_pairs={{0,8},{8,0},{16,24},{24,16},{1,9},{9,1},{17,25},{25,17},{2,10},{10... | collective-permute-start | bytes 1142792 | tf_op jit(solution)/shard_map/ppermute | solution.py:24
  84.6 1.4 %shard_map.206 = (bf16[576,384]{1,0:T(8,128)(2,1)S(1)}, bf16[576,384]{1,0:T(8,128)(2,1)S(1)}, bf16[576,384]{1,0:T(8,128)(2,1)S(1)}, bf16[576,384]{1,0:T(8,128)(2,1)S(1)}) custom-call(s32[17]{0:T(128)S(1)} %concatenate.3.s_ref, bf16[4,576,384]{2,1,0:T(8,128)(2,1)S(1)} %get-tuple-element.145.refs_0_, bf16[4,576,128]{2,1,0:T(8,128)(2,1)S(1)} %collective-permute-done.9.refs_1_, ...), custom_call_target="tpu_custom_call" | custom-call | flops 1000000 | bytes 10000 | tf_op jit(solution)/shard_map/pallas_call | solution.py:41
  86.0 0.6 collective-permute-start.15
  86.6 1.2 collective-permute-start.16
  87.8 3.2 %collective-permute-done.12.refs_2_ = bf16[480,384]{1,0:T(8,128)(2,1)S(1)} collective-permute-done((bf16[480,384]{1,0:T(8,128)(2,1)S(1)}, bf16[480,384]{1,0:T(8,128)(2,1)S(1)}, u32[]{:S(2)}, u32[]{:S(2)}) %collective-permute-start.12) | collective-permute-done | bytes 368672 | tf_op jit(solution)/shard_map/ppermute | solution.py:24
  91.1 1.9 %collective-permute-start.17 = (bf16[576,384]{1,0:T(8,128)(2,1)S(1)}, bf16[576,384]{1,0:T(8,128)(2,1)S(1)}, u32[]{:S(2)}, u32[]{:S(2)}) collective-permute-start(bf16[576,384]{1,0:T(8,128)(2,1)S(1)} %get-tuple-element.162), channel_id=1, source_target_pairs={{0,24},{8,16},{16,8},{24,0},{1,25},{9,17},{17,9},{25,1},{2,26},{10... | collective-permute-start | bytes 1327112 | tf_op jit(solution)/shard_map/ppermute | solution.py:24
  92.9 1.9 %collective-permute-done.13.refs_3_ = bf16[496,384]{1,0:T(8,128)(2,1)S(1)} collective-permute-done((bf16[496,384]{1,0:T(8,128)(2,1)S(1)}, bf16[496,384]{1,0:T(8,128)(2,1)S(1)}, u32[]{:S(2)}, u32[]{:S(2)}) %collective-permute-start.13) | collective-permute-done | bytes 380960 | tf_op jit(solution)/shard_map/ppermute | solution.py:24
  94.9 0.9 shard_map.207
  95.8 0.5 collective-permute-start.18
  96.3 12.2 %collective-permute-done.14.refs_1_ = bf16[4,192,384]{2,1,0:T(8,128)(2,1)S(1)} collective-permute-done((bf16[4,192,384]{2,1,0:T(8,128)(2,1)S(1)}, bf16[4,192,384]{2,1,0:T(8,128)(2,1)S(1)}, u32[]{:S(2)}, u32[]{:S(2)}) %collective-permute-start.14) | collective-permute-done | bytes 589856 | tf_op jit(solution)/shard_map/ppermute | solution.py:24
  108.5 0.7 shard_map.208
  109.1 1.0 collective-permute-start.19
  110.1 1.5 %collective-permute-start.23 = (bf16[640,512]{1,0:T(8,128)(2,1)S(1)}, bf16[640,512]{1,0:T(8,128)(2,1)S(1)}, u32[]{:S(2)}, u32[]{:S(2)}) collective-permute-start(bf16[640,512]{1,0:T(8,128)(2,1)S(1)} %get-tuple-element.181), channel_id=1, source_target_pairs={{0,8},{8,0},{16,24},{24,16},{1,9},{9,1},{17,25},{25,17},{2,10},{10... | collective-permute-start | bytes 1966088 | tf_op jit(solution)/shard_map/ppermute | solution.py:24
  111.6 2.5 %shard_map.209.own_ref = f32[768,512]{1,0:T(8,128)S(1)} custom-call(s32[17]{0:T(128)S(1)} %concatenate.3.s_ref, bf16[768,2304]{1,0:T(8,128)(2,1)S(1)} %copy-done.3, bf16[2304,512]{1,0:T(8,128)(2,1)S(1)} %get-tuple-element.135.dqkv_ref), custom_call_target="tpu_custom_call" | custom-call | flops 1000000 | bytes 10000 | tf_op jit(solution)/shard_map/pallas_call | solution.py:41
  114.1 1.3 shard_map.210
  115.5 0.5 collective-permute-done.18.refs_1_
  116.0 0.6 shard_map.211
  116.6 2.7 %collective-permute-start.22 = (bf16[208,512]{1,0:T(8,128)(2,1)S(1)}, bf16[208,512]{1,0:T(8,128)(2,1)S(1)}, u32[]{:S(2)}, u32[]{:S(2)}) collective-permute-start(bf16[208,512]{1,0:T(8,128)(2,1)S(1)} %get-tuple-element.176), channel_id=1, source_target_pairs={{0,4},{1,5},{2,6},{3,7},{4,0},{5,1},{6,2},{7,3},{8,12},{9,13},{10,... | collective-permute-start | bytes 638984 | tf_op jit(solution)/shard_map/ppermute | solution.py:24
  119.3 0.6 shard_map.212
  120.0 0.6 collective-permute-start.21
  120.6 1.5 %collective-permute-start.24 = (bf16[128,512]{1,0:T(8,128)(2,1)S(1)}, bf16[128,512]{1,0:T(8,128)(2,1)S(1)}, u32[]{:S(2)}, u32[]{:S(2)}) collective-permute-start(bf16[128,512]{1,0:T(8,128)(2,1)S(1)} %get-tuple-element.182), channel_id=1, source_target_pairs={{0,8},{8,0},{16,24},{24,16},{1,9},{9,1},{17,25},{25,17},{2,10},{10... | collective-permute-start | bytes 393224 | tf_op jit(solution)/shard_map/ppermute | solution.py:24
  122.0 6.3 %collective-permute-done.20.refs_1_ = bf16[2,576,96]{2,1,0:T(8,128)(2,1)S(1)} collective-permute-done((bf16[2,576,96]{2,1,0:T(8,128)(2,1)S(1)}, bf16[2,576,96]{2,1,0:T(8,128)(2,1)S(1)}, u32[]{:S(2)}, u32[]{:S(2)}) %collective-permute-start.20) | collective-permute-done | bytes 221216 | tf_op jit(solution)/shard_map/ppermute | solution.py:24
  128.4 0.7 shard_map.213
  129.1 1.8 %collective-permute-done.21.refs_1_ = bf16[192,384]{1,0:T(8,128)(2,1)S(1)} collective-permute-done((bf16[192,384]{1,0:T(8,128)(2,1)S(1)}, bf16[192,384]{1,0:T(8,128)(2,1)S(1)}, u32[]{:S(2)}, u32[]{:S(2)}) %collective-permute-start.21) | collective-permute-done | bytes 147488 | tf_op jit(solution)/shard_map/ppermute | solution.py:24
  130.9 1.3 shard_map.214
  132.2 1.3 shard_map.215
  133.5 0.5 slice_bitcast_fusion
  134.1 1.9 %shard_map.216 = bf16[512,768]{1,0:T(8,128)(2,1)} custom-call(s32[17]{0:T(128)S(1)} %concatenate.3.s_ref, f32[768,512]{1,0:T(8,128)S(1)} %shard_map.209.own_ref, bf16[640,512]{1,0:T(8,128)(2,1)S(1)} %collective-permute-done.23.got_ref, bf16[128,512]{1,0:T(8,128)(2,1)S(1)} %collective-permute-done.24.rest_ref, f32[512,768]{1,0:T(8,128)S(1)} %get-tuple-element.183.dres_ref), custom_call_target="tpu_custom_call" | custom-call | flops 1000000 | bytes 10000 | tf_op jit(solution)/shard_map/pallas_call | solution.py:41
  136.0 0.3 collective-permute-done.25.refs_1_
  136.2 1.4 %shard_map.217 = f32[96,576]{1,0:T(8,128)} custom-call(s32[17]{0:T(128)S(1)} %concatenate.3.s_ref, bf16[576,96]{1,0:T(8,128)(2,1)S(1)} %get-tuple-element.172.refs_0_, bf16[576,96]{1,0:T(8,128)(2,1)S(1)} %collective-permute-done.25.refs_1_), custom_call_target="tpu_custom_call" | custom-call | flops 1000000 | bytes 10000 | tf_op jit(solution)/shard_map/pallas_call | solution.py:41
  (39 shorter events, 0.4 us)
Async XLA Ops:
  0.6 3.0 %copy-start = (s32[2,1]{0,1:T(1,128)S(1)}, s32[2,1]{0,1:T(1,128)}, u32[]{:S(2)}) copy-start(s32[2,1]{0,1:T(1,128)} %param.13) | copy-start | bytes 28
  0.7 20.8 %collective-permute-start = (bf16[512,768]{1,0:T(8,128)(2,1)}, bf16[512,768]{1,0:T(8,128)(2,1)S(1)}, u32[]{:S(2)}, u32[]{:S(2)}) collective-permute-start(bf16[512,768]{1,0:T(8,128)(2,1)} %bitcast.19), channel_id=1, source_target_pairs={{0,8},{8,0},{16,24},{24,16},{1,9},{9,1},{17,25},{25,17},{2,10},{10... | collective-permute-start | bytes 2359304 | tf_op jit(solution)/shard_map/ppermute | solution.py:24
  9.2 2.0 %copy-start.2 = (bf16[768,2304]{1,0:T(8,128)(2,1)S(1)}, bf16[768,2304]{1,0:T(8,128)(2,1)}, u32[]{:S(2)}) copy-start(bf16[768,2304]{1,0:T(8,128)(2,1)} %w_ref.7) | copy-start | bytes 10616836
  11.2 1.1 copy-start.7
  12.3 9.1 %copy-start.3 = (bf16[768,2304]{1,0:T(8,128)(2,1)S(1)}, bf16[768,2304]{1,0:T(8,128)(2,1)}, u32[]{:S(2)}) copy-start(bf16[768,2304]{1,0:T(8,128)(2,1)} %w_ref.7) | copy-start | bytes 10616836
  12.3 9.1 %copy-start.4 = (bf16[768,3072]{1,0:T(8,128)(2,1)S(1)}, bf16[768,3072]{1,0:T(8,128)(2,1)}, u32[]{:S(2)}) copy-start(bf16[768,3072]{1,0:T(8,128)(2,1)} %wu_ref.3) | copy-start | bytes 14155780
  12.3 9.1 %copy-start.5 = (bf16[3072,768]{1,0:T(8,128)(2,1)S(1)}, bf16[3072,768]{1,0:T(8,128)(2,1)}, u32[]{:S(2)}) copy-start(bf16[3072,768]{1,0:T(8,128)(2,1)} %wd_ref.3) | copy-start | bytes 14155780
  12.3 9.1 %copy-start.6 = (bf16[768,768]{1,0:T(8,128)(2,1)S(1)}, bf16[768,768]{1,0:T(8,128)(2,1)}, u32[]{:S(2)}) copy-start(bf16[768,768]{1,0:T(8,128)(2,1)} %wo_ref.3) | copy-start | bytes 3538948
  12.3 9.1 %copy-start.8 = (bf16[1,1,512,768]{3,2,1,0:T(8,128)(2,1)S(1)}, bf16[1,1,512,768]{3,2,1,0:T(8,128)(2,1)}, u32[]{:S(2)}) copy-start(bf16[1,1,512,768]{3,2,1,0:T(8,128)(2,1)} %param.12) | copy-start | bytes 2359300
  12.3 9.1 %copy-start.9 = (bf16[1,1,512,768]{3,2,1,0:T(8,128)(2,1)S(1)}, bf16[1,1,512,768]{3,2,1,0:T(8,128)(2,1)}, u32[]{:S(2)}) copy-start(bf16[1,1,512,768]{3,2,1,0:T(8,128)(2,1)} %param.23) | copy-start | bytes 2359300
  39.0 6.1 %collective-permute-start.1 = (bf16[4,192,1536]{2,1,0:T(8,128)(2,1)S(1)}, bf16[4,192,1536]{2,1,0:T(8,128)(2,1)S(1)}, u32[]{:S(2)}, u32[]{:S(2)}) collective-permute-start(bf16[4,192,1536]{2,1,0:T(8,128)(2,1)S(1)} %get-tuple-element.108), channel_id=1, source_target_pairs={{0,1},{1,0},{2,3},{3,2},{4,5},{5,4},{6,7},{7,6},{8,9},{9,8},{10,11... | collective-permute-start | bytes 7077896 | tf_op jit(solution)/shard_map/ppermute | solution.py:24
  46.2 29.2 %collective-permute-start.6 = (bf16[2,4,192,384]{3,2,1,0:T(8,128)(2,1)S(1)}, bf16[2,4,192,384]{3,2,1,0:T(8,128)(2,1)S(1)}, u32[]{:S(2)}, u32[]{:S(2)}) collective-permute-start(bf16[2,4,192,384]{3,2,1,0:T(8,128)(2,1)S(1)} %get-tuple-element.137), channel_id=1, source_target_pairs={{0,2},{1,3},{2,0},{3,1},{4,6},{5,7},{6,4},{7,5},{8,10},{9,11},{10,... | collective-permute-start | bytes 3538952 | tf_op jit(solution)/shard_map/ppermute | solution.py:24
  51.3 6.0 %collective-permute-start.2 = (bf16[4,256,384]{2,1,0:T(8,128)(2,1)S(1)}, bf16[4,256,384]{2,1,0:T(8,128)(2,1)S(1)}, u32[]{:S(2)}, u32[]{:S(2)}) collective-permute-start(bf16[4,256,384]{2,1,0:T(8,128)(2,1)S(1)} %get-tuple-element.121), channel_id=1, source_target_pairs={{0,1},{1,0},{2,3},{3,2},{4,5},{5,4},{6,7},{7,6},{8,9},{9,8},{10,11... | collective-permute-start | bytes 2359304 | tf_op jit(solution)/shard_map/ppermute | solution.py:24
  51.6 5.7 %collective-permute-start.3 = (bf16[4,256,384]{2,1,0:T(8,128)(2,1)S(1)}, bf16[4,256,384]{2,1,0:T(8,128)(2,1)S(1)}, u32[]{:S(2)}, u32[]{:S(2)}) collective-permute-start(bf16[4,256,384]{2,1,0:T(8,128)(2,1)S(1)} %get-tuple-element.122), channel_id=1, source_target_pairs={{0,1},{1,0},{2,3},{3,2},{4,5},{5,4},{6,7},{7,6},{8,9},{9,8},{10,11... | collective-permute-start | bytes 2359304 | tf_op jit(solution)/shard_map/ppermute | solution.py:24
  51.9 5.4 %collective-permute-start.4 = (bf16[4,256,384]{2,1,0:T(8,128)(2,1)S(1)}, bf16[4,256,384]{2,1,0:T(8,128)(2,1)S(1)}, u32[]{:S(2)}, u32[]{:S(2)}) collective-permute-start(bf16[4,256,384]{2,1,0:T(8,128)(2,1)S(1)} %get-tuple-element.123), channel_id=1, source_target_pairs={{0,1},{1,0},{2,3},{3,2},{4,5},{5,4},{6,7},{7,6},{8,9},{9,8},{10,11... | collective-permute-start | bytes 2359304 | tf_op jit(solution)/shard_map/ppermute | solution.py:24
  55.1 2.1 %collective-permute-start.5 = (bf16[4,208,384]{2,1,0:T(8,128)(2,1)S(1)}, bf16[4,208,384]{2,1,0:T(8,128)(2,1)S(1)}, u32[]{:S(2)}, u32[]{:S(2)}) collective-permute-start(bf16[4,208,384]{2,1,0:T(8,128)(2,1)S(1)} %get-tuple-element.124), channel_id=1, source_target_pairs={{0,1},{1,0},{2,3},{3,2},{4,5},{5,4},{6,7},{7,6},{8,9},{9,8},{10,11... | collective-permute-start | bytes 1916936 | tf_op jit(solution)/shard_map/ppermute | solution.py:24
  58.7 20.0 %collective-permute-start.8 = (bf16[2,496,384]{2,1,0:T(8,128)(2,1)S(1)}, bf16[2,496,384]{2,1,0:T(8,128)(2,1)S(1)}, u32[]{:S(2)}, u32[]{:S(2)}) collective-permute-start(bf16[2,496,384]{2,1,0:T(8,128)(2,1)S(1)} %get-tuple-element.142), channel_id=1, source_target_pairs={{0,16},{8,24},{16,0},{24,8},{1,17},{9,25},{17,1},{25,9},{2,18},{10... | collective-permute-start | bytes 2285576 | tf_op jit(solution)/shard_map/ppermute | solution.py:24
  60.3 18.4 %collective-permute-start.7 = (bf16[2,480,384]{2,1,0:T(8,128)(2,1)S(1)}, bf16[2,480,384]{2,1,0:T(8,128)(2,1)S(1)}, u32[]{:S(2)}, u32[]{:S(2)}) collective-permute-start(bf16[2,480,384]{2,1,0:T(8,128)(2,1)S(1)} %get-tuple-element.141), channel_id=1, source_target_pairs={{0,8},{8,0},{16,24},{24,16},{1,9},{9,1},{17,25},{25,17},{2,10},{10... | collective-permute-start | bytes 2211848 | tf_op jit(solution)/shard_map/ppermute | solution.py:24
  74.9 8.2 %collective-permute-start.9 = (bf16[4,576,128]{2,1,0:T(8,128)(2,1)S(1)}, bf16[4,576,128]{2,1,0:T(8,128)(2,1)S(1)}, u32[]{:S(2)}, u32[]{:S(2)}) collective-permute-start(bf16[4,576,128]{2,1,0:T(8,128)(2,1)S(1)} %get-tuple-element.146), channel_id=1, source_target_pairs={{0,1},{1,0},{2,3},{3,2},{4,5},{5,4},{6,7},{7,6},{8,9},{9,8},{10,11... | collective-permute-start | bytes 1769480 | tf_op jit(solution)/shard_map/ppermute | solution.py:24
  75.0 9.6 %collective-permute-start.10 = (bf16[4,576,128]{2,1,0:T(8,128)(2,1)S(1)}, bf16[4,576,128]{2,1,0:T(8,128)(2,1)S(1)}, u32[]{:S(2)}, u32[]{:S(2)}) collective-permute-start(bf16[4,576,128]{2,1,0:T(8,128)(2,1)S(1)} %get-tuple-element.147), channel_id=1, source_target_pairs={{0,1},{1,0},{2,3},{3,2},{4,5},{5,4},{6,7},{7,6},{8,9},{9,8},{10,11... | collective-permute-start | bytes 1769480 | tf_op jit(solution)/shard_map/ppermute | solution.py:24
  75.5 9.1 %collective-permute-start.11 = (bf16[4,576,128]{2,1,0:T(8,128)(2,1)S(1)}, bf16[4,576,128]{2,1,0:T(8,128)(2,1)S(1)}, u32[]{:S(2)}, u32[]{:S(2)}) collective-permute-start(bf16[4,576,128]{2,1,0:T(8,128)(2,1)S(1)} %get-tuple-element.148), channel_id=1, source_target_pairs={{0,1},{1,0},{2,3},{3,2},{4,5},{5,4},{6,7},{7,6},{8,9},{9,8},{10,11... | collective-permute-start | bytes 1769480 | tf_op jit(solution)/shard_map/ppermute | solution.py:24
  79.6 11.4 %collective-permute-start.12 = (bf16[480,384]{1,0:T(8,128)(2,1)S(1)}, bf16[480,384]{1,0:T(8,128)(2,1)S(1)}, u32[]{:S(2)}, u32[]{:S(2)}) collective-permute-start(bf16[480,384]{1,0:T(8,128)(2,1)S(1)} %get-tuple-element.152), channel_id=1, source_target_pairs={{0,16},{8,24},{16,0},{24,8},{1,17},{9,25},{17,1},{25,9},{2,18},{10... | collective-permute-start | bytes 1105928 | tf_op jit(solution)/shard_map/ppermute | solution.py:24
  80.5 28.0 %collective-permute-start.14 = (bf16[4,192,384]{2,1,0:T(8,128)(2,1)S(1)}, bf16[4,192,384]{2,1,0:T(8,128)(2,1)S(1)}, u32[]{:S(2)}, u32[]{:S(2)}) collective-permute-start(bf16[4,192,384]{2,1,0:T(8,128)(2,1)S(1)} %get-tuple-element.156), channel_id=1, source_target_pairs={{0,4},{1,5},{2,6},{3,7},{4,0},{5,1},{6,2},{7,3},{8,12},{9,13},{10,... | collective-permute-start | bytes 1769480 | tf_op jit(solution)/shard_map/ppermute | solution.py:24
  83.1 11.8 %collective-permute-start.13 = (bf16[496,384]{1,0:T(8,128)(2,1)S(1)}, bf16[496,384]{1,0:T(8,128)(2,1)S(1)}, u32[]{:S(2)}, u32[]{:S(2)}) collective-permute-start(bf16[496,384]{1,0:T(8,128)(2,1)S(1)} %get-tuple-element.153), channel_id=1, source_target_pairs={{0,8},{8,0},{16,24},{24,16},{1,9},{9,1},{17,25},{25,17},{2,10},{10... | collective-permute-start | bytes 1142792 | tf_op jit(solution)/shard_map/ppermute | solution.py:24
  86.0 24.1 %collective-permute-start.15 = (bf16[576,384]{1,0:T(8,128)(2,1)S(1)}, bf16[576,384]{1,0:T(8,128)(2,1)S(1)}, u32[]{:S(2)}, u32[]{:S(2)}) collective-permute-start(bf16[576,384]{1,0:T(8,128)(2,1)S(1)} %get-tuple-element.160), channel_id=1, source_target_pairs={{0,8},{8,0},{16,24},{24,16},{1,9},{9,1},{17,25},{25,17},{2,10},{10... | collective-permute-start | bytes 1327112 | tf_op jit(solution)/shard_map/ppermute | solution.py:24
  86.6 27.5 %collective-permute-start.16 = (bf16[576,384]{1,0:T(8,128)(2,1)S(1)}, bf16[576,384]{1,0:T(8,128)(2,1)S(1)}, u32[]{:S(2)}, u32[]{:S(2)}) collective-permute-start(bf16[576,384]{1,0:T(8,128)(2,1)S(1)} %get-tuple-element.161), channel_id=1, source_target_pairs={{0,16},{8,24},{16,0},{24,8},{1,17},{9,25},{17,1},{25,9},{2,18},{10... | collective-permute-start | bytes 1327112 | tf_op jit(solution)/shard_map/ppermute | solution.py:24
  91.1 23.1 %collective-permute-start.17 = (bf16[576,384]{1,0:T(8,128)(2,1)S(1)}, bf16[576,384]{1,0:T(8,128)(2,1)S(1)}, u32[]{:S(2)}, u32[]{:S(2)}) collective-permute-start(bf16[576,384]{1,0:T(8,128)(2,1)S(1)} %get-tuple-element.162), channel_id=1, source_target_pairs={{0,24},{8,16},{16,8},{24,0},{1,25},{9,17},{17,9},{25,1},{2,26},{10... | collective-permute-start | bytes 1327112 | tf_op jit(solution)/shard_map/ppermute | solution.py:24
  95.8 20.2 %collective-permute-start.18 = (bf16[2,208,512]{2,1,0:T(8,128)(2,1)S(1)}, bf16[2,208,512]{2,1,0:T(8,128)(2,1)S(1)}, u32[]{:S(2)}, u32[]{:S(2)}) collective-permute-start(bf16[2,208,512]{2,1,0:T(8,128)(2,1)S(1)} %get-tuple-element.165), channel_id=1, source_target_pairs={{0,2},{1,3},{2,0},{3,1},{4,6},{5,7},{6,4},{7,5},{8,10},{9,11},{10,... | collective-permute-start | bytes 1277960 | tf_op jit(solution)/shard_map/ppermute | solution.py:24
  109.1 10.2 %collective-permute-start.19 = (bf16[2,192,384]{2,1,0:T(8,128)(2,1)S(1)}, bf16[2,192,384]{2,1,0:T(8,128)(2,1)S(1)}, u32[]{:S(2)}, u32[]{:S(2)}) collective-permute-start(bf16[2,192,384]{2,1,0:T(8,128)(2,1)S(1)} %get-tuple-element.168), channel_id=1, source_target_pairs={{0,16},{8,24},{16,0},{24,8},{1,17},{9,25},{17,1},{25,9},{2,18},{10... | collective-permute-start | bytes 884744 | tf_op jit(solution)/shard_map/ppermute | solution.py:24
  110.1 23.9 %collective-permute-start.23 = (bf16[640,512]{1,0:T(8,128)(2,1)S(1)}, bf16[640,512]{1,0:T(8,128)(2,1)S(1)}, u32[]{:S(2)}, u32[]{:S(2)}) collective-permute-start(bf16[640,512]{1,0:T(8,128)(2,1)S(1)} %get-tuple-element.181), channel_id=1, source_target_pairs={{0,8},{8,0},{16,24},{24,16},{1,9},{9,1},{17,25},{25,17},{2,10},{10... | collective-permute-start | bytes 1966088 | tf_op jit(solution)/shard_map/ppermute | solution.py:24
  115.4 12.9 %collective-permute-start.20 = (bf16[2,576,96]{2,1,0:T(8,128)(2,1)S(1)}, bf16[2,576,96]{2,1,0:T(8,128)(2,1)S(1)}, u32[]{:S(2)}, u32[]{:S(2)}) collective-permute-start(bf16[2,576,96]{2,1,0:T(8,128)(2,1)S(1)} %get-tuple-element.171), channel_id=1, source_target_pairs={{0,2},{1,3},{2,0},{3,1},{4,6},{5,7},{6,4},{7,5},{8,10},{9,11},{10,... | collective-permute-start | bytes 663560 | tf_op jit(solution)/shard_map/ppermute | solution.py:24
  116.6 15.6 %collective-permute-start.22 = (bf16[208,512]{1,0:T(8,128)(2,1)S(1)}, bf16[208,512]{1,0:T(8,128)(2,1)S(1)}, u32[]{:S(2)}, u32[]{:S(2)}) collective-permute-start(bf16[208,512]{1,0:T(8,128)(2,1)S(1)} %get-tuple-element.176), channel_id=1, source_target_pairs={{0,4},{1,5},{2,6},{3,7},{4,0},{5,1},{6,2},{7,3},{8,12},{9,13},{10,... | collective-permute-start | bytes 638984 | tf_op jit(solution)/shard_map/ppermute | solution.py:24
  120.0 10.9 %collective-permute-start.21 = (bf16[192,384]{1,0:T(8,128)(2,1)S(1)}, bf16[192,384]{1,0:T(8,128)(2,1)S(1)}, u32[]{:S(2)}, u32[]{:S(2)}) collective-permute-start(bf16[192,384]{1,0:T(8,128)(2,1)S(1)} %get-tuple-element.174), channel_id=1, source_target_pairs={{0,8},{8,0},{16,24},{24,16},{1,9},{9,1},{17,25},{25,17},{2,10},{10... | collective-permute-start | bytes 442376 | tf_op jit(solution)/shard_map/ppermute | solution.py:24
  120.6 13.5 %collective-permute-start.24 = (bf16[128,512]{1,0:T(8,128)(2,1)S(1)}, bf16[128,512]{1,0:T(8,128)(2,1)S(1)}, u32[]{:S(2)}, u32[]{:S(2)}) collective-permute-start(bf16[128,512]{1,0:T(8,128)(2,1)S(1)} %get-tuple-element.182), channel_id=1, source_target_pairs={{0,8},{8,0},{16,24},{24,16},{1,9},{9,1},{17,25},{25,17},{2,10},{10... | collective-permute-start | bytes 393224 | tf_op jit(solution)/shard_map/ppermute | solution.py:24
  129.1 7.2 %collective-permute-start.25 = (bf16[576,96]{1,0:T(8,128)(2,1)S(1)}, bf16[576,96]{1,0:T(8,128)(2,1)S(1)}, u32[]{:S(2)}, u32[]{:S(2)}) collective-permute-start(bf16[576,96]{1,0:T(8,128)(2,1)S(1)} %get-tuple-element.185), channel_id=1, source_target_pairs={{0,4},{1,5},{2,6},{3,7},{4,0},{5,1},{6,2},{7,3},{8,12},{9,13},{10,... | collective-permute-start | bytes 331784 | tf_op jit(solution)/shard_map/ppermute | solution.py:24
  134.1 3.6 %copy-start.1 = (s32[2,1]{0,1:T(1,128)S(1)}, s32[2,1]{0,1:T(1,128)}, u32[]{:S(2)}) copy-start(s32[2,1]{0,1:T(1,128)} %param.13) | copy-start | bytes 28

commit v3 on v2

--- a/solution.py
+++ b/solution.py
@@ -718,7 +718,7 @@
         s = after(s, chip2[0])
     far_q, far_kv, *give = call(
         functools.partial(far_back_kernel, heads), s, (qkv, kv, ctx, dctx, far_lse, w_qkv),
-        [((width // 2, rows), BF16), square, ((width - 128, rows), BF16), ((128, rows), BF16)],
+        [((width // 2, rows), BF16), square, ((width - 64, rows), BF16), ((64, rows), BF16)],
         [((2 * width, rows), BF16)], mib=8,
     )
     s = after(s, far_q)

time: 138 us -> 138 us (level)
  waiting for transfers between devices: 33.7 us -> 30.5 us
  starting transfers between devices: 26.3 us -> 28.8 us
    ppermute x26, waiting for transfers between devices: 33.7 us -> 30.5 us  [swap(): lax.ppermute(block, axis, [(i, i ^ bits) for i in range(lax.axis_size(axi...]
    ppermute x26, starting transfers between devices: 26.3 us -> 28.8 us  [swap(): lax.ppermute(block, axis, [(i, i ^ bits) for i in range(lax.axis_size(axi...]
  transfers between devices with their start and end apart: 26 -> 26, of which waited for: 10 -> 9; matrix products, arithmetic and copies ran while one was open for 3% -> 3% of each run, Pallas kernels for 34% -> 35%
where the time goes in v3:
time: 138 us; the launch traced here: 137 us
  Pallas kernels  67.7 us (49%)
  waiting for transfers between devices  30.5 us (22%)
  starting transfers between devices  28.8 us (21%)
  local copies, waits for them, and re-layouts  7.13 us (5%)
  between operations  2.19 us (2%)
    pallas_call x23, Pallas kernels, call(): pl.pallas_call(kernel, in_specs=[pl.BlockSpec(memory_space=pltpu.SMEM)] +...  67.7 us
    ppermute x26, waiting for transfers between devices, swap(): lax.ppermute(block, axis, [(i, i ^ bits) for i in range(lax.axis_size(axi...  30.5 us
    ppermute x26, starting transfers between devices, swap(): lax.ppermute(block, axis, [(i, i ^ bits) for i in range(lax.axis_size(axi...  28.8 us
    unnamed x20, local copies, waits for them, and re-layouts  3.18 us
  transfers between devices with their start and end apart: 26, of which 9 were waited for; matrix products, arithmetic and copies ran while one was open for 3% of the time, Pallas kernels for 35%

profile of v3, /device:TPU:0, one launch (start us, length us, event | category | flops | bytes accessed | tf_op | source)
XLA Modules:
  0.0 137.2 jit_solution(10698672391388438744)
XLA Ops:
  0.7 3.0 %collective-permute-start = (bf16[512,768]{1,0:T(8,128)(2,1)}, bf16[512,768]{1,0:T(8,128)(2,1)S(1)}, u32[]{:S(2)}, u32[]{:S(2)}) collective-permute-start(bf16[512,768]{1,0:T(8,128)(2,1)} %bitcast.19), channel_id=1, source_target_pairs={{0,8},{8,0},{16,24},{24,16},{1,9},{9,1},{17,25},{25,17},{2,10},{10... | collective-permute-start | bytes 2359304 | tf_op jit(solution)/shard_map/ppermute | solution.py:24
  3.7 0.6 constant_dynamic-slice_fusion
  5.5 0.8 select_reduce_fusion
  6.3 0.7 reshape.48.gain1_ref
  7.0 0.7 reshape.49.bias1_ref
  7.7 0.7 reshape.50.gain2_ref
  8.4 0.7 reshape.51.bias2_ref
  9.2 2.0 %copy-done.2 = bf16[768,2304]{1,0:T(8,128)(2,1)S(1)} copy-done((bf16[768,2304]{1,0:T(8,128)(2,1)S(1)}, bf16[768,2304]{1,0:T(8,128)(2,1)}, u32[]{:S(2)}) %copy-start.2) | copy-done | bytes 3538968
  11.2 1.1 copy-done.7
  12.3 5.8 %shard_map.195 = (bf16[2304,512]{1,0:T(8,128)(2,1)S(1)}, bf16[768,512]{1,0:T(8,128)(2,1)S(1)}, f32[12,1,512]{2,1,0:T(1,128)S(1)}, bf16[2,512,384]{2,1,0:T(8,128)(2,1)S(1)}) custom-call(s32[17]{0:T(128)S(1)} %concatenate.3.s_ref, bf16[512,768]{1,0:T(8,128)(2,1)S(1)} %bitcast.20, bf16[768,2304]{1,0:T(8,128)(2,1)S(1)} %copy-done.2), custom_call_target="tpu_custom_call" | custom-call | flops 9201000448 | bytes 10000 | tf_op jit(solution)/shard_map/pallas_call | solution.py:41
  18.1 3.3 %collective-permute-done.xp_ref = bf16[512,768]{1,0:T(8,128)(2,1)S(1)} collective-permute-done((bf16[512,768]{1,0:T(8,128)(2,1)}, bf16[512,768]{1,0:T(8,128)(2,1)S(1)}, u32[]{:S(2)}, u32[]{:S(2)}) %collective-permute-start) | collective-permute-done | bytes 786464 | tf_op jit(solution)/shard_map/ppermute | solution.py:24
  21.5 17.6 %shard_map.196 = (bf16[1536,512]{1,0:T(8,128)(2,1)S(1)}, bf16[768,512]{1,0:T(8,128)(2,1)S(1)}, f32[12,1,512]{2,1,0:T(1,128)S(1)}, bf16[512,768]{1,0:T(8,128)(2,1...) custom-call(s32[17]{0:T(128)S(1)} %concatenate.3.s_ref, ...), custom_call_target="tpu_custom_call" | custom-call | flops 20700999680 | bytes 10000 | tf_op jit(solution)/shard_map/pallas_call | solution.py:41
  39.0 6.1 %shard_map.197 = (bf16[512,3072]{1,0:T(8,128)(2,1)S(1)}, f32[512,768]{1,0:T(8,128)S(1)}) custom-call(s32[17]{0:T(128)S(1)} %concatenate.3.s_ref, f32[512,768]{1,0:T(8,128)S(1)} %get-tuple-element.102.dtwo_ref, bf16[512,3072]{1,0:T(8,128)(2,1)S(1)} %get-tuple-element.104.slope_ref, bf16[3072,768]{1,0:T(8,128)(2,1)S(1)} %copy-done.5, ...), custom_call_target="tpu_custom_call" | custom-call | flops 1000000 | bytes 10000 | tf_op jit(solution)/shard_map/pallas_call | solution.py:41
  45.2 1.1 shard_map.198
  46.2 1.9 %collective-permute-start.6 = (bf16[2,4,192,384]{3,2,1,0:T(8,128)(2,1)S(1)}, bf16[2,4,192,384]{3,2,1,0:T(8,128)(2,1)S(1)}, u32[]{:S(2)}, u32[]{:S(2)}) collective-permute-start(bf16[2,4,192,384]{3,2,1,0:T(8,128)(2,1)S(1)} %get-tuple-element.137), channel_id=1, source_target_pairs={{0,2},{1,3},{2,0},{3,1},{4,6},{5,7},{6,4},{7,5},{8,10},{9,11},{10,... | collective-permute-start | bytes 3538952 | tf_op jit(solution)/shard_map/ppermute | solution.py:24
  48.1 3.2 %shard_map.199 = (bf16[4,768,384]{2,1,0:T(8,128)(2,1)S(1)}, bf16[4,256,384]{2,1,0:T(8,128)(2,1)S(1)}, bf16[4,256,384]{2,1,0:T(8,128)(2,1)S(1)}, bf16[4,256,384]{2,1,0:T(8,128)(2,1)S(1)}) custom-call(s32[17]{0:T(128)S(1)} %concatenate.3.s_ref, bf16[512,3072]{1,0:T(8,128)(2,1)S(1)} %get-tuple-element.111.dpre_ref, bf16[768,512]{1,0:T(8,128)(2,1)S(1)} %get-tuple-element.112.upt_ref), custom_call_target="tpu_custom_call" | custom-call | flops 1000000 | bytes 10000 | tf_op jit(solution)/shard_map/pallas_call | solution.py:41
  51.3 0.3 collective-permute-start.2
  51.6 0.3 collective-permute-start.3
  51.9 0.2 collective-permute-start.4
  52.1 3.0 %shard_map.200 = (f32[512,768]{1,0:T(8,128)S(1)}, bf16[768,512]{1,0:T(8,128)(2,1)S(1)}, bf16[4,208,384]{2,1,0:T(8,128)(2,1)S(1)}, bf16[4,208,384]{2,1,0:T(8,128)(2,1)S(1)}) custom-call(s32[17]{0:T(128)S(1)} %concatenate.3.s_ref, f32[512,768]{1,0:T(8,128)S(1)} %get-tuple-element.105.done_ref, f32[512,768]{1,0:T(8,128)S(1)} %get-tuple-element.115.resid_ref, ...), custom_call_target="tpu_custom_call" | custom-call | flops 1000000 | bytes 10000 | tf_op jit(solution)/shard_map/pallas_call | solution.py:41
  55.1 0.4 collective-permute-start.5
  55.5 1.8 %collective-permute-done.5.refs_5_ = bf16[4,208,384]{2,1,0:T(8,128)(2,1)S(1)} collective-permute-done((bf16[4,208,384]{2,1,0:T(8,128)(2,1)S(1)}, bf16[4,208,384]{2,1,0:T(8,128)(2,1)S(1)}, u32[]{:S(2)}, u32[]{:S(2)}) %collective-permute-start.5) | collective-permute-done | bytes 639008 | tf_op jit(solution)/shard_map/ppermute | solution.py:24
  57.3 1.4 %shard_map.201 = (bf16[2,480,384]{2,1,0:T(8,128)(2,1)S(1)}, bf16[2,480,384]{2,1,0:T(8,128)(2,1)S(1)}, bf16[2,496,384]{2,1,0:T(8,128)(2,1)S(1)}, bf16[2,496,384]{2,1,0:T(8,128)(2,1)S(1)}) custom-call(s32[17]{0:T(128)S(1)} %concatenate.3.s_ref, bf16[4,768,384]{2,1,0:T(8,128)(2,1)S(1)} %get-tuple-element.113.refs_0_, ...), custom_call_target="tpu_custom_call" | custom-call | flops 1000000 | bytes 10000 | tf_op jit(solution)/shard_map/pallas_call | solution.py:41
  58.7 1.6 %collective-permute-start.7 = (bf16[2,480,384]{2,1,0:T(8,128)(2,1)S(1)}, bf16[2,480,384]{2,1,0:T(8,128)(2,1)S(1)}, u32[]{:S(2)}, u32[]{:S(2)}) collective-permute-start(bf16[2,480,384]{2,1,0:T(8,128)(2,1)S(1)} %get-tuple-element.141), channel_id=1, source_target_pairs={{0,8},{8,0},{16,24},{24,16},{1,9},{9,1},{17,25},{25,17},{2,10},{10... | collective-permute-start | bytes 2211848 | tf_op jit(solution)/shard_map/ppermute | solution.py:24
  60.3 1.5 %collective-permute-start.8 = (bf16[2,496,384]{2,1,0:T(8,128)(2,1)S(1)}, bf16[2,496,384]{2,1,0:T(8,128)(2,1)S(1)}, u32[]{:S(2)}, u32[]{:S(2)}) collective-permute-start(bf16[2,496,384]{2,1,0:T(8,128)(2,1)S(1)} %get-tuple-element.142), channel_id=1, source_target_pairs={{0,16},{8,24},{16,0},{24,8},{1,17},{9,25},{17,1},{25,9},{2,18},{10... | collective-permute-start | bytes 2285576 | tf_op jit(solution)/shard_map/ppermute | solution.py:24
  61.8 6.2 %shard_map.202 = (bf16[384,512]{1,0:T(8,128)(2,1)S(1)}, bf16[768,512]{1,0:T(8,128)(2,1)S(1)}, bf16[704,512]{1,0:T(8,128)(2,1)S(1)}, bf16[64,512]{1,0:T(8,128)(2,1)S(1)}) custom-call(s32[17]{0:T(128)S(1)} %concatenate.3.s_ref, bf16[2304,512]{1,0:T(8,128)(2,1)S(1)} %get-tuple-element.99.qkv_ref, bf16[1536,512]{1,0:T(8,128)(2,1)S(1)} %get-tuple-element.127.kv_ref, ...), custom_call_target="tpu_custom_call" | custom-call | flops 1000000 | bytes 10000 | tf_op jit(solution)/shard_map/pallas_call | solution.py:41
  68.0 6.9 %shard_map.203 = (bf16[2304,512]{1,0:T(8,128)(2,1)S(1)}, bf16[4,576,384]{2,1,0:T(8,128)(2,1)S(1)}, bf16[4,576,128]{2,1,0:T(8,128)(2,1)S(1)}, bf16[4,576,128]{2,1,0:T(8,128)(2,1)S(1)}, bf16[4,576,128]{2,1,0:T(8,128)(2,1)S(1)}) custom-call(s32[17]{0:T(128)S(1)} %concatenate.3.s_ref, bf16[2304,512]{1,0:T(8,128)(2,1)S(1)} %get-tuple-element.99.qkv_ref, ...), custom_call_target="tpu_custom_call" | custom-call | flops 1000000 | bytes 10000 | tf_op jit(solution)/shard_map/pallas_call | solution.py:41
  75.0 0.5 collective-permute-start.10
  75.6 0.8 shard_map.204
  76.3 1.2 collective-permute-done.7.refs_2_
  77.5 2.6 %collective-permute-start.14 = (bf16[4,192,384]{2,1,0:T(8,128)(2,1)S(1)}, bf16[4,192,384]{2,1,0:T(8,128)(2,1)S(1)}, u32[]{:S(2)}, u32[]{:S(2)}) collective-permute-start(bf16[4,192,384]{2,1,0:T(8,128)(2,1)S(1)} %get-tuple-element.156), channel_id=1, source_target_pairs={{0,4},{1,5},{2,6},{3,7},{4,0},{5,1},{6,2},{7,3},{8,12},{9,13},{10,... | collective-permute-start | bytes 1769480 | tf_op jit(solution)/shard_map/ppermute | solution.py:24
  80.1 0.9 shard_map.205
  81.0 1.6 %collective-permute-start.12 = (bf16[480,384]{1,0:T(8,128)(2,1)S(1)}, bf16[480,384]{1,0:T(8,128)(2,1)S(1)}, u32[]{:S(2)}, u32[]{:S(2)}) collective-permute-start(bf16[480,384]{1,0:T(8,128)(2,1)S(1)} %get-tuple-element.152), channel_id=1, source_target_pairs={{0,16},{8,24},{16,0},{24,8},{1,17},{9,25},{17,1},{25,9},{2,18},{10... | collective-permute-start | bytes 1105928 | tf_op jit(solution)/shard_map/ppermute | solution.py:24
  82.6 1.5 %collective-permute-start.13 = (bf16[496,384]{1,0:T(8,128)(2,1)S(1)}, bf16[496,384]{1,0:T(8,128)(2,1)S(1)}, u32[]{:S(2)}, u32[]{:S(2)}) collective-permute-start(bf16[496,384]{1,0:T(8,128)(2,1)S(1)} %get-tuple-element.153), channel_id=1, source_target_pairs={{0,8},{8,0},{16,24},{24,16},{1,9},{9,1},{17,25},{25,17},{2,10},{10... | collective-permute-start | bytes 1142792 | tf_op jit(solution)/shard_map/ppermute | solution.py:24
  84.1 1.4 %shard_map.206 = (bf16[576,384]{1,0:T(8,128)(2,1)S(1)}, bf16[576,384]{1,0:T(8,128)(2,1)S(1)}, bf16[576,384]{1,0:T(8,128)(2,1)S(1)}, bf16[576,384]{1,0:T(8,128)(2,1)S(1)}) custom-call(s32[17]{0:T(128)S(1)} %concatenate.3.s_ref, bf16[4,576,384]{2,1,0:T(8,128)(2,1)S(1)} %get-tuple-element.145.refs_0_, bf16[4,576,128]{2,1,0:T(8,128)(2,1)S(1)} %collective-permute-done.9.refs_1_, ...), custom_call_target="tpu_custom_call" | custom-call | flops 1000000 | bytes 10000 | tf_op jit(solution)/shard_map/pallas_call | solution.py:41
  85.5 0.6 collective-permute-start.15
  86.1 0.5 collective-permute-start.16
  86.6 6.0 %collective-permute-done.12.refs_2_ = bf16[480,384]{1,0:T(8,128)(2,1)S(1)} collective-permute-done((bf16[480,384]{1,0:T(8,128)(2,1)S(1)}, bf16[480,384]{1,0:T(8,128)(2,1)S(1)}, u32[]{:S(2)}, u32[]{:S(2)}) %collective-permute-start.12) | collective-permute-done | bytes 368672 | tf_op jit(solution)/shard_map/ppermute | solution.py:24
  92.6 2.4 %collective-permute-start.17 = (bf16[576,384]{1,0:T(8,128)(2,1)S(1)}, bf16[576,384]{1,0:T(8,128)(2,1)S(1)}, u32[]{:S(2)}, u32[]{:S(2)}) collective-permute-start(bf16[576,384]{1,0:T(8,128)(2,1)S(1)} %get-tuple-element.162), channel_id=1, source_target_pairs={{0,24},{8,16},{16,8},{24,0},{1,25},{9,17},{17,9},{25,1},{2,26},{10... | collective-permute-start | bytes 1327112 | tf_op jit(solution)/shard_map/ppermute | solution.py:24
  95.0 0.9 shard_map.207
  96.0 0.5 collective-permute-start.18
  96.4 9.4 %collective-permute-done.14.refs_1_ = bf16[4,192,384]{2,1,0:T(8,128)(2,1)S(1)} collective-permute-done((bf16[4,192,384]{2,1,0:T(8,128)(2,1)S(1)}, bf16[4,192,384]{2,1,0:T(8,128)(2,1)S(1)}, u32[]{:S(2)}, u32[]{:S(2)}) %collective-permute-start.14) | collective-permute-done | bytes 589856 | tf_op jit(solution)/shard_map/ppermute | solution.py:24
  105.9 1.5 %collective-permute-start.23 = (bf16[704,512]{1,0:T(8,128)(2,1)S(1)}, bf16[704,512]{1,0:T(8,128)(2,1)S(1)}, u32[]{:S(2)}, u32[]{:S(2)}) collective-permute-start(bf16[704,512]{1,0:T(8,128)(2,1)S(1)} %get-tuple-element.181), channel_id=1, source_target_pairs={{0,8},{8,0},{16,24},{24,16},{1,9},{9,1},{17,25},{25,17},{2,10},{10... | collective-permute-start | bytes 2162696 | tf_op jit(solution)/shard_map/ppermute | solution.py:24
  107.4 0.7 shard_map.208
  108.0 1.6 %collective-permute-start.19 = (bf16[2,192,384]{2,1,0:T(8,128)(2,1)S(1)}, bf16[2,192,384]{2,1,0:T(8,128)(2,1)S(1)}, u32[]{:S(2)}, u32[]{:S(2)}) collective-permute-start(bf16[2,192,384]{2,1,0:T(8,128)(2,1)S(1)} %get-tuple-element.168), channel_id=1, source_target_pairs={{0,16},{8,24},{16,0},{24,8},{1,17},{9,25},{17,1},{25,9},{2,18},{10... | collective-permute-start | bytes 884744 | tf_op jit(solution)/shard_map/ppermute | solution.py:24
  109.6 2.5 %shard_map.209.own_ref = f32[768,512]{1,0:T(8,128)S(1)} custom-call(s32[17]{0:T(128)S(1)} %concatenate.3.s_ref, bf16[768,2304]{1,0:T(8,128)(2,1)S(1)} %copy-done.3, bf16[2304,512]{1,0:T(8,128)(2,1)S(1)} %get-tuple-element.135.dqkv_ref), custom_call_target="tpu_custom_call" | custom-call | flops 1000000 | bytes 10000 | tf_op jit(solution)/shard_map/pallas_call | solution.py:41
  112.2 1.1 collective-permute-done.17.refs_3_
  113.3 1.3 shard_map.210
  114.6 0.5 collective-permute-start.20
  115.1 0.6 shard_map.211
  115.7 2.0 %collective-permute-start.22 = (bf16[208,512]{1,0:T(8,128)(2,1)S(1)}, bf16[208,512]{1,0:T(8,128)(2,1)S(1)}, u32[]{:S(2)}, u32[]{:S(2)}) collective-permute-start(bf16[208,512]{1,0:T(8,128)(2,1)S(1)} %get-tuple-element.176), channel_id=1, source_target_pairs={{0,4},{1,5},{2,6},{3,7},{4,0},{5,1},{6,2},{7,3},{8,12},{9,13},{10,... | collective-permute-start | bytes 638984 | tf_op jit(solution)/shard_map/ppermute | solution.py:24
  117.7 0.3 collective-permute-done.19.refs_1_
  117.9 0.6 shard_map.212
  118.6 1.1 collective-permute-start.21
  119.6 1.0 collective-permute-start.24
  120.6 4.3 %collective-permute-done.20.refs_1_ = bf16[2,576,96]{2,1,0:T(8,128)(2,1)S(1)} collective-permute-done((bf16[2,576,96]{2,1,0:T(8,128)(2,1)S(1)}, bf16[2,576,96]{2,1,0:T(8,128)(2,1)S(1)}, u32[]{:S(2)}, u32[]{:S(2)}) %collective-permute-start.20) | collective-permute-done | bytes 221216 | tf_op jit(solution)/shard_map/ppermute | solution.py:24
  124.9 0.7 shard_map.213
  125.6 1.7 %collective-permute-start.25 = (bf16[576,96]{1,0:T(8,128)(2,1)S(1)}, bf16[576,96]{1,0:T(8,128)(2,1)S(1)}, u32[]{:S(2)}, u32[]{:S(2)}) collective-permute-start(bf16[576,96]{1,0:T(8,128)(2,1)S(1)} %get-tuple-element.185), channel_id=1, source_target_pairs={{0,4},{1,5},{2,6},{3,7},{4,0},{5,1},{6,2},{7,3},{8,12},{9,13},{10,... | collective-permute-start | bytes 331784 | tf_op jit(solution)/shard_map/ppermute | solution.py:24
  127.3 3.2 %collective-permute-done.21.refs_1_ = bf16[192,384]{1,0:T(8,128)(2,1)S(1)} collective-permute-done((bf16[192,384]{1,0:T(8,128)(2,1)S(1)}, bf16[192,384]{1,0:T(8,128)(2,1)S(1)}, u32[]{:S(2)}, u32[]{:S(2)}) %collective-permute-start.21) | collective-permute-done | bytes 147488 | tf_op jit(solution)/shard_map/ppermute | solution.py:24
  130.5 1.3 shard_map.214
  131.8 1.3 shard_map.215
  133.1 0.5 slice_bitcast_fusion
  133.7 2.1 %shard_map.216 = bf16[512,768]{1,0:T(8,128)(2,1)} custom-call(s32[17]{0:T(128)S(1)} %concatenate.3.s_ref, f32[768,512]{1,0:T(8,128)S(1)} %shard_map.209.own_ref, bf16[704,512]{1,0:T(8,128)(2,1)S(1)} %collective-permute-done.23.got_ref, bf16[64,512]{1,0:T(8,128)(2,1)S(1)} %collective-permute-done.24.rest_ref, f32[512,768]{1,0:T(8,128)S(1)} %get-tuple-element.183.dres_ref), custom_call_target="tpu_custom_call" | custom-call | flops 1000000 | bytes 10000 | tf_op jit(solution)/shard_map/pallas_call | solution.py:41
  135.8 1.4 %shard_map.217 = f32[96,576]{1,0:T(8,128)} custom-call(s32[17]{0:T(128)S(1)} %concatenate.3.s_ref, bf16[576,96]{1,0:T(8,128)(2,1)S(1)} %get-tuple-element.172.refs_0_, bf16[576,96]{1,0:T(8,128)(2,1)S(1)} %collective-permute-done.25.refs_1_), custom_call_target="tpu_custom_call" | custom-call | flops 1000000 | bytes 10000 | tf_op jit(solution)/shard_map/pallas_call | solution.py:41
  (39 shorter events, 0.3 us)
Async XLA Ops:
  0.6 3.0 %copy-start = (s32[2,1]{0,1:T(1,128)S(1)}, s32[2,1]{0,1:T(1,128)}, u32[]{:S(2)}) copy-start(s32[2,1]{0,1:T(1,128)} %param.13) | copy-start | bytes 28
  0.7 20.8 %collective-permute-start = (bf16[512,768]{1,0:T(8,128)(2,1)}, bf16[512,768]{1,0:T(8,128)(2,1)S(1)}, u32[]{:S(2)}, u32[]{:S(2)}) collective-permute-start(bf16[512,768]{1,0:T(8,128)(2,1)} %bitcast.19), channel_id=1, source_target_pairs={{0,8},{8,0},{16,24},{24,16},{1,9},{9,1},{17,25},{25,17},{2,10},{10... | collective-permute-start | bytes 2359304 | tf_op jit(solution)/shard_map/ppermute | solution.py:24
  9.2 2.0 %copy-start.2 = (bf16[768,2304]{1,0:T(8,128)(2,1)S(1)}, bf16[768,2304]{1,0:T(8,128)(2,1)}, u32[]{:S(2)}) copy-start(bf16[768,2304]{1,0:T(8,128)(2,1)} %w_ref.7) | copy-start | bytes 10616836
  11.2 1.1 copy-start.7
  12.3 9.1 %copy-start.3 = (bf16[768,2304]{1,0:T(8,128)(2,1)S(1)}, bf16[768,2304]{1,0:T(8,128)(2,1)}, u32[]{:S(2)}) copy-start(bf16[768,2304]{1,0:T(8,128)(2,1)} %w_ref.7) | copy-start | bytes 10616836
  12.3 9.1 %copy-start.4 = (bf16[768,3072]{1,0:T(8,128)(2,1)S(1)}, bf16[768,3072]{1,0:T(8,128)(2,1)}, u32[]{:S(2)}) copy-start(bf16[768,3072]{1,0:T(8,128)(2,1)} %wu_ref.3) | copy-start | bytes 14155780
  12.3 9.1 %copy-start.5 = (bf16[3072,768]{1,0:T(8,128)(2,1)S(1)}, bf16[3072,768]{1,0:T(8,128)(2,1)}, u32[]{:S(2)}) copy-start(bf16[3072,768]{1,0:T(8,128)(2,1)} %wd_ref.3) | copy-start | bytes 14155780
  12.3 9.1 %copy-start.6 = (bf16[768,768]{1,0:T(8,128)(2,1)S(1)}, bf16[768,768]{1,0:T(8,128)(2,1)}, u32[]{:S(2)}) copy-start(bf16[768,768]{1,0:T(8,128)(2,1)} %wo_ref.3) | copy-start | bytes 3538948
  12.3 9.1 %copy-start.8 = (bf16[1,1,512,768]{3,2,1,0:T(8,128)(2,1)S(1)}, bf16[1,1,512,768]{3,2,1,0:T(8,128)(2,1)}, u32[]{:S(2)}) copy-start(bf16[1,1,512,768]{3,2,1,0:T(8,128)(2,1)} %param.12) | copy-start | bytes 2359300
  12.3 9.1 %copy-start.9 = (bf16[1,1,512,768]{3,2,1,0:T(8,128)(2,1)S(1)}, bf16[1,1,512,768]{3,2,1,0:T(8,128)(2,1)}, u32[]{:S(2)}) copy-start(bf16[1,1,512,768]{3,2,1,0:T(8,128)(2,1)} %param.23) | copy-start | bytes 2359300
  39.0 6.1 %collective-permute-start.1 = (bf16[4,192,1536]{2,1,0:T(8,128)(2,1)S(1)}, bf16[4,192,1536]{2,1,0:T(8,128)(2,1)S(1)}, u32[]{:S(2)}, u32[]{:S(2)}) collective-permute-start(bf16[4,192,1536]{2,1,0:T(8,128)(2,1)S(1)} %get-tuple-element.108), channel_id=1, source_target_pairs={{0,1},{1,0},{2,3},{3,2},{4,5},{5,4},{6,7},{7,6},{8,9},{9,8},{10,11... | collective-permute-start | bytes 7077896 | tf_op jit(solution)/shard_map/ppermute | solution.py:24
  46.2 29.2 %collective-permute-start.6 = (bf16[2,4,192,384]{3,2,1,0:T(8,128)(2,1)S(1)}, bf16[2,4,192,384]{3,2,1,0:T(8,128)(2,1)S(1)}, u32[]{:S(2)}, u32[]{:S(2)}) collective-permute-start(bf16[2,4,192,384]{3,2,1,0:T(8,128)(2,1)S(1)} %get-tuple-element.137), channel_id=1, source_target_pairs={{0,2},{1,3},{2,0},{3,1},{4,6},{5,7},{6,4},{7,5},{8,10},{9,11},{10,... | collective-permute-start | bytes 3538952 | tf_op jit(solution)/shard_map/ppermute | solution.py:24
  51.3 6.0 %collective-permute-start.2 = (bf16[4,256,384]{2,1,0:T(8,128)(2,1)S(1)}, bf16[4,256,384]{2,1,0:T(8,128)(2,1)S(1)}, u32[]{:S(2)}, u32[]{:S(2)}) collective-permute-start(bf16[4,256,384]{2,1,0:T(8,128)(2,1)S(1)} %get-tuple-element.121), channel_id=1, source_target_pairs={{0,1},{1,0},{2,3},{3,2},{4,5},{5,4},{6,7},{7,6},{8,9},{9,8},{10,11... | collective-permute-start | bytes 2359304 | tf_op jit(solution)/shard_map/ppermute | solution.py:24
  51.6 5.7 %collective-permute-start.3 = (bf16[4,256,384]{2,1,0:T(8,128)(2,1)S(1)}, bf16[4,256,384]{2,1,0:T(8,128)(2,1)S(1)}, u32[]{:S(2)}, u32[]{:S(2)}) collective-permute-start(bf16[4,256,384]{2,1,0:T(8,128)(2,1)S(1)} %get-tuple-element.122), channel_id=1, source_target_pairs={{0,1},{1,0},{2,3},{3,2},{4,5},{5,4},{6,7},{7,6},{8,9},{9,8},{10,11... | collective-permute-start | bytes 2359304 | tf_op jit(solution)/shard_map/ppermute | solution.py:24
  51.9 5.4 %collective-permute-start.4 = (bf16[4,256,384]{2,1,0:T(8,128)(2,1)S(1)}, bf16[4,256,384]{2,1,0:T(8,128)(2,1)S(1)}, u32[]{:S(2)}, u32[]{:S(2)}) collective-permute-start(bf16[4,256,384]{2,1,0:T(8,128)(2,1)S(1)} %get-tuple-element.123), channel_id=1, source_target_pairs={{0,1},{1,0},{2,3},{3,2},{4,5},{5,4},{6,7},{7,6},{8,9},{9,8},{10,11... | collective-permute-start | bytes 2359304 | tf_op jit(solution)/shard_map/ppermute | solution.py:24
  55.1 2.1 %collective-permute-start.5 = (bf16[4,208,384]{2,1,0:T(8,128)(2,1)S(1)}, bf16[4,208,384]{2,1,0:T(8,128)(2,1)S(1)}, u32[]{:S(2)}, u32[]{:S(2)}) collective-permute-start(bf16[4,208,384]{2,1,0:T(8,128)(2,1)S(1)} %get-tuple-element.124), channel_id=1, source_target_pairs={{0,1},{1,0},{2,3},{3,2},{4,5},{5,4},{6,7},{7,6},{8,9},{9,8},{10,11... | collective-permute-start | bytes 1916936 | tf_op jit(solution)/shard_map/ppermute | solution.py:24
  58.7 18.8 %collective-permute-start.7 = (bf16[2,480,384]{2,1,0:T(8,128)(2,1)S(1)}, bf16[2,480,384]{2,1,0:T(8,128)(2,1)S(1)}, u32[]{:S(2)}, u32[]{:S(2)}) collective-permute-start(bf16[2,480,384]{2,1,0:T(8,128)(2,1)S(1)} %get-tuple-element.141), channel_id=1, source_target_pairs={{0,8},{8,0},{16,24},{24,16},{1,9},{9,1},{17,25},{25,17},{2,10},{10... | collective-permute-start | bytes 2211848 | tf_op jit(solution)/shard_map/ppermute | solution.py:24
  60.3 19.8 %collective-permute-start.8 = (bf16[2,496,384]{2,1,0:T(8,128)(2,1)S(1)}, bf16[2,496,384]{2,1,0:T(8,128)(2,1)S(1)}, u32[]{:S(2)}, u32[]{:S(2)}) collective-permute-start(bf16[2,496,384]{2,1,0:T(8,128)(2,1)S(1)} %get-tuple-element.142), channel_id=1, source_target_pairs={{0,16},{8,24},{16,0},{24,8},{1,17},{9,25},{17,1},{25,9},{2,18},{10... | collective-permute-start | bytes 2285576 | tf_op jit(solution)/shard_map/ppermute | solution.py:24
  74.9 7.7 %collective-permute-start.9 = (bf16[4,576,128]{2,1,0:T(8,128)(2,1)S(1)}, bf16[4,576,128]{2,1,0:T(8,128)(2,1)S(1)}, u32[]{:S(2)}, u32[]{:S(2)}) collective-permute-start(bf16[4,576,128]{2,1,0:T(8,128)(2,1)S(1)} %get-tuple-element.146), channel_id=1, source_target_pairs={{0,1},{1,0},{2,3},{3,2},{4,5},{5,4},{6,7},{7,6},{8,9},{9,8},{10,11... | collective-permute-start | bytes 1769480 | tf_op jit(solution)/shard_map/ppermute | solution.py:24
  75.0 9.1 %collective-permute-start.10 = (bf16[4,576,128]{2,1,0:T(8,128)(2,1)S(1)}, bf16[4,576,128]{2,1,0:T(8,128)(2,1)S(1)}, u32[]{:S(2)}, u32[]{:S(2)}) collective-permute-start(bf16[4,576,128]{2,1,0:T(8,128)(2,1)S(1)} %get-tuple-element.147), channel_id=1, source_target_pairs={{0,1},{1,0},{2,3},{3,2},{4,5},{5,4},{6,7},{7,6},{8,9},{9,8},{10,11... | collective-permute-start | bytes 1769480 | tf_op jit(solution)/shard_map/ppermute | solution.py:24
  75.5 8.6 %collective-permute-start.11 = (bf16[4,576,128]{2,1,0:T(8,128)(2,1)S(1)}, bf16[4,576,128]{2,1,0:T(8,128)(2,1)S(1)}, u32[]{:S(2)}, u32[]{:S(2)}) collective-permute-start(bf16[4,576,128]{2,1,0:T(8,128)(2,1)S(1)} %get-tuple-element.148), channel_id=1, source_target_pairs={{0,1},{1,0},{2,3},{3,2},{4,5},{5,4},{6,7},{7,6},{8,9},{9,8},{10,11... | collective-permute-start | bytes 1769480 | tf_op jit(solution)/shard_map/ppermute | solution.py:24
  77.5 28.4 %collective-permute-start.14 = (bf16[4,192,384]{2,1,0:T(8,128)(2,1)S(1)}, bf16[4,192,384]{2,1,0:T(8,128)(2,1)S(1)}, u32[]{:S(2)}, u32[]{:S(2)}) collective-permute-start(bf16[4,192,384]{2,1,0:T(8,128)(2,1)S(1)} %get-tuple-element.156), channel_id=1, source_target_pairs={{0,4},{1,5},{2,6},{3,7},{4,0},{5,1},{6,2},{7,3},{8,12},{9,13},{10,... | collective-permute-start | bytes 1769480 | tf_op jit(solution)/shard_map/ppermute | solution.py:24
  81.0 11.6 %collective-permute-start.12 = (bf16[480,384]{1,0:T(8,128)(2,1)S(1)}, bf16[480,384]{1,0:T(8,128)(2,1)S(1)}, u32[]{:S(2)}, u32[]{:S(2)}) collective-permute-start(bf16[480,384]{1,0:T(8,128)(2,1)S(1)} %get-tuple-element.152), channel_id=1, source_target_pairs={{0,16},{8,24},{16,0},{24,8},{1,17},{9,25},{17,1},{25,9},{2,18},{10... | collective-permute-start | bytes 1105928 | tf_op jit(solution)/shard_map/ppermute | solution.py:24
  82.6 12.5 %collective-permute-start.13 = (bf16[496,384]{1,0:T(8,128)(2,1)S(1)}, bf16[496,384]{1,0:T(8,128)(2,1)S(1)}, u32[]{:S(2)}, u32[]{:S(2)}) collective-permute-start(bf16[496,384]{1,0:T(8,128)(2,1)S(1)} %get-tuple-element.153), channel_id=1, source_target_pairs={{0,8},{8,0},{16,24},{24,16},{1,9},{9,1},{17,25},{25,17},{2,10},{10... | collective-permute-start | bytes 1142792 | tf_op jit(solution)/shard_map/ppermute | solution.py:24
  85.5 22.5 %collective-permute-start.15 = (bf16[576,384]{1,0:T(8,128)(2,1)S(1)}, bf16[576,384]{1,0:T(8,128)(2,1)S(1)}, u32[]{:S(2)}, u32[]{:S(2)}) collective-permute-start(bf16[576,384]{1,0:T(8,128)(2,1)S(1)} %get-tuple-element.160), channel_id=1, source_target_pairs={{0,8},{8,0},{16,24},{24,16},{1,9},{9,1},{17,25},{25,17},{2,10},{10... | collective-permute-start | bytes 1327112 | tf_op jit(solution)/shard_map/ppermute | solution.py:24
  86.1 26.1 %collective-permute-start.16 = (bf16[576,384]{1,0:T(8,128)(2,1)S(1)}, bf16[576,384]{1,0:T(8,128)(2,1)S(1)}, u32[]{:S(2)}, u32[]{:S(2)}) collective-permute-start(bf16[576,384]{1,0:T(8,128)(2,1)S(1)} %get-tuple-element.161), channel_id=1, source_target_pairs={{0,16},{8,24},{16,0},{24,8},{1,17},{9,25},{17,1},{25,9},{2,18},{10... | collective-permute-start | bytes 1327112 | tf_op jit(solution)/shard_map/ppermute | solution.py:24
  92.6 20.7 %collective-permute-start.17 = (bf16[576,384]{1,0:T(8,128)(2,1)S(1)}, bf16[576,384]{1,0:T(8,128)(2,1)S(1)}, u32[]{:S(2)}, u32[]{:S(2)}) collective-permute-start(bf16[576,384]{1,0:T(8,128)(2,1)S(1)} %get-tuple-element.162), channel_id=1, source_target_pairs={{0,24},{8,16},{16,8},{24,0},{1,25},{9,17},{17,9},{25,1},{2,26},{10... | collective-permute-start | bytes 1327112 | tf_op jit(solution)/shard_map/ppermute | solution.py:24
  96.0 19.1 %collective-permute-start.18 = (bf16[2,208,512]{2,1,0:T(8,128)(2,1)S(1)}, bf16[2,208,512]{2,1,0:T(8,128)(2,1)S(1)}, u32[]{:S(2)}, u32[]{:S(2)}) collective-permute-start(bf16[2,208,512]{2,1,0:T(8,128)(2,1)S(1)} %get-tuple-element.165), channel_id=1, source_target_pairs={{0,2},{1,3},{2,0},{3,1},{4,6},{5,7},{6,4},{7,5},{8,10},{9,11},{10,... | collective-permute-start | bytes 1277960 | tf_op jit(solution)/shard_map/ppermute | solution.py:24
  105.9 27.8 %collective-permute-start.23 = (bf16[704,512]{1,0:T(8,128)(2,1)S(1)}, bf16[704,512]{1,0:T(8,128)(2,1)S(1)}, u32[]{:S(2)}, u32[]{:S(2)}) collective-permute-start(bf16[704,512]{1,0:T(8,128)(2,1)S(1)} %get-tuple-element.181), channel_id=1, source_target_pairs={{0,8},{8,0},{16,24},{24,16},{1,9},{9,1},{17,25},{25,17},{2,10},{10... | collective-permute-start | bytes 2162696 | tf_op jit(solution)/shard_map/ppermute | solution.py:24
  108.0 9.9 %collective-permute-start.19 = (bf16[2,192,384]{2,1,0:T(8,128)(2,1)S(1)}, bf16[2,192,384]{2,1,0:T(8,128)(2,1)S(1)}, u32[]{:S(2)}, u32[]{:S(2)}) collective-permute-start(bf16[2,192,384]{2,1,0:T(8,128)(2,1)S(1)} %get-tuple-element.168), channel_id=1, source_target_pairs={{0,16},{8,24},{16,0},{24,8},{1,17},{9,25},{17,1},{25,9},{2,18},{10... | collective-permute-start | bytes 884744 | tf_op jit(solution)/shard_map/ppermute | solution.py:24
  114.6 10.4 %collective-permute-start.20 = (bf16[2,576,96]{2,1,0:T(8,128)(2,1)S(1)}, bf16[2,576,96]{2,1,0:T(8,128)(2,1)S(1)}, u32[]{:S(2)}, u32[]{:S(2)}) collective-permute-start(bf16[2,576,96]{2,1,0:T(8,128)(2,1)S(1)} %get-tuple-element.171), channel_id=1, source_target_pairs={{0,2},{1,3},{2,0},{3,1},{4,6},{5,7},{6,4},{7,5},{8,10},{9,11},{10,... | collective-permute-start | bytes 663560 | tf_op jit(solution)/shard_map/ppermute | solution.py:24
  115.7 16.1 %collective-permute-start.22 = (bf16[208,512]{1,0:T(8,128)(2,1)S(1)}, bf16[208,512]{1,0:T(8,128)(2,1)S(1)}, u32[]{:S(2)}, u32[]{:S(2)}) collective-permute-start(bf16[208,512]{1,0:T(8,128)(2,1)S(1)} %get-tuple-element.176), channel_id=1, source_target_pairs={{0,4},{1,5},{2,6},{3,7},{4,0},{5,1},{6,2},{7,3},{8,12},{9,13},{10,... | collective-permute-start | bytes 638984 | tf_op jit(solution)/shard_map/ppermute | solution.py:24
  118.6 12.0 %collective-permute-start.21 = (bf16[192,384]{1,0:T(8,128)(2,1)S(1)}, bf16[192,384]{1,0:T(8,128)(2,1)S(1)}, u32[]{:S(2)}, u32[]{:S(2)}) collective-permute-start(bf16[192,384]{1,0:T(8,128)(2,1)S(1)} %get-tuple-element.174), channel_id=1, source_target_pairs={{0,8},{8,0},{16,24},{24,16},{1,9},{9,1},{17,25},{25,17},{2,10},{10... | collective-permute-start | bytes 442376 | tf_op jit(solution)/shard_map/ppermute | solution.py:24
  119.6 14.0 %collective-permute-start.24 = (bf16[64,512]{1,0:T(8,128)(2,1)S(1)}, bf16[64,512]{1,0:T(8,128)(2,1)S(1)}, u32[]{:S(2)}, u32[]{:S(2)}) collective-permute-start(bf16[64,512]{1,0:T(8,128)(2,1)S(1)} %get-tuple-element.182), channel_id=1, source_target_pairs={{0,8},{8,0},{16,24},{24,16},{1,9},{9,1},{17,25},{25,17},{2,10},{10... | collective-permute-start | bytes 196616 | tf_op jit(solution)/shard_map/ppermute | solution.py:24
  125.6 10.2 %collective-permute-start.25 = (bf16[576,96]{1,0:T(8,128)(2,1)S(1)}, bf16[576,96]{1,0:T(8,128)(2,1)S(1)}, u32[]{:S(2)}, u32[]{:S(2)}) collective-permute-start(bf16[576,96]{1,0:T(8,128)(2,1)S(1)} %get-tuple-element.185), channel_id=1, source_target_pairs={{0,4},{1,5},{2,6},{3,7},{4,0},{5,1},{6,2},{7,3},{8,12},{9,13},{10,... | collective-permute-start | bytes 331784 | tf_op jit(solution)/shard_map/ppermute | solution.py:24
  133.7 3.5 %copy-start.1 = (s32[2,1]{0,1:T(1,128)S(1)}, s32[2,1]{0,1:T(1,128)}, u32[]{:S(2)}) copy-start(s32[2,1]{0,1:T(1,128)} %param.13) | copy-start | bytes 28
